TPU v7x, 32 devices: a whole 2x2x4 slice. The times are simulated.
32 devices in a mesh: grp: 2 (over x), yz: 8 (over z, y), gx: 2 (over core).
Axes of the slice: x: 2, y: 2, z: 4, core: 2. Of those that a mesh axis runs over, the one named last changes fastest.
Arguments:
- field: bfloat16 [4096, 256, 128], P(('grp', 'gx'), 'yz'), parts along dimension 0, may hold values from -6 to 6
- sketch_seeds: int32 [12], P('grp'), parts along dimension 0, may hold values from 1 to 32748
Outputs:
- basis: float32 [4096, 256], P(('grp', 'gx')), parts along dimension 0
- core: bfloat16 [512, 256, 128], P(('grp', 'gx'), 'yz'), parts along dimension 0
There are 2 independent parts, one for each index of `grp`. A program takes and returns all parts, laid end to end along the dimension named above; each array names one. Nothing has to cross between parts.
All inputs are finite; a program needn't handle non-finite values.
Results may differ from a plain program's by a relative error of at most 0.0057.
Values sent between devices are 32-bit elements; how exact they have to be, the bound alone decides.
No kernel may reach another device: no remote copies, remote signals or barrier semaphores. Data moves between devices by JAX's collectives and lax.ppermute only.
A program may use at most 64 MiB of HBM per device.

v0:
```python
import jax
import jax.numpy as jnp
from jax import lax
from jax.experimental import pallas as pl
from jax.experimental.pallas import tpu as pltpu
from jax.sharding import PartitionSpec as P

RANK = 256
prime = 32749
f32, bf16, i32 = jnp.float32, jnp.bfloat16, jnp.int32


def remainder(value):
    quotient = (value.astype(f32) * (1.0 / prime)).astype(i32)
    rest = value - quotient * prime
    rest = jnp.where(rest < 0, rest + prime, rest)
    return jnp.where(rest >= prime, rest - prime, rest)


def omega_table(a, b, c, start, count):
    place = start + 1 + lax.broadcasted_iota(i32, (count, 1), 0)
    column = 1 + lax.broadcasted_iota(i32, (1, RANK), 1)
    first = remainder(a * place)
    second = remainder(b * column + c)
    square = remainder(place * place)
    third = remainder(c * column)
    mixed = remainder(remainder(first * second) + remainder(square * third))
    return mixed.astype(f32) * (2.0 / prime) - 1.0


LIMIT = 14 << 20
VMEM_SPACE = pl.BlockSpec(memory_space=pltpu.VMEM)
SMEM_SPACE = pl.BlockSpec(memory_space=pltpu.SMEM)
ANY_SPACE = pl.BlockSpec(memory_space=pl.ANY)
HBM_SPACE = pl.BlockSpec(memory_space=pltpu.HBM)
SUB = 64


def held(shape, dtype):
    return pltpu.VMEM(shape, dtype)


def call(kernel, out_shape, in_specs, flops=0, moved=0, **more):
    return pl.pallas_call(
        kernel,
        out_shape=out_shape,
        in_specs=in_specs,
        compiler_params=pltpu.CompilerParams(vmem_limit_bytes=LIMIT),
        cost_estimate=pl.CostEstimate(flops=flops, bytes_accessed=moved, transcendentals=0),
        **more,
    )


def sketch_chunks(field, seeds, wanted, sizes, joined, tables=None):
    outer, inner, chunk = sizes
    _, y_local, z_local = field.shape
    sub = min(SUB, chunk)
    stride = y_local + 1
    parts = chunk // sub
    total = len(wanted) * chunk

    def kernel(seeds_ref, field_ref, *refs):
        refs = list(refs)
        if tables is not None:
            omega_z, omega_y = refs.pop(0), refs.pop(0)
        outs = [refs.pop(0) for _ in range(1 if joined else len(wanted))]
        flat = refs.pop(0)
        if tables is None:
            omega_z, omega_y = refs.pop(0), refs.pop(0)
        rows, first, second, sems = refs
        me = lax.axis_index("yz")
        o, y = me // inner, me % inner
        copies = []
        for k, (d, flip) in enumerate(wanted):
            chosen = lax.rem(o + d, outer) * inner + (inner - 1 - y if flip else y)
            copy = pltpu.make_async_copy(
                field_ref.at[pl.ds(chosen * chunk, chunk)], rows.at[pl.ds(k * chunk, chunk)], sems.at[k]
            )
            copy.start()
            copies.append(copy)
        if tables is None:
            omega_z[...] = omega_table(
                seeds_ref[3], seeds_ref[4], seeds_ref[5], 0, z_local
            ).astype(bf16)
            omega_y[...] = omega_table(
                seeds_ref[0], seeds_ref[1], seeds_ref[2], me * y_local, y_local
            )
        table_z = omega_z[...]
        scratch = (first, second)

        def spread(block):
            if block % parts == 0:
                copies[block // parts].wait()
            for x in range(sub):
                scratch[block % 2][x * stride:x * stride + y_local, :] = rows[block * sub + x].astype(f32)

        spread(0)
        for block in range(len(wanted) * parts):
            if block + 1 < len(wanted) * parts:
                spread(block + 1)
            low = block * sub
            sums = None
            for y_cell in range(y_local):
                cells = scratch[block % 2][pl.ds(y_cell, sub, stride=stride), :].astype(bf16)
                flat[low:low + sub, y_cell * z_local:(y_cell + 1) * z_local] = cells
                part = jnp.dot(cells, table_z, preferred_element_type=f32)
                part = part * omega_y[y_cell:y_cell + 1, :]
                sums = part if sums is None else sums + part
            if joined:
                outs[0][low:low + sub, :] = sums
            else:
                start = block % parts * sub
                outs[block // parts][start:start + sub, :] = sums

    count = 1 if joined else len(wanted)
    shape = jax.ShapeDtypeStruct((total if joined else chunk, RANK), f32)
    out_shape = [shape] * count + [held((total, y_local * z_local), bf16)]
    operands = [seeds, pltpu.with_memory_space_constraint(field, pltpu.HBM)]
    in_specs = [SMEM_SPACE, HBM_SPACE]
    if tables is None:
        out_shape += [held((z_local, RANK), bf16), held((y_local, RANK), f32)]
    else:
        operands += list(tables)
        in_specs += [VMEM_SPACE] * 2
    scratch_shapes = [
        pltpu.VMEM((total, y_local, z_local), bf16),
        pltpu.VMEM((sub * stride, z_local), f32),
        pltpu.VMEM((sub * stride, z_local), f32),
        pltpu.SemaphoreType.DMA((len(wanted),)),
    ]
    result = call(
        kernel, out_shape, in_specs,
        flops=2 * total * y_local * z_local * RANK, moved=2 * total * y_local * z_local,
        scratch_shapes=scratch_shapes,
    )(*operands)
    tail = result[count + 1:] if tables is None else tables
    return result[:count], result[count], tail


def split3(value):
    high = value.astype(bf16)
    rest = value - high.astype(f32)
    middle = rest.astype(bf16)
    return high, middle, (rest - middle.astype(f32)).astype(bf16)


PANEL = 32


def inverse_factor_kernel(gram, came, out, state):
    size = gram.shape[0]
    state[...] = gram[...] + came[...]
    lane = lax.broadcasted_iota(i32, (PANEL, 128), 1)
    row = lax.broadcasted_iota(i32, (PANEL, 128), 0)
    for low in range(0, size, PANEL):
        high = low + PANEL
        tile, offset = low // 128, low % 128
        rows = [state[low:high, 0:128], state[low:high, 128:256]]
        rows.append(jnp.where(lane == row + offset, 1.0, 0.0).astype(f32))
        done = [[None] * PANEL for _ in rows]
        for i in range(0, PANEL, 2):
            first = jnp.broadcast_to(rows[tile][:, offset + i:offset + i + 1], (PANEL, 128))
            second = jnp.broadcast_to(rows[tile][:, offset + i + 1:offset + i + 2], (PANEL, 128))
            d11, d12, d22 = first[i:i + 1], second[i:i + 1], second[i + 1:i + 2]
            scale = 1.0 / (d11 * d22 - d12 * d12)
            k11, k12, k22 = d22 * scale, d12 * scale, d11 * scale
            first = jnp.where(row > i + 1, first, 0.0)
            second = jnp.where(row > i + 1, second, 0.0)
            ratio = d12 / d11
            root1, root2 = lax.rsqrt(d11), lax.rsqrt(d22 - ratio * d12)
            for k in range(3):
                upper, lower = rows[k][i:i + 1], rows[k][i + 1:i + 2]
                done[k][i] = upper * root1
                done[k][i + 1] = (lower - ratio * upper) * root2
                if i + 2 < PANEL:
                    rows[k] = rows[k] - (
                        first * (k11 * upper - k12 * lower) + second * (k22 * lower - k12 * upper)
                    )
        factor = [jnp.concatenate(part, axis=0) for part in done]
        inside = (lane >= offset) & (lane < offset + PANEL)
        mixed = list(factor[:2])
        mixed[tile] = jnp.where(inside, factor[2], factor[tile])
        for k in range(2):
            if k < tile:
                value = mixed[k]
            elif k == tile:
                value = jnp.where(lane < offset + PANEL, mixed[k], 0.0)
            else:
                value = jnp.zeros((PANEL, 128), f32)
            out[low:high, 128 * k:128 * (k + 1)] = value
        if high < size:
            h, m, l = split3(jnp.concatenate(factor[:2], axis=1))
            eh, em, el = split3(jnp.concatenate(mixed, axis=1))
            left = jnp.concatenate([h, h, m, m, h, l], axis=0)
            right = jnp.concatenate([eh, em, eh, em, el, eh], axis=0)
            update = lax.dot_general(
                left, right, (((0,), (0,)), ((), ())), preferred_element_type=f32
            )
            lanes = lax.broadcasted_iota(i32, (size - high, size), 1)
            rest = jnp.where((lanes >= low) & (lanes < high), 0.0, state[high:, :])
            state[high:, :] = rest - update[high:, :]


def inverse_factor(gram, came):
    return call(
        inverse_factor_kernel, held(gram.shape, f32), [VMEM_SPACE] * 2,
        flops=3 * gram.shape[0] ** 3, moved=8 * gram.shape[0] ** 2,
        scratch_shapes=[pltpu.VMEM(gram.shape, f32)],
    )(gram, came)


def merge(kept, came):
    chunk = kept[0].shape[0]

    def kernel(*refs):
        came_ref = refs[len(kept)]
        for k in range(len(kept)):
            refs[len(kept) + 1 + k][...] = refs[k][...] + came_ref[k * chunk:(k + 1) * chunk, :]

    return call(
        kernel, [held(kept[0].shape, f32)] * len(kept), [VMEM_SPACE] * (len(kept) + 1),
        flops=came.size, moved=12 * came.size,
    )(*kept, came)


def total_of(parts):
    def kernel(*refs):
        sums = refs[0][...]
        for ref in refs[1:-1]:
            sums = sums + ref[...]
        refs[-1][...] = sums

    return call(
        kernel, held(parts[0].shape, f32), [VMEM_SPACE] * len(parts),
        flops=parts[0].size * len(parts), moved=4 * parts[0].size * len(parts),
    )(*parts)


def gram_of(chunks):
    chunk = chunks[0].shape[0]
    total = len(chunks) * chunk

    def kernel(*refs):
        rows_refs, (out, terms) = refs[:-2], refs[-2:]
        for k, ref in enumerate(rows_refs):
            for j, term in enumerate(split3(ref[...])):
                terms[k * chunk:(k + 1) * chunk, j * RANK:(j + 1) * RANK] = term
        over_rows = (((0,), (0,)), ((), ()))
        first = lax.dot_general(
            terms[:, :RANK], terms[...], over_rows, preferred_element_type=f32
        )
        middle = terms[:, RANK:2 * RANK]
        second = lax.dot_general(middle, middle, over_rows, preferred_element_type=f32)
        mixed = first[:, RANK:2 * RANK] + first[:, 2 * RANK:]
        out[...] = first[:, :RANK] + (second + (mixed + mixed.T))

    return call(
        kernel, held((RANK, RANK), f32), [VMEM_SPACE] * len(chunks),
        flops=8 * total * RANK ** 2, moved=4 * total * RANK,
        scratch_shapes=[pltpu.VMEM((total, 3 * RANK), bf16)],
    )(*chunks)


def split2(value):
    high = value.astype(bf16)
    return high, (value - high.astype(f32)).astype(bf16)


def solve_rows(chunks, inverse, sizes, places):
    outer, inner, chunk = sizes
    total = len(chunks) * chunk
    half = RANK // 2

    def kernel(inverse_ref, *refs):
        rows_refs, (basis, turned, rounded) = refs[:-3], refs[-3:]
        me = lax.axis_index("yz")
        o, y = me // inner, me % inner
        high, low = split2(inverse_ref[...])
        right = jnp.concatenate([high, high, low], axis=1)
        for k in range(outer * inner):
            d, flip = k // inner, k % inner
            high, low = split2(rows_refs[k][...])
            left = jnp.concatenate([high, low, high], axis=1)
            value = lax.dot_general(left, right, (((1,), (1,)), ((), ())), preferred_element_type=f32)
            chosen = lax.rem(o + outer - d, outer) * inner + (inner - 1 - y if flip else y)
            basis[pl.ds(pl.multiple_of(chosen * chunk, chunk), chunk), :] = value
            rounded[places[k] * chunk:(places[k] + 1) * chunk, :] = value
        step = 128
        for start in range(0, total, step):
            block = rounded[start:start + step, :].T.astype(bf16)
            first = lax.axis_index("gx") == 0
            turned[:half, start:start + step] = jnp.where(first, block[half:], block[:half])
            turned[half:, start:start + step] = jnp.where(first, block[:half], block[half:])

    return call(
        kernel, [jax.ShapeDtypeStruct((total, RANK), f32), held((RANK, total), bf16)],
        [VMEM_SPACE] * (1 + len(chunks)),
        flops=6 * total * RANK ** 2, moved=8 * total * RANK,
        scratch_shapes=[pltpu.VMEM((total, RANK), f32)],
    )(inverse, *chunks)


WIDTH = 256


def product(turned, flats, low, high):
    half = RANK // 2

    def kernel(turned_ref, *refs):
        flat_refs, (other, own) = refs[:-2], refs[-2:]
        for start in range(low, high, WIDTH):
            sums, depth = None, 0
            for flat in flat_refs:
                part = jnp.dot(
                    turned_ref[:, depth:depth + flat.shape[0]], flat[:, start:start + WIDTH],
                    preferred_element_type=f32,
                )
                depth += flat.shape[0]
                sums = part if sums is None else sums + part
            other[:, start - low:start - low + WIDTH] = sums[:half]
            own[:, start - low:start - low + WIDTH] = sums[half:]

    shape = (half, high - low)
    depth = turned.shape[1]
    return call(
        kernel, [held(shape, f32), held(shape, f32)], [VMEM_SPACE] * (1 + len(flats)),
        flops=2 * RANK * depth * (high - low), moved=2 * depth * (high - low),
    )(turned, *flats)


def finish(own, came, y_local, z_local):
    half = own[0].shape[0]
    pieces = len(own)
    cells = y_local // pieces
    stride = y_local + 1
    step = min(half, 32)

    def kernel(*refs):
        out, scratch, sems = refs[-3:]
        rounded = scratch[1]
        spread = scratch[0]
        copies = []
        for start in range(0, half, step):
            for y_cell in range(y_local):
                k, at = y_cell // cells, y_cell % cells * z_local
                spread[pl.ds(start * stride + y_cell, step, stride=stride), :] = (
                    refs[k][start:start + step, at:at + z_local]
                    + refs[pieces + k][start:start + step, at:at + z_local]
                )
            for r in range(start, start + step):
                rounded[r] = spread[r * stride:r * stride + y_local, :].astype(bf16)
            copy = pltpu.make_async_copy(
                rounded.at[pl.ds(start, step)], out.at[pl.ds(start, step)], sems.at[start // step]
            )
            copy.start()
            copies.append(copy)
        for copy in copies:
            copy.wait()

    return call(
        lambda *refs: kernel(*refs[:-3], (refs[-3], refs[-2]), refs[-1]),
        jax.ShapeDtypeStruct((half, y_local, z_local), bf16), [VMEM_SPACE] * (2 * pieces),
        out_specs=ANY_SPACE, moved=10 * half * y_local * z_local,
        scratch_shapes=[
            pltpu.VMEM((half * stride, z_local), f32), pltpu.VMEM((half, y_local, z_local), bf16),
            pltpu.SemaphoreType.DMA((half // step,)),
        ],
    )(*own, *came)


def local(field, sketch_seeds):
    x_local, y_local, z_local = field.shape
    count = lax.axis_size("yz")
    inner = 2 if count % 2 == 0 else 1
    outer = count // inner
    chunk = x_local // count

    def neighbour(value):
        return lax.ppermute(value, "yz", [(i, i ^ 1) for i in range(count)])

    def shift(value, d):
        pairs = [(i, (i // inner + d) % outer * inner + i % inner) for i in range(count)]
        return lax.ppermute(value, "yz", pairs)

    def other_core(value):
        return lax.ppermute(value, "gx", [(0, 1), (1, 0)])

    sizes = (outer, inner, chunk)
    order = sorted(range(1, outer), key=lambda d: -min(d, outer - d)) + [0]
    cut = (outer + 1) // 2
    groups = [group for group in (order[:cut], order[cut:]) if group]
    wanted, flats, sends, tables = [], [], [], None
    if inner == 2:
        for group in groups:
            pairs = [(d, 1) for d in group]
            (rows,), flat, tables = sketch_chunks(field, sketch_seeds, pairs, sizes, True, tables)
            sends.append(neighbour(rows))
            wanted += pairs
            flats.append(flat)
    parts = []
    for k, group in enumerate(groups):
        pairs = [(d, 0) for d in group]
        kept, flat, tables = sketch_chunks(
            field, sketch_seeds, pairs, sizes, False, tables
        )
        wanted += pairs
        flats.append(flat)
        if inner == 2:
            kept = merge(kept, sends[k])
        for j, d in enumerate(group):
            parts.append(shift(kept[j], d) if d else kept[j])
    own = total_of(parts)
    chunks = [None] * count
    near = [0] + sorted(range(1, outer), key=lambda d: min(d, outer - d))
    for d in near:
        came = shift(own, d) if d else own
        chunks[d * inner] = came
        if inner == 2:
            chunks[d * inner + 1] = neighbour(came)
    gram = gram_of(chunks)
    came = other_core(gram)
    inverse = inverse_factor(gram, came)
    places = [wanted.index(((outer - k // inner) % outer, k % inner)) for k in range(count)]
    basis, turned = solve_rows(chunks, inverse, sizes, places)
    columns = y_local * z_local
    own_parts, came_parts = [], []
    for k in range(PIECES):
        other, mine = product(
            turned, flats, columns * k // PIECES, columns * (k + 1) // PIECES
        )
        came_parts.append(other_core(other))
        own_parts.append(mine)
    core = finish(own_parts, came_parts, y_local, z_local)
    return (basis, core)


PIECES = 2


def solution(mesh):
    in_specs = (P(("grp", "gx"), "yz", None), P("grp"))
    out_specs = (P(("grp", "gx"), None), P(("grp", "gx"), "yz", None))

    return jax.shard_map(local, mesh=mesh, in_specs=in_specs, out_specs=out_specs, check_vma=False)
```

profile of v0, /device:TPU:0, one launch (start us, length us, event | category | flops | bytes accessed | tf_op | source)
XLA Modules:
  0.0 81.3 jit_solution(12456424913774136537)
XLA Ops:
  0.6 0.6 copy-done
  1.3 3.5 %shard_map.41 = (f32[256,256]{1,0:T(8,128)S(1)}, bf16[256,4096]{1,0:T(8,128)(2,1)S(1)}, bf16[128,256]{1,0:T(8,128)(2,1)S(1)}, f32[32,256]{1,0:T(8,128)S(1)}) custom-call(s32[6]{0:T(128)S(1)} %copy-done, bf16[1024,32,128]{2,1,0:T(8,128)(2,1)} %field_ref.7), custom_call_target="tpu_custom_call" | custom-call | flops 536870912 | bytes 2097152 | tf_op jit(solution)/shard_map/pallas_call | solution.py:131
  4.8 3.1 %collective-permute-start = (f32[256,256]{1,0:T(8,128)S(1)}, f32[256,256]{1,0:T(8,128)S(1)}, u32[]{:S(2)}, u32[]{:S(2)}) collective-permute-start(f32[256,256]{1,0:T(8,128)S(1)} %get-tuple-element.28), channel_id=1, source_target_pairs={{0,2},{2,0},{4,6},{6,4},{8,10},{10,8},{12,14},{14,12},{1,3},{3,1},... | collective-permute-start | bytes 786440 | tf_op jit(solution)/shard_map/ppermute | solution.py:379
  7.9 3.5 %shard_map.45 = (f32[256,256]{1,0:T(8,128)S(1)}, bf16[256,4096]{1,0:T(8,128)(2,1)S(1)}) custom-call(s32[6]{0:T(128)S(1)} %copy-done, bf16[1024,32,128]{2,1,0:T(8,128)(2,1)} %field_ref.7, bf16[128,256]{1,0:T(8,128)(2,1)S(1)} %get-tuple-element.24.refs_0_, f32[32,256]{1,0:T(8,128)S(1)} %get-tuple-element.25.refs_1_), custom_call_target="tpu_custom_call" | custom-call | flops 536870912 | bytes 2097152 | tf_op jit(solution)/shard_map/pallas_call | solution.py:131
  11.5 3.5 %shard_map.44 = (f32[128,256]{1,0:T(8,128)S(1)}, f32[128,256]{1,0:T(8,128)S(1)}, bf16[256,4096]{1,0:T(8,128)(2,1)S(1)}) custom-call(s32[6]{0:T(128)S(1)} %copy-done, bf16[1024,32,128]{2,1,0:T(8,128)(2,1)} %field_ref.7, bf16[128,256]{1,0:T(8,128)(2,1)S(1)} %get-tuple-element.24.refs_0_, f32[32,256]{1,0:T(8,128)S(1)} %get-tuple-element.25.refs_1_), custom_call_target="tpu_custom_call" | custom-call | flops 536870912 | bytes 2097152 | tf_op jit(solution)/shard_map/pallas_call | solution.py:131
  15.1 3.5 %shard_map.42 = (f32[128,256]{1,0:T(8,128)S(1)}, f32[128,256]{1,0:T(8,128)S(1)}, bf16[256,4096]{1,0:T(8,128)(2,1)S(1)}) custom-call(s32[6]{0:T(128)S(1)} %copy-done, bf16[1024,32,128]{2,1,0:T(8,128)(2,1)} %field_ref.7, bf16[128,256]{1,0:T(8,128)(2,1)S(1)} %get-tuple-element.24.refs_0_, f32[32,256]{1,0:T(8,128)S(1)} %get-tuple-element.25.refs_1_), custom_call_target="tpu_custom_call" | custom-call | flops 536870912 | bytes 2097152 | tf_op jit(solution)/shard_map/pallas_call | solution.py:131
  18.7 3.1 %collective-permute-start.1 = (f32[128,256]{1,0:T(8,128)S(1)}, f32[128,256]{1,0:T(8,128)S(1)}, u32[]{:S(2)}, u32[]{:S(2)}) collective-permute-start(f32[128,256]{1,0:T(8,128)S(1)} %get-tuple-element.29), channel_id=1, source_target_pairs={{0,8},{2,10},{4,12},{6,14},{8,0},{10,2},{12,4},{14,6},{1,9},{3,11}... | collective-permute-start | bytes 393224 | tf_op jit(solution)/shard_map/ppermute | solution.py:383
  21.8 1.6 %collective-permute-start.2 = (f32[128,256]{1,0:T(8,128)S(1)}, f32[128,256]{1,0:T(8,128)S(1)}, u32[]{:S(2)}, u32[]{:S(2)}) collective-permute-start(f32[128,256]{1,0:T(8,128)S(1)} %get-tuple-element.30), channel_id=1, source_target_pairs={{0,4},{2,6},{4,8},{6,10},{8,12},{10,14},{12,0},{14,2},{1,5},{3,7},... | collective-permute-start | bytes 393224 | tf_op jit(solution)/shard_map/ppermute | solution.py:383
  23.4 2.3 %collective-permute-start.4 = (f32[128,256]{1,0:T(8,128)S(1)}, f32[128,256]{1,0:T(8,128)S(1)}, u32[]{:S(2)}, u32[]{:S(2)}) collective-permute-start(f32[128,256]{1,0:T(8,128)S(1)} %get-tuple-element.34), channel_id=1, source_target_pairs={{0,12},{2,14},{4,0},{6,2},{8,4},{10,6},{12,8},{14,10},{1,13},{3,15... | collective-permute-start | bytes 393224 | tf_op jit(solution)/shard_map/ppermute | solution.py:383
  25.7 5.8 %collective-permute-done.1.refs_0_ = f32[128,256]{1,0:T(8,128)S(1)} collective-permute-done((f32[128,256]{1,0:T(8,128)S(1)}, f32[128,256]{1,0:T(8,128)S(1)}, u32[]{:S(2)}, u32[]{:S(2)}) %collective-permute-start.1) | collective-permute-done | bytes 131104 | tf_op jit(solution)/shard_map/ppermute | solution.py:383
  31.6 0.3 collective-permute-done.4.refs_2_
  31.9 2.5 %collective-permute-start.10 = (f32[128,256]{1,0:T(8,128)S(1)}, f32[128,256]{1,0:T(8,128)S(1)}, u32[]{:S(2)}, u32[]{:S(2)}) collective-permute-start(f32[128,256]{1,0:T(8,128)S(1)} %shard_map.47.refs_0_), channel_id=1, source_target_pairs={{0,12},{2,14},{4,0},{6,2},{8,4},{10,6},{12,8},{14,10},{1,13},{3,15... | collective-permute-start | bytes 393224 | tf_op jit(solution)/shard_map/ppermute | solution.py:383
  34.3 1.7 %collective-permute-start.8 = (f32[128,256]{1,0:T(8,128)S(1)}, f32[128,256]{1,0:T(8,128)S(1)}, u32[]{:S(2)}, u32[]{:S(2)}) collective-permute-start(f32[128,256]{1,0:T(8,128)S(1)} %shard_map.47.refs_0_), channel_id=1, source_target_pairs={{0,8},{2,10},{4,12},{6,14},{8,0},{10,2},{12,4},{14,6},{1,9},{3,11}... | collective-permute-start | bytes 393224 | tf_op jit(solution)/shard_map/ppermute | solution.py:383
  36.0 1.9 %collective-permute-start.6 = (f32[128,256]{1,0:T(8,128)S(1)}, f32[128,256]{1,0:T(8,128)S(1)}, u32[]{:S(2)}, u32[]{:S(2)}) collective-permute-start(f32[128,256]{1,0:T(8,128)S(1)} %shard_map.47.refs_0_), channel_id=1, source_target_pairs={{0,4},{2,6},{4,8},{6,10},{8,12},{10,14},{12,0},{14,2},{1,5},{3,7},... | collective-permute-start | bytes 393224 | tf_op jit(solution)/shard_map/ppermute | solution.py:383
  37.9 1.5 %collective-permute-start.5 = (f32[128,256]{1,0:T(8,128)S(1)}, f32[128,256]{1,0:T(8,128)S(1)}, u32[]{:S(2)}, u32[]{:S(2)}) collective-permute-start(f32[128,256]{1,0:T(8,128)S(1)} %shard_map.47.refs_0_), channel_id=1, source_target_pairs={{0,2},{2,0},{4,6},{6,4},{8,10},{10,8},{12,14},{14,12},{1,3},{3,1},... | collective-permute-start | bytes 393224 | tf_op jit(solution)/shard_map/ppermute | solution.py:379
  39.5 0.5 collective-permute-start.11
  40.0 7.8 %collective-permute-done.8.refs_4_ = f32[128,256]{1,0:T(8,128)S(1)} collective-permute-done((f32[128,256]{1,0:T(8,128)S(1)}, f32[128,256]{1,0:T(8,128)S(1)}, u32[]{:S(2)}, u32[]{:S(2)}) %collective-permute-start.8) | collective-permute-done | bytes 131104 | tf_op jit(solution)/shard_map/ppermute | solution.py:383
  47.8 1.5 %collective-permute-start.9 = (f32[128,256]{1,0:T(8,128)S(1)}, f32[128,256]{1,0:T(8,128)S(1)}, u32[]{:S(2)}, u32[]{:S(2)}) collective-permute-start(f32[128,256]{1,0:T(8,128)S(1)} %collective-permute-done.8.refs_4_), channel_id=1, source_target_pairs={{0,2},{2,0},{4,6},{6,4},{8,10},{10,8},{12,14},{14,12},{1,3},{3,1},... | collective-permute-start | bytes 393224 | tf_op jit(solution)/shard_map/ppermute | solution.py:379
  49.3 0.5 collective-permute-start.7
  49.8 4.0 %collective-permute-done.9.refs_5_ = f32[128,256]{1,0:T(8,128)S(1)} collective-permute-done((f32[128,256]{1,0:T(8,128)S(1)}, f32[128,256]{1,0:T(8,128)S(1)}, u32[]{:S(2)}, u32[]{:S(2)}) %collective-permute-start.9) | collective-permute-done | bytes 131104 | tf_op jit(solution)/shard_map/ppermute | solution.py:379
  53.8 1.4 %collective-permute-done.7.refs_3_ = f32[128,256]{1,0:T(8,128)S(1)} collective-permute-done((f32[128,256]{1,0:T(8,128)S(1)}, f32[128,256]{1,0:T(8,128)S(1)}, u32[]{:S(2)}, u32[]{:S(2)}) %collective-permute-start.7) | collective-permute-done | bytes 131104 | tf_op jit(solution)/shard_map/ppermute | solution.py:379
  55.2 0.8 shard_map.48.gram
  56.1 1.5 %collective-permute-done.12.came = f32[256,256]{1,0:T(8,128)S(1)} collective-permute-done((f32[256,256]{1,0:T(8,128)S(1)}, f32[256,256]{1,0:T(8,128)S(1)}, u32[]{:S(2)}, u32[]{:S(2)}) %collective-permute-start.12) | collective-permute-done | bytes 262176 | tf_op jit(solution)/shard_map/ppermute | solution.py:386
  57.6 13.6 %shard_map.49.inverse_ref = f32[256,256]{1,0:T(8,128)S(1)} custom-call(f32[256,256]{1,0:T(8,128)S(1)} %shard_map.48.gram, f32[256,256]{1,0:T(8,128)S(1)} %collective-permute-done.12.came), custom_call_target="tpu_custom_call" | custom-call | flops 50331648 | bytes 524288 | tf_op jit(solution)/shard_map/pallas_call | solution.py:205
  71.2 2.2 %shard_map.50 = (f32[1024,256]{1,0:T(8,128)}, bf16[256,1024]{1,0:T(8,128)(2,1)S(1)}) custom-call(f32[256,256]{1,0:T(8,128)S(1)} %shard_map.49.inverse_ref, f32[128,256]{1,0:T(8,128)S(1)} %shard_map.47.refs_0_, f32[128,256]{1,0:T(8,128)S(1)} %collective-permute-done.5.refs_1_, f32[128,256]{1,0:T(8,128)S(1)} %collective-permute-done.6.refs_2_, ...), custom_call_target="tpu_custom_call" | custom-call | flops 402653184 | bytes 2097152 | tf_op jit(solution)/shard_map/pallas_call | solution.py:295
  73.3 1.2 %shard_map.52 = (f32[128,2048]{1,0:T(8,128)S(1)}, f32[128,2048]{1,0:T(8,128)S(1)}) custom-call(bf16[256,1024]{1,0:T(8,128)(2,1)S(1)} %get-tuple-element.37.turned_ref, bf16[256,4096]{1,0:T(8,128)(2,1)S(1)} %get-tuple-element.38.refs_0_, bf16[256,4096]{1,0:T(8,128)(2,1)S(1)} %get-tuple-element.39.refs_1_, bf16[256,4096]{1,0:T(8,128)(2,1)S(1)} %get-tuple-element.40.refs_2_, ...), custom_call_target="tpu_custom_call" | custom-call | flops 1073741824 | bytes 4194304 | tf_op jit(solution)/shard_map/pallas_call | solution.py:325
  74.6 1.2 %shard_map.51 = (f32[128,2048]{1,0:T(8,128)S(1)}, f32[128,2048]{1,0:T(8,128)S(1)}) custom-call(bf16[256,1024]{1,0:T(8,128)(2,1)S(1)} %get-tuple-element.37.turned_ref, bf16[256,4096]{1,0:T(8,128)(2,1)S(1)} %get-tuple-element.38.refs_0_, bf16[256,4096]{1,0:T(8,128)(2,1)S(1)} %get-tuple-element.39.refs_1_, bf16[256,4096]{1,0:T(8,128)(2,1)S(1)} %get-tuple-element.40.refs_2_, ...), custom_call_target="tpu_custom_call" | custom-call | flops 1073741824 | bytes 4194304 | tf_op jit(solution)/shard_map/pallas_call | solution.py:325
  75.9 0.2 collective-permute-start.14
  76.1 0.4 collective-permute-start.13
  76.4 2.1 %collective-permute-done.14.refs_3_ = f32[128,2048]{1,0:T(8,128)S(1)} collective-permute-done((f32[128,2048]{1,0:T(8,128)S(1)}, f32[128,2048]{1,0:T(8,128)S(1)}, u32[]{:S(2)}, u32[]{:S(2)}) %collective-permute-start.14) | collective-permute-done | bytes 1048608 | tf_op jit(solution)/shard_map/ppermute | solution.py:386
  78.6 1.5 %collective-permute-done.13.refs_2_ = f32[128,2048]{1,0:T(8,128)S(1)} collective-permute-done((f32[128,2048]{1,0:T(8,128)S(1)}, f32[128,2048]{1,0:T(8,128)S(1)}, u32[]{:S(2)}, u32[]{:S(2)}) %collective-permute-start.13) | collective-permute-done | bytes 1048608 | tf_op jit(solution)/shard_map/ppermute | solution.py:386
  80.1 1.1 %shard_map.53 = bf16[128,32,128]{2,1,0:T(8,128)(2,1)} custom-call(f32[128,2048]{1,0:T(8,128)S(1)} %get-tuple-element.42.refs_0_, f32[128,2048]{1,0:T(8,128)S(1)} %get-tuple-element.43.refs_1_, f32[128,2048]{1,0:T(8,128)S(1)} %collective-permute-done.13.refs_2_, f32[128,2048]{1,0:T(8,128)S(1)} %collective-permute-done.14.refs_3_), custom_call_target="tpu_custom_call" | custom-call | bytes 5242880 | tf_op jit(solution)/shard_map/pallas_call | solution.py:360
  (13 shorter events, 0.3 us)
Async XLA Ops:
  0.6 0.7 copy-start
  4.8 13.8 %collective-permute-start = (f32[256,256]{1,0:T(8,128)S(1)}, f32[256,256]{1,0:T(8,128)S(1)}, u32[]{:S(2)}, u32[]{:S(2)}) collective-permute-start(f32[256,256]{1,0:T(8,128)S(1)} %get-tuple-element.28), channel_id=1, source_target_pairs={{0,2},{2,0},{4,6},{6,4},{8,10},{10,8},{12,14},{14,12},{1,3},{3,1},... | collective-permute-start | bytes 786440 | tf_op jit(solution)/shard_map/ppermute | solution.py:379
  11.4 12.0 %collective-permute-start.3 = (f32[256,256]{1,0:T(8,128)S(1)}, f32[256,256]{1,0:T(8,128)S(1)}, u32[]{:S(2)}, u32[]{:S(2)}) collective-permute-start(f32[256,256]{1,0:T(8,128)S(1)} %get-tuple-element.33), channel_id=1, source_target_pairs={{0,2},{2,0},{4,6},{6,4},{8,10},{10,8},{12,14},{14,12},{1,3},{3,1},... | collective-permute-start | bytes 786440 | tf_op jit(solution)/shard_map/ppermute | solution.py:379
  18.7 12.9 %collective-permute-start.1 = (f32[128,256]{1,0:T(8,128)S(1)}, f32[128,256]{1,0:T(8,128)S(1)}, u32[]{:S(2)}, u32[]{:S(2)}) collective-permute-start(f32[128,256]{1,0:T(8,128)S(1)} %get-tuple-element.29), channel_id=1, source_target_pairs={{0,8},{2,10},{4,12},{6,14},{8,0},{10,2},{12,4},{14,6},{1,9},{3,11}... | collective-permute-start | bytes 393224 | tf_op jit(solution)/shard_map/ppermute | solution.py:383
  21.8 9.8 %collective-permute-start.2 = (f32[128,256]{1,0:T(8,128)S(1)}, f32[128,256]{1,0:T(8,128)S(1)}, u32[]{:S(2)}, u32[]{:S(2)}) collective-permute-start(f32[128,256]{1,0:T(8,128)S(1)} %get-tuple-element.30), channel_id=1, source_target_pairs={{0,4},{2,6},{4,8},{6,10},{8,12},{10,14},{12,0},{14,2},{1,5},{3,7},... | collective-permute-start | bytes 393224 | tf_op jit(solution)/shard_map/ppermute | solution.py:383
  23.4 8.4 %collective-permute-start.4 = (f32[128,256]{1,0:T(8,128)S(1)}, f32[128,256]{1,0:T(8,128)S(1)}, u32[]{:S(2)}, u32[]{:S(2)}) collective-permute-start(f32[128,256]{1,0:T(8,128)S(1)} %get-tuple-element.34), channel_id=1, source_target_pairs={{0,12},{2,14},{4,0},{6,2},{8,4},{10,6},{12,8},{14,10},{1,13},{3,15... | collective-permute-start | bytes 393224 | tf_op jit(solution)/shard_map/ppermute | solution.py:383
  31.9 7.6 %collective-permute-start.10 = (f32[128,256]{1,0:T(8,128)S(1)}, f32[128,256]{1,0:T(8,128)S(1)}, u32[]{:S(2)}, u32[]{:S(2)}) collective-permute-start(f32[128,256]{1,0:T(8,128)S(1)} %shard_map.47.refs_0_), channel_id=1, source_target_pairs={{0,12},{2,14},{4,0},{6,2},{8,4},{10,6},{12,8},{14,10},{1,13},{3,15... | collective-permute-start | bytes 393224 | tf_op jit(solution)/shard_map/ppermute | solution.py:383
  34.3 13.4 %collective-permute-start.8 = (f32[128,256]{1,0:T(8,128)S(1)}, f32[128,256]{1,0:T(8,128)S(1)}, u32[]{:S(2)}, u32[]{:S(2)}) collective-permute-start(f32[128,256]{1,0:T(8,128)S(1)} %shard_map.47.refs_0_), channel_id=1, source_target_pairs={{0,8},{2,10},{4,12},{6,14},{8,0},{10,2},{12,4},{14,6},{1,9},{3,11}... | collective-permute-start | bytes 393224 | tf_op jit(solution)/shard_map/ppermute | solution.py:383
  36.0 13.3 %collective-permute-start.6 = (f32[128,256]{1,0:T(8,128)S(1)}, f32[128,256]{1,0:T(8,128)S(1)}, u32[]{:S(2)}, u32[]{:S(2)}) collective-permute-start(f32[128,256]{1,0:T(8,128)S(1)} %shard_map.47.refs_0_), channel_id=1, source_target_pairs={{0,4},{2,6},{4,8},{6,10},{8,12},{10,14},{12,0},{14,2},{1,5},{3,7},... | collective-permute-start | bytes 393224 | tf_op jit(solution)/shard_map/ppermute | solution.py:383
  37.9 11.9 %collective-permute-start.5 = (f32[128,256]{1,0:T(8,128)S(1)}, f32[128,256]{1,0:T(8,128)S(1)}, u32[]{:S(2)}, u32[]{:S(2)}) collective-permute-start(f32[128,256]{1,0:T(8,128)S(1)} %shard_map.47.refs_0_), channel_id=1, source_target_pairs={{0,2},{2,0},{4,6},{6,4},{8,10},{10,8},{12,14},{14,12},{1,3},{3,1},... | collective-permute-start | bytes 393224 | tf_op jit(solution)/shard_map/ppermute | solution.py:379
  39.5 10.3 %collective-permute-start.11 = (f32[128,256]{1,0:T(8,128)S(1)}, f32[128,256]{1,0:T(8,128)S(1)}, u32[]{:S(2)}, u32[]{:S(2)}) collective-permute-start(f32[128,256]{1,0:T(8,128)S(1)} %collective-permute-done.10.refs_6_), channel_id=1, source_target_pairs={{0,2},{2,0},{4,6},{6,4},{8,10},{10,8},{12,14},{14,12},{1,3},{3,1},... | collective-permute-start | bytes 393224 | tf_op jit(solution)/shard_map/ppermute | solution.py:379
  47.8 6.0 %collective-permute-start.9 = (f32[128,256]{1,0:T(8,128)S(1)}, f32[128,256]{1,0:T(8,128)S(1)}, u32[]{:S(2)}, u32[]{:S(2)}) collective-permute-start(f32[128,256]{1,0:T(8,128)S(1)} %collective-permute-done.8.refs_4_), channel_id=1, source_target_pairs={{0,2},{2,0},{4,6},{6,4},{8,10},{10,8},{12,14},{14,12},{1,3},{3,1},... | collective-permute-start | bytes 393224 | tf_op jit(solution)/shard_map/ppermute | solution.py:379
  49.3 5.9 %collective-permute-start.7 = (f32[128,256]{1,0:T(8,128)S(1)}, f32[128,256]{1,0:T(8,128)S(1)}, u32[]{:S(2)}, u32[]{:S(2)}) collective-permute-start(f32[128,256]{1,0:T(8,128)S(1)} %collective-permute-done.6.refs_2_), channel_id=1, source_target_pairs={{0,2},{2,0},{4,6},{6,4},{8,10},{10,8},{12,14},{14,12},{1,3},{3,1},... | collective-permute-start | bytes 393224 | tf_op jit(solution)/shard_map/ppermute | solution.py:379
  56.0 1.6 %collective-permute-start.12 = (f32[256,256]{1,0:T(8,128)S(1)}, f32[256,256]{1,0:T(8,128)S(1)}, u32[]{:S(2)}, u32[]{:S(2)}) collective-permute-start(f32[256,256]{1,0:T(8,128)S(1)} %shard_map.48.gram), channel_id=1, source_target_pairs={{0,1},{1,0},{2,3},{3,2},{4,5},{5,4},{6,7},{7,6},{8,9},{9,8},{10,11... | collective-permute-start | bytes 786440 | tf_op jit(solution)/shard_map/ppermute | solution.py:386
  75.9 2.7 %collective-permute-start.14 = (f32[128,2048]{1,0:T(8,128)S(1)}, f32[128,2048]{1,0:T(8,128)S(1)}, u32[]{:S(2)}, u32[]{:S(2)}) collective-permute-start(f32[128,2048]{1,0:T(8,128)S(1)} %get-tuple-element.45), channel_id=1, source_target_pairs={{0,1},{1,0},{2,3},{3,2},{4,5},{5,4},{6,7},{7,6},{8,9},{9,8},{10,11... | collective-permute-start | bytes 3145736 | tf_op jit(solution)/shard_map/ppermute | solution.py:386
  76.1 4.0 %collective-permute-start.13 = (f32[128,2048]{1,0:T(8,128)S(1)}, f32[128,2048]{1,0:T(8,128)S(1)}, u32[]{:S(2)}, u32[]{:S(2)}) collective-permute-start(f32[128,2048]{1,0:T(8,128)S(1)} %get-tuple-element.44), channel_id=1, source_target_pairs={{0,1},{1,0},{2,3},{3,2},{4,5},{5,4},{6,7},{7,6},{8,9},{9,8},{10,11... | collective-permute-start | bytes 3145736 | tf_op jit(solution)/shard_map/ppermute | solution.py:386
where the time goes:
time: 81.5 us; the launch traced here: 81.3 us
  Pallas kernels  34.4 us (42%)
  waiting for transfers between devices  24.5 us (30%)
  starting transfers between devices  20.9 us (26%)
  between operations  0.9 us (1%)
    pallas_call x4, Pallas kernels, sketch_chunks(): call(kernel, out_shape, in_specs, flops=2 * total * y_local * z_local * R...  14.2 us
    ppermute x6, waiting for transfers between devices, shift(): return lax.ppermute(value, 'yz', pairs)  13.9 us
    pallas_call x1, Pallas kernels, inverse_factor(): call(inverse_factor_kernel, held(gram.shape, f32), [VMEM_SPACE] * 2, flop...  13.6 us
    ppermute x6, starting transfers between devices, shift(): return lax.ppermute(value, 'yz', pairs)  13.1 us
    ppermute x6, starting transfers between devices, neighbour(): return lax.ppermute(value, 'yz', [(i, i ^ 1) for i in range(count)])  7.19 us
    ppermute x6, waiting for transfers between devices, neighbour(): return lax.ppermute(value, 'yz', [(i, i ^ 1) for i in range(count)])  5.37 us
    ppermute x3, waiting for transfers between devices, other_core(): return lax.ppermute(value, 'gx', [(0, 1), (1, 0)])  5.17 us
    pallas_call x2, Pallas kernels, product(): call(kernel, [held(shape, f32), held(shape, f32)], [VMEM_SPACE] * (1 + le...  2.49 us
  transfers between devices with their start and end apart: 15, of which 8 were waited for; matrix products, arithmetic and copies ran while one was open for 0% of the time, Pallas kernels for 13%

commit v1 on v0

--- a/solution.py
+++ b/solution.py
@@ -51,90 +51,111 @@
     )
 
 
-def sketch_chunks(field, seeds, wanted, sizes, joined, tables=None):
+CELLS = 4
+
+
+def sketch_chunks(source, seeds, wanted, first, span, sizes, joined, tables=None):
     outer, inner, chunk = sizes
-    _, y_local, z_local = field.shape
+    x_local, y_local, z_local = source.shape
     sub = min(SUB, chunk)
     stride = y_local + 1
     parts = chunk // sub
-    total = len(wanted) * chunk
-
-    def kernel(seeds_ref, field_ref, *refs):
+    total = span * chunk
+    opening = tables is None
+
+    def kernel(*refs):
         refs = list(refs)
-        if tables is not None:
+        seeds_ref = refs.pop(0) if opening else None
+        source_ref = refs.pop(0)
+        if not opening:
             omega_z, omega_y = refs.pop(0), refs.pop(0)
-        outs = [refs.pop(0) for _ in range(1 if joined else len(wanted))]
+        outs = [refs.pop(0) for _ in range(1 if joined else span)]
         flat = refs.pop(0)
-        if tables is None:
-            omega_z, omega_y = refs.pop(0), refs.pop(0)
-        rows, first, second, sems = refs
-        me = lax.axis_index("yz")
-        o, y = me // inner, me % inner
         copies = []
-        for k, (d, flip) in enumerate(wanted):
-            chosen = lax.rem(o + d, outer) * inner + (inner - 1 - y if flip else y)
-            copy = pltpu.make_async_copy(
-                field_ref.at[pl.ds(chosen * chunk, chunk)], rows.at[pl.ds(k * chunk, chunk)], sems.at[k]
-            )
-            copy.start()
-            copies.append(copy)
-        if tables is None:
+        if opening:
+            rows, omega_z, omega_y = refs.pop(0), refs.pop(0), refs.pop(0)
+            sems = refs.pop()
+            me = lax.axis_index("yz")
+            o, y = me // inner, me % inner
+            for k, (d, flip) in enumerate(wanted):
+                chosen = lax.rem(o + d, outer) * inner + (inner - 1 - y if flip else y)
+                copy = pltpu.make_async_copy(
+                    source_ref.at[pl.ds(chosen * chunk, chunk)],
+                    rows.at[pl.ds(k * chunk, chunk)],
+                    sems.at[k],
+                )
+                copy.start()
+                copies.append(copy)
             omega_z[...] = omega_table(
                 seeds_ref[3], seeds_ref[4], seeds_ref[5], 0, z_local
             ).astype(bf16)
             omega_y[...] = omega_table(
                 seeds_ref[0], seeds_ref[1], seeds_ref[2], me * y_local, y_local
             )
+        else:
+            rows = source_ref
+        scratch = refs
         table_z = omega_z[...]
-        scratch = (first, second)
 
         def spread(block):
-            if block % parts == 0:
-                copies[block // parts].wait()
+            if opening and block % parts == 0:
+                copies[first + block // parts].wait()
             for x in range(sub):
-                scratch[block % 2][x * stride:x * stride + y_local, :] = rows[block * sub + x].astype(f32)
+                scratch[block % 2][x * stride:x * stride + y_local, :] = (
+                    rows[first * chunk + block * sub + x].astype(f32)
+                )
 
         spread(0)
-        for block in range(len(wanted) * parts):
-            if block + 1 < len(wanted) * parts:
+        for block in range(span * parts):
+            if block + 1 < span * parts:
                 spread(block + 1)
             low = block * sub
             sums = None
-            for y_cell in range(y_local):
-                cells = scratch[block % 2][pl.ds(y_cell, sub, stride=stride), :].astype(bf16)
-                flat[low:low + sub, y_cell * z_local:(y_cell + 1) * z_local] = cells
-                part = jnp.dot(cells, table_z, preferred_element_type=f32)
-                part = part * omega_y[y_cell:y_cell + 1, :]
-                sums = part if sums is None else sums + part
+            for y_cell in range(0, y_local, CELLS):
+                cells = []
+                for y_at in range(y_cell, y_cell + CELLS):
+                    cell = scratch[block % 2][pl.ds(y_at, sub, stride=stride), :].astype(bf16)
+                    flat[low:low + sub, y_at * z_local:(y_at + 1) * z_local] = cell
+                    cells.append(cell)
+                parted = jnp.dot(
+                    jnp.concatenate(cells, axis=0), table_z, preferred_element_type=f32
+                )
+                for k in range(CELLS):
+                    part = parted[k * sub:(k + 1) * sub] * omega_y[y_cell + k:y_cell + k + 1, :]
+                    sums = part if sums is None else sums + part
             if joined:
                 outs[0][low:low + sub, :] = sums
             else:
                 start = block % parts * sub
                 outs[block // parts][start:start + sub, :] = sums
-
-    count = 1 if joined else len(wanted)
-    shape = jax.ShapeDtypeStruct((total if joined else chunk, RANK), f32)
+        for k, copy in enumerate(copies):
+            if not first <= k < first + span:
+                copy.wait()
+
+    count = 1 if joined else span
+    shape = held((total if joined else chunk, RANK), f32)
     out_shape = [shape] * count + [held((total, y_local * z_local), bf16)]
-    operands = [seeds, pltpu.with_memory_space_constraint(field, pltpu.HBM)]
-    in_specs = [SMEM_SPACE, HBM_SPACE]
-    if tables is None:
-        out_shape += [held((z_local, RANK), bf16), held((y_local, RANK), f32)]
+    scratch_shapes = [pltpu.VMEM((sub * stride, z_local), f32)] * 2
+    if opening:
+        operands = [seeds, pltpu.with_memory_space_constraint(source, pltpu.HBM)]
+        in_specs = [SMEM_SPACE, HBM_SPACE]
+        out_shape += [
+            held((x_local, y_local, z_local), bf16),
+            held((z_local, RANK), bf16),
+            held((y_local, RANK), f32),
+        ]
+        scratch_shapes = scratch_shapes + [pltpu.SemaphoreType.DMA((len(wanted),))]
     else:
-        operands += list(tables)
-        in_specs += [VMEM_SPACE] * 2
-    scratch_shapes = [
-        pltpu.VMEM((total, y_local, z_local), bf16),
-        pltpu.VMEM((sub * stride, z_local), f32),
-        pltpu.VMEM((sub * stride, z_local), f32),
-        pltpu.SemaphoreType.DMA((len(wanted),)),
-    ]
+        operands = [source] + list(tables)
+        in_specs = [VMEM_SPACE] * 3
     result = call(
         kernel, out_shape, in_specs,
         flops=2 * total * y_local * z_local * RANK, moved=2 * total * y_local * z_local,
         scratch_shapes=scratch_shapes,
     )(*operands)
-    tail = result[count + 1:] if tables is None else tables
-    return result[:count], result[count], tail
+    if opening:
+        source, tables = result[count + 1], result[count + 2:]
+    return result[:count], result[count], source, tables
 
 
 def split3(value):
@@ -293,7 +314,7 @@
             turned[half:, start:start + step] = jnp.where(first, block[:half], block[half:])
 
     return call(
-        kernel, [jax.ShapeDtypeStruct((total, RANK), f32), held((RANK, total), bf16)],
+        kernel, [held((total, RANK), f32), held((RANK, total), bf16)],
         [VMEM_SPACE] * (1 + len(chunks)),
         flops=6 * total * RANK ** 2, moved=8 * total * RANK,
         scratch_shapes=[pltpu.VMEM((total, RANK), f32)],
@@ -389,21 +410,22 @@
     order = sorted(range(1, outer), key=lambda d: -min(d, outer - d)) + [0]
     cut = (outer + 1) // 2
     groups = [group for group in (order[:cut], order[cut:]) if group]
-    wanted, flats, sends, tables = [], [], [], None
+    wanted = [(d, 1) for d in order if inner == 2] + [(d, 0) for d in order]
+    source, flats, sends, tables, at = field, [], [], None, 0
     if inner == 2:
         for group in groups:
-            pairs = [(d, 1) for d in group]
-            (rows,), flat, tables = sketch_chunks(field, sketch_seeds, pairs, sizes, True, tables)
+            (rows,), flat, source, tables = sketch_chunks(
+                source, sketch_seeds, wanted, at, len(group), sizes, True, tables
+            )
             sends.append(neighbour(rows))
-            wanted += pairs
+            at += len(group)
             flats.append(flat)
     parts = []
     for k, group in enumerate(groups):
-        pairs = [(d, 0) for d in group]
-        kept, flat, tables = sketch_chunks(
-            field, sketch_seeds, pairs, sizes, False, tables
+        kept, flat, source, tables = sketch_chunks(
+            source, sketch_seeds, wanted, at, len(group), sizes, False, tables
         )
-        wanted += pairs
+        at += len(group)
         flats.append(flat)
         if inner == 2:
             kept = merge(kept, sends[k])
@@ -434,7 +456,7 @@
     return (basis, core)
 
 
-PIECES = 2
+PIECES = 4
 
 
 def solution(mesh):

time: 81.5 us -> 78.3 us (0.961)
  Pallas kernels: 34.4 us -> 28.8 us
  starting transfers between devices: 20.9 us -> 22.9 us
  local copies, waits for them, and re-layouts: 0.65 us -> 1.62 us
    pallas_call x4, Pallas kernels: 14.2 us -> 9.12 us  [sketch_chunks(): call(kernel, out_shape, in_specs, flops=2 * total * y_local * z_local * R...]
    ppermute x6, waiting for transfers between devices: 5.37 us -> 7.72 us  [neighbour(): return lax.ppermute(value, 'yz', [(i, i ^ 1) for i in range(count)])]
    ppermute x3 -> x5, waiting for transfers between devices: 5.17 us -> 3.69 us  [other_core(): return lax.ppermute(value, 'gx', [(0, 1), (1, 0)])]
    ppermute x6, waiting for transfers between devices: 13.9 us -> 12.5 us  [shift(): return lax.ppermute(value, 'yz', pairs)]
    ppermute x6, starting transfers between devices: 7.19 us -> 8.48 us  [neighbour(): return lax.ppermute(value, 'yz', [(i, i ^ 1) for i in range(count)])]
    unnamed x2 -> x3, local copies, waits for them, and re-layouts: 0.65 us -> 1.62 us
    pallas_call x1, Pallas kernels: 2.16 us -> 1.32 us  [solve_rows(): call(kernel, [held((total, RANK), f32), held((RANK, total), bf16)], [VMEM...]
    pallas_call x2 -> x4, Pallas kernels: 2.49 us -> 2.84 us  [product(): call(kernel, [held(shape, f32), held(shape, f32)], [VMEM_SPACE] * (1 + le...]
  transfers between devices with their start and end apart: 15 -> 17, of which waited for: 8 -> 11; matrix products, arithmetic and copies ran while one was open for 0% -> 1% of each run, Pallas kernels for 13% -> 4%
where the time goes in v1:
time: 78.3 us; the launch traced here: 78.1 us
  Pallas kernels  28.8 us (37%)
  waiting for transfers between devices  23.9 us (31%)
  starting transfers between devices  22.9 us (29%)
  local copies, waits for them, and re-layouts  1.62 us (2%)
  between operations  0.91 us (1%)
    pallas_call x1, Pallas kernels, inverse_factor(): call(inverse_factor_kernel, held(gram.shape, f32), [VMEM_SPACE] * 2, flop...  13.6 us
    ppermute x6, starting transfers between devices, shift(): return lax.ppermute(value, 'yz', pairs)  13.2 us
    ppermute x6, waiting for transfers between devices, shift(): return lax.ppermute(value, 'yz', pairs)  12.5 us
    pallas_call x4, Pallas kernels, sketch_chunks(): call(kernel, out_shape, in_specs, flops=2 * total * y_local * z_local * R...  9.12 us
    ppermute x6, starting transfers between devices, neighbour(): return lax.ppermute(value, 'yz', [(i, i ^ 1) for i in range(count)])  8.48 us
    ppermute x6, waiting for transfers between devices, neighbour(): return lax.ppermute(value, 'yz', [(i, i ^ 1) for i in range(count)])  7.72 us
    ppermute x5, waiting for transfers between devices, other_core(): return lax.ppermute(value, 'gx', [(0, 1), (1, 0)])  3.69 us
    pallas_call x4, Pallas kernels, product(): call(kernel, [held(shape, f32), held(shape, f32)], [VMEM_SPACE] * (1 + le...  2.84 us
  transfers between devices with their start and end apart: 17, of which 11 were waited for; matrix products, arithmetic and copies ran while one was open for 1% of the time, Pallas kernels for 4%

profile of v1, /device:TPU:0, one launch (start us, length us, event | category | flops | bytes accessed | tf_op | source)
XLA Modules:
  0.0 78.1 jit_solution(10636771927911527651)
XLA Ops:
  1.3 4.0 %shard_map.41 = (f32[256,256]{1,0:T(8,128)S(1)}, bf16[256,4096]{1,0:T(8,128)(2,1)S(1)}, bf16[1024,32,128]{2,1,0:T(8,128)(2,1)S(1)}, bf16[128,256]{1,0:T(8,128)(2,1)S(1)}, f32[32,256]{1,0:T(8,128)S(1)}) custom-call(s32[6]{0:T(128)S(1)} %copy-done, bf16[1024,32,128]{2,1,0:T(8,128)(2,1)} %refs_1_.1), custom_call_target="tpu_custom_call" | custom-call | flops 536870912 | bytes 2097152 | tf_op jit(solution)/shard_map/pallas_call | solution.py:151
  5.3 1.7 %shard_map.45 = (f32[256,256]{1,0:T(8,128)S(1)}, bf16[256,4096]{1,0:T(8,128)(2,1)S(1)}) custom-call(bf16[1024,32,128]{2,1,0:T(8,128)(2,1)S(1)} %get-tuple-element.29.refs_0_, bf16[128,256]{1,0:T(8,128)(2,1)S(1)} %get-tuple-element.30.refs_1_, f32[32,256]{1,0:T(8,128)S(1)} %get-tuple-element.31.refs_2_), custom_call_target="tpu_custom_call" | custom-call | flops 536870912 | bytes 2097152 | tf_op jit(solution)/shard_map/pallas_call | solution.py:151
  7.0 3.1 %collective-permute-start.3 = (f32[256,256]{1,0:T(8,128)S(1)}, f32[256,256]{1,0:T(8,128)S(1)}, u32[]{:S(2)}, u32[]{:S(2)}) collective-permute-start(f32[256,256]{1,0:T(8,128)S(1)} %get-tuple-element.39), channel_id=1, source_target_pairs={{0,2},{2,0},{4,6},{6,4},{8,10},{10,8},{12,14},{14,12},{1,3},{3,1},... | collective-permute-start | bytes 786440 | tf_op jit(solution)/shard_map/ppermute | solution.py:400
  10.2 1.7 %shard_map.44 = (f32[128,256]{1,0:T(8,128)S(1)}, f32[128,256]{1,0:T(8,128)S(1)}, bf16[256,4096]{1,0:T(8,128)(2,1)S(1)}) custom-call(bf16[1024,32,128]{2,1,0:T(8,128)(2,1)S(1)} %get-tuple-element.29.refs_0_, bf16[128,256]{1,0:T(8,128)(2,1)S(1)} %get-tuple-element.30.refs_1_, f32[32,256]{1,0:T(8,128)S(1)} %get-tuple-element.31.refs_2_), custom_call_target="tpu_custom_call" | custom-call | flops 536870912 | bytes 2097152 | tf_op jit(solution)/shard_map/pallas_call | solution.py:151
  11.9 1.7 %shard_map.42 = (f32[128,256]{1,0:T(8,128)S(1)}, f32[128,256]{1,0:T(8,128)S(1)}, bf16[256,4096]{1,0:T(8,128)(2,1)S(1)}) custom-call(bf16[1024,32,128]{2,1,0:T(8,128)(2,1)S(1)} %get-tuple-element.29.refs_0_, bf16[128,256]{1,0:T(8,128)(2,1)S(1)} %get-tuple-element.30.refs_1_, f32[32,256]{1,0:T(8,128)S(1)} %get-tuple-element.31.refs_2_), custom_call_target="tpu_custom_call" | custom-call | flops 536870912 | bytes 2097152 | tf_op jit(solution)/shard_map/pallas_call | solution.py:151
  13.6 3.7 %collective-permute-done.3.refs_2_ = f32[256,256]{1,0:T(8,128)S(1)} collective-permute-done((f32[256,256]{1,0:T(8,128)S(1)}, f32[256,256]{1,0:T(8,128)S(1)}, u32[]{:S(2)}, u32[]{:S(2)}) %collective-permute-start.3) | collective-permute-done | bytes 262176 | tf_op jit(solution)/shard_map/ppermute | solution.py:400
  17.3 4.2 %collective-permute-start.4 = (f32[128,256]{1,0:T(8,128)S(1)}, f32[128,256]{1,0:T(8,128)S(1)}, u32[]{:S(2)}, u32[]{:S(2)}) collective-permute-start(f32[128,256]{1,0:T(8,128)S(1)} %get-tuple-element.40), channel_id=1, source_target_pairs={{0,12},{2,14},{4,0},{6,2},{8,4},{10,6},{12,8},{14,10},{1,13},{3,15... | collective-permute-start | bytes 393224 | tf_op jit(solution)/shard_map/ppermute | solution.py:404
  22.1 2.9 %collective-permute-start.1 = (f32[128,256]{1,0:T(8,128)S(1)}, f32[128,256]{1,0:T(8,128)S(1)}, u32[]{:S(2)}, u32[]{:S(2)}) collective-permute-start(f32[128,256]{1,0:T(8,128)S(1)} %get-tuple-element.35), channel_id=1, source_target_pairs={{0,8},{2,10},{4,12},{6,14},{8,0},{10,2},{12,4},{14,6},{1,9},{3,11}... | collective-permute-start | bytes 393224 | tf_op jit(solution)/shard_map/ppermute | solution.py:404
  24.9 1.6 %collective-permute-start.2 = (f32[128,256]{1,0:T(8,128)S(1)}, f32[128,256]{1,0:T(8,128)S(1)}, u32[]{:S(2)}, u32[]{:S(2)}) collective-permute-start(f32[128,256]{1,0:T(8,128)S(1)} %get-tuple-element.36), channel_id=1, source_target_pairs={{0,4},{2,6},{4,8},{6,10},{8,12},{10,14},{12,0},{14,2},{1,5},{3,7},... | collective-permute-start | bytes 393224 | tf_op jit(solution)/shard_map/ppermute | solution.py:404
  26.5 6.8 %collective-permute-done.1.refs_0_ = f32[128,256]{1,0:T(8,128)S(1)} collective-permute-done((f32[128,256]{1,0:T(8,128)S(1)}, f32[128,256]{1,0:T(8,128)S(1)}, u32[]{:S(2)}, u32[]{:S(2)}) %collective-permute-start.1) | collective-permute-done | bytes 131104 | tf_op jit(solution)/shard_map/ppermute | solution.py:404
  33.3 1.3 %collective-permute-start.10 = (f32[128,256]{1,0:T(8,128)S(1)}, f32[128,256]{1,0:T(8,128)S(1)}, u32[]{:S(2)}, u32[]{:S(2)}) collective-permute-start(f32[128,256]{1,0:T(8,128)S(1)} %shard_map.47.refs_0_), channel_id=1, source_target_pairs={{0,12},{2,14},{4,0},{6,2},{8,4},{10,6},{12,8},{14,10},{1,13},{3,15... | collective-permute-start | bytes 393224 | tf_op jit(solution)/shard_map/ppermute | solution.py:404
  34.7 0.8 collective-permute-start.6
  35.4 2.5 %collective-permute-start.8 = (f32[128,256]{1,0:T(8,128)S(1)}, f32[128,256]{1,0:T(8,128)S(1)}, u32[]{:S(2)}, u32[]{:S(2)}) collective-permute-start(f32[128,256]{1,0:T(8,128)S(1)} %shard_map.47.refs_0_), channel_id=1, source_target_pairs={{0,8},{2,10},{4,12},{6,14},{8,0},{10,2},{12,4},{14,6},{1,9},{3,11}... | collective-permute-start | bytes 393224 | tf_op jit(solution)/shard_map/ppermute | solution.py:404
  37.9 1.5 %collective-permute-start.5 = (f32[128,256]{1,0:T(8,128)S(1)}, f32[128,256]{1,0:T(8,128)S(1)}, u32[]{:S(2)}, u32[]{:S(2)}) collective-permute-start(f32[128,256]{1,0:T(8,128)S(1)} %shard_map.47.refs_0_), channel_id=1, source_target_pairs={{0,2},{2,0},{4,6},{6,4},{8,10},{10,8},{12,14},{14,12},{1,3},{3,1},... | collective-permute-start | bytes 393224 | tf_op jit(solution)/shard_map/ppermute | solution.py:400
  39.5 0.8 %collective-permute-start.11 = (f32[128,256]{1,0:T(8,128)S(1)}, f32[128,256]{1,0:T(8,128)S(1)}, u32[]{:S(2)}, u32[]{:S(2)}) collective-permute-start(f32[128,256]{1,0:T(8,128)S(1)} %collective-permute-done.10.refs_6_), channel_id=1, source_target_pairs={{0,2},{2,0},{4,6},{6,4},{8,10},{10,8},{12,14},{14,12},{1,3},{3,1},... | collective-permute-start | bytes 393224 | tf_op jit(solution)/shard_map/ppermute | solution.py:400
  40.3 4.2 %collective-permute-done.6.refs_2_ = f32[128,256]{1,0:T(8,128)S(1)} collective-permute-done((f32[128,256]{1,0:T(8,128)S(1)}, f32[128,256]{1,0:T(8,128)S(1)}, u32[]{:S(2)}, u32[]{:S(2)}) %collective-permute-start.6) | collective-permute-done | bytes 131104 | tf_op jit(solution)/shard_map/ppermute | solution.py:404
  44.4 1.5 %collective-permute-start.7 = (f32[128,256]{1,0:T(8,128)S(1)}, f32[128,256]{1,0:T(8,128)S(1)}, u32[]{:S(2)}, u32[]{:S(2)}) collective-permute-start(f32[128,256]{1,0:T(8,128)S(1)} %collective-permute-done.6.refs_2_), channel_id=1, source_target_pairs={{0,2},{2,0},{4,6},{6,4},{8,10},{10,8},{12,14},{14,12},{1,3},{3,1},... | collective-permute-start | bytes 393224 | tf_op jit(solution)/shard_map/ppermute | solution.py:400
  46.0 1.5 %collective-permute-done.8.refs_4_ = f32[128,256]{1,0:T(8,128)S(1)} collective-permute-done((f32[128,256]{1,0:T(8,128)S(1)}, f32[128,256]{1,0:T(8,128)S(1)}, u32[]{:S(2)}, u32[]{:S(2)}) %collective-permute-start.8) | collective-permute-done | bytes 131104 | tf_op jit(solution)/shard_map/ppermute | solution.py:404
  47.5 1.5 %collective-permute-start.9 = (f32[128,256]{1,0:T(8,128)S(1)}, f32[128,256]{1,0:T(8,128)S(1)}, u32[]{:S(2)}, u32[]{:S(2)}) collective-permute-start(f32[128,256]{1,0:T(8,128)S(1)} %collective-permute-done.8.refs_4_), channel_id=1, source_target_pairs={{0,2},{2,0},{4,6},{6,4},{8,10},{10,8},{12,14},{14,12},{1,3},{3,1},... | collective-permute-start | bytes 393224 | tf_op jit(solution)/shard_map/ppermute | solution.py:400
  49.0 0.9 %collective-permute-done.7.refs_3_ = f32[128,256]{1,0:T(8,128)S(1)} collective-permute-done((f32[128,256]{1,0:T(8,128)S(1)}, f32[128,256]{1,0:T(8,128)S(1)}, u32[]{:S(2)}, u32[]{:S(2)}) %collective-permute-start.7) | collective-permute-done | bytes 131104 | tf_op jit(solution)/shard_map/ppermute | solution.py:400
  49.9 2.6 %collective-permute-done.9.refs_5_ = f32[128,256]{1,0:T(8,128)S(1)} collective-permute-done((f32[128,256]{1,0:T(8,128)S(1)}, f32[128,256]{1,0:T(8,128)S(1)}, u32[]{:S(2)}, u32[]{:S(2)}) %collective-permute-start.9) | collective-permute-done | bytes 131104 | tf_op jit(solution)/shard_map/ppermute | solution.py:400
  52.5 0.8 %shard_map.48.gram = f32[256,256]{1,0:T(8,128)S(1)} custom-call(f32[128,256]{1,0:T(8,128)S(1)} %shard_map.47.refs_0_, f32[128,256]{1,0:T(8,128)S(1)} %collective-permute-done.5.refs_1_, f32[128,256]{1,0:T(8,128)S(1)} %collective-permute-done.6.refs_2_, f32[128,256]{1,0:T(8,128)S(1)} %collective-permute-done.7.refs_3_, ...), custom_call_target="tpu_custom_call" | custom-call | flops 536870912 | bytes 1048576 | tf_op jit(solution)/shard_map/pallas_call | solution.py:278
  53.3 1.5 %collective-permute-done.12.came = f32[256,256]{1,0:T(8,128)S(1)} collective-permute-done((f32[256,256]{1,0:T(8,128)S(1)}, f32[256,256]{1,0:T(8,128)S(1)}, u32[]{:S(2)}, u32[]{:S(2)}) %collective-permute-start.12) | collective-permute-done | bytes 262176 | tf_op jit(solution)/shard_map/ppermute | solution.py:407
  54.9 13.6 %shard_map.49.inverse_ref = f32[256,256]{1,0:T(8,128)S(1)} custom-call(f32[256,256]{1,0:T(8,128)S(1)} %shard_map.48.gram, f32[256,256]{1,0:T(8,128)S(1)} %collective-permute-done.12.came), custom_call_target="tpu_custom_call" | custom-call | flops 50331648 | bytes 524288 | tf_op jit(solution)/shard_map/pallas_call | solution.py:226
  68.5 1.3 %shard_map.50 = (f32[1024,256]{1,0:T(8,128)S(1)}, bf16[256,1024]{1,0:T(8,128)(2,1)S(1)}) custom-call(f32[256,256]{1,0:T(8,128)S(1)} %shard_map.49.inverse_ref, f32[128,256]{1,0:T(8,128)S(1)} %shard_map.47.refs_0_, f32[128,256]{1,0:T(8,128)S(1)} %collective-permute-done.5.refs_1_, f32[128,256]{1,0:T(8,128)S(1)} %collective-permute-done.6.refs_2_, ...), custom_call_target="tpu_custom_call" | custom-call | flops 402653184 | bytes 2097152 | tf_op jit(solution)/shard_map/pallas_call | solution.py:316
  69.8 0.7 shard_map.54
  70.5 0.7 shard_map.53
  71.2 0.7 shard_map.52
  73.8 1.0 %copy.4 = f32[1024,256]{1,0:T(8,128)} copy(f32[1024,256]{1,0:T(8,128)S(1)} %get-tuple-element.56) | data formatting | bytes 2097152
  75.4 0.7 collective-permute-done.14.refs_5_
  76.1 0.7 collective-permute-done.13.refs_4_
  76.9 1.1 %shard_map.55 = bf16[128,32,128]{2,1,0:T(8,128)(2,1)} custom-call(f32[128,1024]{1,0:T(8,128)S(1)} %get-tuple-element.48.refs_0_, f32[128,1024]{1,0:T(8,128)S(1)} %get-tuple-element.49.refs_1_, f32[128,1024]{1,0:T(8,128)S(1)} %get-tuple-element.50.refs_2_, f32[128,1024]{1,0:T(8,128)S(1)} %get-tuple-element.51.refs_3_, ...), custom_call_target="tpu_custom_call" | custom-call | bytes 5242880 | tf_op jit(solution)/shard_map/pallas_call | solution.py:381
  (20 shorter events, 3.9 us)
Async XLA Ops:
  0.6 0.7 copy-start
  7.0 10.2 %collective-permute-start.3 = (f32[256,256]{1,0:T(8,128)S(1)}, f32[256,256]{1,0:T(8,128)S(1)}, u32[]{:S(2)}, u32[]{:S(2)}) collective-permute-start(f32[256,256]{1,0:T(8,128)S(1)} %get-tuple-element.39), channel_id=1, source_target_pairs={{0,2},{2,0},{4,6},{6,4},{8,10},{10,8},{12,14},{14,12},{1,3},{3,1},... | collective-permute-start | bytes 786440 | tf_op jit(solution)/shard_map/ppermute | solution.py:400
  10.1 11.9 %collective-permute-start = (f32[256,256]{1,0:T(8,128)S(1)}, f32[256,256]{1,0:T(8,128)S(1)}, u32[]{:S(2)}, u32[]{:S(2)}) collective-permute-start(f32[256,256]{1,0:T(8,128)S(1)} %get-tuple-element.34), channel_id=1, source_target_pairs={{0,2},{2,0},{4,6},{6,4},{8,10},{10,8},{12,14},{14,12},{1,3},{3,1},... | collective-permute-start | bytes 786440 | tf_op jit(solution)/shard_map/ppermute | solution.py:400
  17.3 9.2 %collective-permute-start.4 = (f32[128,256]{1,0:T(8,128)S(1)}, f32[128,256]{1,0:T(8,128)S(1)}, u32[]{:S(2)}, u32[]{:S(2)}) collective-permute-start(f32[128,256]{1,0:T(8,128)S(1)} %get-tuple-element.40), channel_id=1, source_target_pairs={{0,12},{2,14},{4,0},{6,2},{8,4},{10,6},{12,8},{14,10},{1,13},{3,15... | collective-permute-start | bytes 393224 | tf_op jit(solution)/shard_map/ppermute | solution.py:404
  22.1 11.2 %collective-permute-start.1 = (f32[128,256]{1,0:T(8,128)S(1)}, f32[128,256]{1,0:T(8,128)S(1)}, u32[]{:S(2)}, u32[]{:S(2)}) collective-permute-start(f32[128,256]{1,0:T(8,128)S(1)} %get-tuple-element.35), channel_id=1, source_target_pairs={{0,8},{2,10},{4,12},{6,14},{8,0},{10,2},{12,4},{14,6},{1,9},{3,11}... | collective-permute-start | bytes 393224 | tf_op jit(solution)/shard_map/ppermute | solution.py:404
  24.9 8.4 %collective-permute-start.2 = (f32[128,256]{1,0:T(8,128)S(1)}, f32[128,256]{1,0:T(8,128)S(1)}, u32[]{:S(2)}, u32[]{:S(2)}) collective-permute-start(f32[128,256]{1,0:T(8,128)S(1)} %get-tuple-element.36), channel_id=1, source_target_pairs={{0,4},{2,6},{4,8},{6,10},{8,12},{10,14},{12,0},{14,2},{1,5},{3,7},... | collective-permute-start | bytes 393224 | tf_op jit(solution)/shard_map/ppermute | solution.py:404
  33.3 6.1 %collective-permute-start.10 = (f32[128,256]{1,0:T(8,128)S(1)}, f32[128,256]{1,0:T(8,128)S(1)}, u32[]{:S(2)}, u32[]{:S(2)}) collective-permute-start(f32[128,256]{1,0:T(8,128)S(1)} %shard_map.47.refs_0_), channel_id=1, source_target_pairs={{0,12},{2,14},{4,0},{6,2},{8,4},{10,6},{12,8},{14,10},{1,13},{3,15... | collective-permute-start | bytes 393224 | tf_op jit(solution)/shard_map/ppermute | solution.py:404
  34.7 9.8 %collective-permute-start.6 = (f32[128,256]{1,0:T(8,128)S(1)}, f32[128,256]{1,0:T(8,128)S(1)}, u32[]{:S(2)}, u32[]{:S(2)}) collective-permute-start(f32[128,256]{1,0:T(8,128)S(1)} %shard_map.47.refs_0_), channel_id=1, source_target_pairs={{0,4},{2,6},{4,8},{6,10},{8,12},{10,14},{12,0},{14,2},{1,5},{3,7},... | collective-permute-start | bytes 393224 | tf_op jit(solution)/shard_map/ppermute | solution.py:404
  35.4 12.1 %collective-permute-start.8 = (f32[128,256]{1,0:T(8,128)S(1)}, f32[128,256]{1,0:T(8,128)S(1)}, u32[]{:S(2)}, u32[]{:S(2)}) collective-permute-start(f32[128,256]{1,0:T(8,128)S(1)} %shard_map.47.refs_0_), channel_id=1, source_target_pairs={{0,8},{2,10},{4,12},{6,14},{8,0},{10,2},{12,4},{14,6},{1,9},{3,11}... | collective-permute-start | bytes 393224 | tf_op jit(solution)/shard_map/ppermute | solution.py:404
  37.9 11.0 %collective-permute-start.5 = (f32[128,256]{1,0:T(8,128)S(1)}, f32[128,256]{1,0:T(8,128)S(1)}, u32[]{:S(2)}, u32[]{:S(2)}) collective-permute-start(f32[128,256]{1,0:T(8,128)S(1)} %shard_map.47.refs_0_), channel_id=1, source_target_pairs={{0,2},{2,0},{4,6},{6,4},{8,10},{10,8},{12,14},{14,12},{1,3},{3,1},... | collective-permute-start | bytes 393224 | tf_op jit(solution)/shard_map/ppermute | solution.py:400
  39.5 9.5 %collective-permute-start.11 = (f32[128,256]{1,0:T(8,128)S(1)}, f32[128,256]{1,0:T(8,128)S(1)}, u32[]{:S(2)}, u32[]{:S(2)}) collective-permute-start(f32[128,256]{1,0:T(8,128)S(1)} %collective-permute-done.10.refs_6_), channel_id=1, source_target_pairs={{0,2},{2,0},{4,6},{6,4},{8,10},{10,8},{12,14},{14,12},{1,3},{3,1},... | collective-permute-start | bytes 393224 | tf_op jit(solution)/shard_map/ppermute | solution.py:400
  44.4 5.4 %collective-permute-start.7 = (f32[128,256]{1,0:T(8,128)S(1)}, f32[128,256]{1,0:T(8,128)S(1)}, u32[]{:S(2)}, u32[]{:S(2)}) collective-permute-start(f32[128,256]{1,0:T(8,128)S(1)} %collective-permute-done.6.refs_2_), channel_id=1, source_target_pairs={{0,2},{2,0},{4,6},{6,4},{8,10},{10,8},{12,14},{14,12},{1,3},{3,1},... | collective-permute-start | bytes 393224 | tf_op jit(solution)/shard_map/ppermute | solution.py:400
  47.5 5.0 %collective-permute-start.9 = (f32[128,256]{1,0:T(8,128)S(1)}, f32[128,256]{1,0:T(8,128)S(1)}, u32[]{:S(2)}, u32[]{:S(2)}) collective-permute-start(f32[128,256]{1,0:T(8,128)S(1)} %collective-permute-done.8.refs_4_), channel_id=1, source_target_pairs={{0,2},{2,0},{4,6},{6,4},{8,10},{10,8},{12,14},{14,12},{1,3},{3,1},... | collective-permute-start | bytes 393224 | tf_op jit(solution)/shard_map/ppermute | solution.py:400
  53.3 1.6 %collective-permute-start.12 = (f32[256,256]{1,0:T(8,128)S(1)}, f32[256,256]{1,0:T(8,128)S(1)}, u32[]{:S(2)}, u32[]{:S(2)}) collective-permute-start(f32[256,256]{1,0:T(8,128)S(1)} %shard_map.48.gram), channel_id=1, source_target_pairs={{0,1},{1,0},{2,3},{3,2},{4,5},{5,4},{6,7},{7,6},{8,9},{9,8},{10,11... | collective-permute-start | bytes 786440 | tf_op jit(solution)/shard_map/ppermute | solution.py:407
  72.7 2.1 %collective-permute-start.16 = (f32[128,1024]{1,0:T(8,128)S(1)}, f32[128,1024]{1,0:T(8,128)S(1)}, u32[]{:S(2)}, u32[]{:S(2)}) collective-permute-start(f32[128,1024]{1,0:T(8,128)S(1)} %get-tuple-element.55), channel_id=1, source_target_pairs={{0,1},{1,0},{2,3},{3,2},{4,5},{5,4},{6,7},{7,6},{8,9},{9,8},{10,11... | collective-permute-start | bytes 1572872 | tf_op jit(solution)/shard_map/ppermute | solution.py:407
  72.9 2.5 %collective-permute-start.15 = (f32[128,1024]{1,0:T(8,128)S(1)}, f32[128,1024]{1,0:T(8,128)S(1)}, u32[]{:S(2)}, u32[]{:S(2)}) collective-permute-start(f32[128,1024]{1,0:T(8,128)S(1)} %get-tuple-element.54), channel_id=1, source_target_pairs={{0,1},{1,0},{2,3},{3,2},{4,5},{5,4},{6,7},{7,6},{8,9},{9,8},{10,11... | collective-permute-start | bytes 1572872 | tf_op jit(solution)/shard_map/ppermute | solution.py:407
  73.2 2.9 %collective-permute-start.14 = (f32[128,1024]{1,0:T(8,128)S(1)}, f32[128,1024]{1,0:T(8,128)S(1)}, u32[]{:S(2)}, u32[]{:S(2)}) collective-permute-start(f32[128,1024]{1,0:T(8,128)S(1)} %get-tuple-element.53), channel_id=1, source_target_pairs={{0,1},{1,0},{2,3},{3,2},{4,5},{5,4},{6,7},{7,6},{8,9},{9,8},{10,11... | collective-permute-start | bytes 1572872 | tf_op jit(solution)/shard_map/ppermute | solution.py:407
  73.4 3.5 %collective-permute-start.13 = (f32[128,1024]{1,0:T(8,128)S(1)}, f32[128,1024]{1,0:T(8,128)S(1)}, u32[]{:S(2)}, u32[]{:S(2)}) collective-permute-start(f32[128,1024]{1,0:T(8,128)S(1)} %get-tuple-element.52), channel_id=1, source_target_pairs={{0,1},{1,0},{2,3},{3,2},{4,5},{5,4},{6,7},{7,6},{8,9},{9,8},{10,11... | collective-permute-start | bytes 1572872 | tf_op jit(solution)/shard_map/ppermute | solution.py:407

commit v2 on v1

--- a/solution.py
+++ b/solution.py
@@ -54,55 +54,58 @@
 CELLS = 4
 
 
-def sketch_chunks(source, seeds, wanted, first, span, sizes, joined, tables=None):
+def sketch_chunks(field, seeds, wanted, follow, sizes, joined, carried=None):
     outer, inner, chunk = sizes
-    x_local, y_local, z_local = source.shape
+    _, y_local, z_local = field.shape
     sub = min(SUB, chunk)
     stride = y_local + 1
     parts = chunk // sub
+    span = len(wanted)
     total = span * chunk
-    opening = tables is None
+    opening = carried is None
 
     def kernel(*refs):
         refs = list(refs)
-        seeds_ref = refs.pop(0) if opening else None
-        source_ref = refs.pop(0)
-        if not opening:
-            omega_z, omega_y = refs.pop(0), refs.pop(0)
+        field_ref, sems = refs.pop(0), refs.pop()
+        if opening:
+            seeds_ref, rows = refs.pop(0), refs.pop()
+        else:
+            rows, omega_z, omega_y = refs.pop(0), refs.pop(0), refs.pop(0)
         outs = [refs.pop(0) for _ in range(1 if joined else span)]
         flat = refs.pop(0)
+        later = refs.pop(0) if follow else None
+        if opening:
+            omega_z, omega_y = refs.pop(0), refs.pop(0)
+        me = lax.axis_index("yz")
+        o, y = me // inner, me % inner
+        moves = [(pair, rows, k) for k, pair in enumerate(wanted) if opening]
+        moves += [(pair, later, k) for k, pair in enumerate(follow)]
         copies = []
+        for (d, flip), target, k in moves:
+            chosen = lax.rem(o + d, outer) * inner + (inner - 1 - y if flip else y)
+            copy = pltpu.make_async_copy(
+                field_ref.at[pl.ds(chosen * chunk, chunk)],
+                target.at[pl.ds(k * chunk, chunk)],
+                sems.at[len(copies)],
+            )
+            copy.start()
+            copies.append(copy)
         if opening:
-            rows, omega_z, omega_y = refs.pop(0), refs.pop(0), refs.pop(0)
-            sems = refs.pop()
-            me = lax.axis_index("yz")
-            o, y = me // inner, me % inner
-            for k, (d, flip) in enumerate(wanted):
-                chosen = lax.rem(o + d, outer) * inner + (inner - 1 - y if flip else y)
-                copy = pltpu.make_async_copy(
-                    source_ref.at[pl.ds(chosen * chunk, chunk)],
-                    rows.at[pl.ds(k * chunk, chunk)],
-                    sems.at[k],
-                )
-                copy.start()
-                copies.append(copy)
             omega_z[...] = omega_table(
                 seeds_ref[3], seeds_ref[4], seeds_ref[5], 0, z_local
             ).astype(bf16)
             omega_y[...] = omega_table(
                 seeds_ref[0], seeds_ref[1], seeds_ref[2], me * y_local, y_local
             )
-        else:
-            rows = source_ref
         scratch = refs
         table_z = omega_z[...]
 
         def spread(block):
             if opening and block % parts == 0:
-                copies[first + block // parts].wait()
+                copies[block // parts].wait()
             for x in range(sub):
                 scratch[block % 2][x * stride:x * stride + y_local, :] = (
-                    rows[first * chunk + block * sub + x].astype(f32)
+                    rows[block * sub + x].astype(f32)
                 )
 
         spread(0)
@@ -128,34 +131,34 @@
             else:
                 start = block % parts * sub
                 outs[block // parts][start:start + sub, :] = sums
-        for k, copy in enumerate(copies):
-            if not first <= k < first + span:
-                copy.wait()
+        for copy in copies[span if opening else 0:]:
+            copy.wait()
 
     count = 1 if joined else span
     shape = held((total if joined else chunk, RANK), f32)
     out_shape = [shape] * count + [held((total, y_local * z_local), bf16)]
     scratch_shapes = [pltpu.VMEM((sub * stride, z_local), f32)] * 2
+    operands = [pltpu.with_memory_space_constraint(field, pltpu.HBM)]
+    if follow:
+        out_shape.append(held((len(follow) * chunk, y_local, z_local), bf16))
     if opening:
-        operands = [seeds, pltpu.with_memory_space_constraint(source, pltpu.HBM)]
-        in_specs = [SMEM_SPACE, HBM_SPACE]
-        out_shape += [
-            held((x_local, y_local, z_local), bf16),
-            held((z_local, RANK), bf16),
-            held((y_local, RANK), f32),
-        ]
-        scratch_shapes = scratch_shapes + [pltpu.SemaphoreType.DMA((len(wanted),))]
+        operands.append(seeds)
+        in_specs = [HBM_SPACE, SMEM_SPACE]
+        out_shape += [held((z_local, RANK), bf16), held((y_local, RANK), f32)]
+        scratch_shapes.append(pltpu.VMEM((total, y_local, z_local), bf16))
     else:
-        operands = [source] + list(tables)
-        in_specs = [VMEM_SPACE] * 3
+        operands += carried
+        in_specs = [HBM_SPACE] + [VMEM_SPACE] * 3
+    copies = len(follow) + (span if opening else 0)
+    scratch_shapes.append(pltpu.SemaphoreType.DMA((max(copies, 1),)))
     result = call(
         kernel, out_shape, in_specs,
         flops=2 * total * y_local * z_local * RANK, moved=2 * total * y_local * z_local,
         scratch_shapes=scratch_shapes,
     )(*operands)
-    if opening:
-        source, tables = result[count + 1], result[count + 2:]
-    return result[:count], result[count], source, tables
+    coming = list(result[count + 1:count + 2]) if follow else []
+    tables = list(result[-2:]) if opening else carried[1:]
+    return result[:count], result[count], coming + tables
 
 
 def split3(value):
@@ -171,55 +174,85 @@
 def inverse_factor_kernel(gram, came, out, state):
     size = gram.shape[0]
     state[...] = gram[...] + came[...]
-    lane = lax.broadcasted_iota(i32, (PANEL, 128), 1)
-    row = lax.broadcasted_iota(i32, (PANEL, 128), 0)
+    lane = lax.broadcasted_iota(i32, (8, 128), 1)
+    row = lax.broadcasted_iota(i32, (8, 128), 0)
+    zero = jnp.where(lane < 0, 1.0, 0.0).astype(f32)
+    groups = PANEL // 8
+
+    def over_rows(value, i):
+        return jnp.broadcast_to(value[i:i + 1], (8, 128))
+
+    def over_lanes(value, i):
+        return jnp.broadcast_to(value[:, i:i + 1], (8, 128))
+
     for low in range(0, size, PANEL):
         high = low + PANEL
         tile, offset = low // 128, low % 128
-        rows = [state[low:high, 0:128], state[low:high, 128:256]]
-        rows.append(jnp.where(lane == row + offset, 1.0, 0.0).astype(f32))
-        done = [[None] * PANEL for _ in rows]
-        for i in range(0, PANEL, 2):
-            first = jnp.broadcast_to(rows[tile][:, offset + i:offset + i + 1], (PANEL, 128))
-            second = jnp.broadcast_to(rows[tile][:, offset + i + 1:offset + i + 2], (PANEL, 128))
-            d11, d12, d22 = first[i:i + 1], second[i:i + 1], second[i + 1:i + 2]
-            scale = 1.0 / (d11 * d22 - d12 * d12)
-            k11, k12, k22 = d22 * scale, d12 * scale, d11 * scale
-            first = jnp.where(row > i + 1, first, 0.0)
-            second = jnp.where(row > i + 1, second, 0.0)
-            ratio = d12 / d11
-            root1, root2 = lax.rsqrt(d11), lax.rsqrt(d22 - ratio * d12)
+        rows = [
+            [state[low + 8 * q:low + 8 * q + 8, 128 * k:128 * k + 128] for q in range(groups)]
+            for k in range(2)
+        ]
+        rows.append(
+            [jnp.where(lane == row + (offset + 8 * q), 1.0, 0.0).astype(f32) for q in range(groups)]
+        )
+        done = [[None] * groups for _ in range(3)]
+        for g in range(groups):
+            base = offset + 8 * g
+            column = [
+                {q: over_lanes(rows[tile][q], base + m) + zero for q in range(g, groups)}
+                for m in range(8)
+            ]
+            scales, ratios = jnp.zeros((8, 128), f32), jnp.zeros((8, 128), f32)
+            for i in range(0, 8, 2):
+                d11, d12 = over_rows(column[i][g], i), over_rows(column[i + 1][g], i)
+                d22 = over_rows(column[i + 1][g], i + 1)
+                inverse = pl.reciprocal(d11 * d22 - d12 * d12)
+                k11, k12, k22 = d22 * inverse, d12 * inverse, d11 * inverse
+                ratio = d12 * pl.reciprocal(d11)
+                root1, root2 = lax.rsqrt(d11), lax.rsqrt(d22 - ratio * d12)
+                scales = jnp.where(row == i, root1, jnp.where(row == i + 1, root2, scales))
+                ratios = jnp.where(row == i + 1, ratio, ratios)
+                left, right = dict(column[i]), dict(column[i + 1])
+                left[g] = jnp.where(row > i + 1, left[g], 0.0)
+                right[g] = jnp.where(row > i + 1, right[g], 0.0)
+                for m in range(i + 2, 8):
+                    a, b = over_rows(column[m][g], i), over_rows(column[m][g], i + 1)
+                    first, second = k11 * a - k12 * b, k22 * b - k12 * a
+                    for q in range(g, groups):
+                        column[m][q] = column[m][q] - (left[q] * first + right[q] * second)
+                for k in range(3):
+                    a, b = over_rows(rows[k][g], i), over_rows(rows[k][g], i + 1)
+                    first, second = k11 * a - k12 * b, k22 * b - k12 * a
+                    for q in range(g if i + 2 < 8 else g + 1, groups):
+                        rows[k][q] = rows[k][q] - (left[q] * first + right[q] * second)
             for k in range(3):
-                upper, lower = rows[k][i:i + 1], rows[k][i + 1:i + 2]
-                done[k][i] = upper * root1
-                done[k][i + 1] = (lower - ratio * upper) * root2
-                if i + 2 < PANEL:
-                    rows[k] = rows[k] - (
-                        first * (k11 * upper - k12 * lower) + second * (k22 * lower - k12 * upper)
-                    )
+                above = pltpu.roll(rows[k][g], 1, 0)
+                done[k][g] = (rows[k][g] - ratios * above) * scales
         factor = [jnp.concatenate(part, axis=0) for part in done]
-        inside = (lane >= offset) & (lane < offset + PANEL)
+        lanes = lax.broadcasted_iota(i32, (PANEL, 128), 1)
+        inside = (lanes >= offset) & (lanes < offset + PANEL)
         mixed = list(factor[:2])
         mixed[tile] = jnp.where(inside, factor[2], factor[tile])
         for k in range(2):
             if k < tile:
                 value = mixed[k]
             elif k == tile:
-                value = jnp.where(lane < offset + PANEL, mixed[k], 0.0)
+                value = jnp.where(lanes < offset + PANEL, mixed[k], 0.0)
             else:
                 value = jnp.zeros((PANEL, 128), f32)
             out[low:high, 128 * k:128 * (k + 1)] = value
         if high < size:
-            h, m, l = split3(jnp.concatenate(factor[:2], axis=1))
+            start = high // 128 * 128
+            h, m, l = split3(jnp.concatenate(factor[:2], axis=1)[:, start:])
             eh, em, el = split3(jnp.concatenate(mixed, axis=1))
             left = jnp.concatenate([h, h, m, m, h, l], axis=0)
             right = jnp.concatenate([eh, em, eh, em, el, eh], axis=0)
             update = lax.dot_general(
                 left, right, (((0,), (0,)), ((), ())), preferred_element_type=f32
             )
-            lanes = lax.broadcasted_iota(i32, (size - high, size), 1)
-            rest = jnp.where((lanes >= low) & (lanes < high), 0.0, state[high:, :])
-            state[high:, :] = rest - update[high:, :]
+            columns = lax.broadcasted_iota(i32, (size - high, size), 1)
+            rest = jnp.where((columns >= low) & (columns < high), 0.0, state[high:, :])
+            state[high:, :] = rest - update[high - start:, :]
 
 
 def inverse_factor(gram, came):
@@ -410,22 +443,25 @@
     order = sorted(range(1, outer), key=lambda d: -min(d, outer - d)) + [0]
     cut = (outer + 1) // 2
     groups = [group for group in (order[:cut], order[cut:]) if group]
-    wanted = [(d, 1) for d in order if inner == 2] + [(d, 0) for d in order]
-    source, flats, sends, tables, at = field, [], [], None, 0
+    turns = [(group, 1) for group in groups if inner == 2] + [(group, 0) for group in groups]
+    turns = [[(d, flip) for d in group] for group, flip in turns]
+    wanted = [pair for pairs in turns for pair in pairs]
+    flats, sends, carried, turn = [], [], None, 0
     if inner == 2:
-        for group in groups:
-            (rows,), flat, source, tables = sketch_chunks(
-                source, sketch_seeds, wanted, at, len(group), sizes, True, tables
+        for _ in range(len(groups)):
+            (rows,), flat, carried = sketch_chunks(
+                field, sketch_seeds, turns[turn], turns[turn + 1], sizes, True, carried
             )
             sends.append(neighbour(rows))
-            at += len(group)
+            turn += 1
             flats.append(flat)
     parts = []
     for k, group in enumerate(groups):
-        kept, flat, source, tables = sketch_chunks(
-            source, sketch_seeds, wanted, at, len(group), sizes, False, tables
+        follow = turns[turn + 1] if turn + 1 < len(turns) else []
+        kept, flat, carried = sketch_chunks(
+            field, sketch_seeds, turns[turn], follow, sizes, False, carried
         )
-        at += len(group)
+        turn += 1
         flats.append(flat)
         if inner == 2:
             kept = merge(kept, sends[k])

time: 78.3 us -> 71.1 us (0.908)
  Pallas kernels: 28.8 us -> 24 us
  waiting for transfers between devices: 23.9 us -> 22.2 us
    pallas_call x1, Pallas kernels: 13.6 us -> 6.43 us  [inverse_factor(): call(inverse_factor_kernel, held(gram.shape, f32), [VMEM_SPACE] * 2, flop...]
    ppermute x6, waiting for transfers between devices: 7.72 us -> 5.38 us  [neighbour(): return lax.ppermute(value, 'yz', [(i, i ^ 1) for i in range(count)])]
    pallas_call x4, Pallas kernels: 9.12 us -> 11.4 us  [sketch_chunks(): call(kernel, out_shape, in_specs, flops=2 * total * y_local * z_local * R...]
    ppermute x6, starting transfers between devices: 8.48 us -> 7.2 us  [neighbour(): return lax.ppermute(value, 'yz', [(i, i ^ 1) for i in range(count)])]
  transfers between devices with their start and end apart: 17 -> 17, of which waited for: 11 -> 9; matrix products, arithmetic and copies ran while one was open for 1% -> 1% of each run, Pallas kernels for 4% -> 11%
where the time goes in v2:
time: 71.1 us; the launch traced here: 70.9 us
  Pallas kernels  24 us (34%)
  starting transfers between devices  22.2 us (31%)
  waiting for transfers between devices  22.2 us (31%)
  local copies, waits for them, and re-layouts  1.62 us (2%)
  between operations  0.92 us (1%)
    ppermute x6, starting transfers between devices, shift(): return lax.ppermute(value, 'yz', pairs)  13.8 us
    ppermute x6, waiting for transfers between devices, shift(): return lax.ppermute(value, 'yz', pairs)  13.2 us
    pallas_call x4, Pallas kernels, sketch_chunks(): call(kernel, out_shape, in_specs, flops=2 * total * y_local * z_local * R...  11.4 us
    ppermute x6, starting transfers between devices, neighbour(): return lax.ppermute(value, 'yz', [(i, i ^ 1) for i in range(count)])  7.2 us
    pallas_call x1, Pallas kernels, inverse_factor(): call(inverse_factor_kernel, held(gram.shape, f32), [VMEM_SPACE] * 2, flop...  6.43 us
    ppermute x6, waiting for transfers between devices, neighbour(): return lax.ppermute(value, 'yz', [(i, i ^ 1) for i in range(count)])  5.38 us
    ppermute x5, waiting for transfers between devices, other_core(): return lax.ppermute(value, 'gx', [(0, 1), (1, 0)])  3.69 us
    pallas_call x4, Pallas kernels, product(): call(kernel, [held(shape, f32), held(shape, f32)], [VMEM_SPACE] * (1 + le...  2.81 us
  transfers between devices with their start and end apart: 17, of which 9 were waited for; matrix products, arithmetic and copies ran while one was open for 1% of the time, Pallas kernels for 11%

profile of v2, /device:TPU:0, one launch (start us, length us, event | category | flops | bytes accessed | tf_op | source)
XLA Modules:
  0.0 70.9 jit_solution(17488043390424411660)
XLA Ops:
  0.6 0.6 copy-done
  1.3 3.6 %shard_map.41 = (f32[256,256]{1,0:T(8,128)S(1)}, bf16[256,4096]{1,0:T(8,128)(2,1)S(1)}, bf16[256,32,128]{2,1,0:T(8,128)(2,1)S(1)}, bf16[128,256]{1,0:T(8,128)(2,1)S(1)}, f32[32,256]{1,0:T(8,128)S(1)}) custom-call(bf16[1024,32,128]{2,1,0:T(8,128)(2,1)} %refs_0_.7, s32[6]{0:T(128)S(1)} %copy-done), custom_call_target="tpu_custom_call" | custom-call | flops 536870912 | bytes 2097152 | tf_op jit(solution)/shard_map/pallas_call | solution.py:154
  4.9 3.1 %collective-permute-start = (f32[256,256]{1,0:T(8,128)S(1)}, f32[256,256]{1,0:T(8,128)S(1)}, u32[]{:S(2)}, u32[]{:S(2)}) collective-permute-start(f32[256,256]{1,0:T(8,128)S(1)} %get-tuple-element.37), channel_id=1, source_target_pairs={{0,2},{2,0},{4,6},{6,4},{8,10},{10,8},{12,14},{14,12},{1,3},{3,1},... | collective-permute-start | bytes 786440 | tf_op jit(solution)/shard_map/ppermute | solution.py:433
  8.0 3.1 %shard_map.42 = (f32[256,256]{1,0:T(8,128)S(1)}, bf16[256,4096]{1,0:T(8,128)(2,1)S(1)}, bf16[256,32,128]{2,1,0:T(8,128)(2,1)S(1)}) custom-call(bf16[1024,32,128]{2,1,0:T(8,128)(2,1)} %refs_0_.7, bf16[256,32,128]{2,1,0:T(8,128)(2,1)S(1)} %get-tuple-element.31.refs_1_, bf16[128,256]{1,0:T(8,128)(2,1)S(1)} %get-tuple-element.32.refs_2_, ...), custom_call_target="tpu_custom_call" | custom-call | flops 536870912 | bytes 2097152 | tf_op jit(solution)/shard_map/pallas_call | solution.py:154
  11.1 3.1 %shard_map.43 = (f32[128,256]{1,0:T(8,128)S(1)}, f32[128,256]{1,0:T(8,128)S(1)}, bf16[256,4096]{1,0:T(8,128)(2,1)S(1)}, bf16[256,32,128]{2,1,0:T(8,128)(2,1)S(1)}) custom-call(bf16[1024,32,128]{2,1,0:T(8,128)(2,1)} %refs_0_.7, bf16[256,32,128]{2,1,0:T(8,128)(2,1)S(1)} %get-tuple-element.34.refs_1_, bf16[128,256]{1,0:T(8,128)(2,1)S(1)} %get-tuple-element.32.refs_2_, ...), custom_call_target="tpu_custom_call" | custom-call | flops 536870912 | bytes 2097152 | tf_op jit(solution)/shard_map/pallas_call | solution.py:154
  14.2 1.7 %shard_map.45 = (f32[128,256]{1,0:T(8,128)S(1)}, f32[128,256]{1,0:T(8,128)S(1)}, bf16[256,4096]{1,0:T(8,128)(2,1)S(1)}) custom-call(bf16[1024,32,128]{2,1,0:T(8,128)(2,1)} %refs_0_.7, bf16[256,32,128]{2,1,0:T(8,128)(2,1)S(1)} %get-tuple-element.40.refs_1_, bf16[128,256]{1,0:T(8,128)(2,1)S(1)} %get-tuple-element.32.refs_2_, ...), custom_call_target="tpu_custom_call" | custom-call | flops 536870912 | bytes 2097152 | tf_op jit(solution)/shard_map/pallas_call | solution.py:154
  16.0 3.1 %collective-permute-start.1 = (f32[128,256]{1,0:T(8,128)S(1)}, f32[128,256]{1,0:T(8,128)S(1)}, u32[]{:S(2)}, u32[]{:S(2)}) collective-permute-start(f32[128,256]{1,0:T(8,128)S(1)} %get-tuple-element.38), channel_id=1, source_target_pairs={{0,8},{2,10},{4,12},{6,14},{8,0},{10,2},{12,4},{14,6},{1,9},{3,11}... | collective-permute-start | bytes 393224 | tf_op jit(solution)/shard_map/ppermute | solution.py:437
  19.1 1.6 %collective-permute-start.2 = (f32[128,256]{1,0:T(8,128)S(1)}, f32[128,256]{1,0:T(8,128)S(1)}, u32[]{:S(2)}, u32[]{:S(2)}) collective-permute-start(f32[128,256]{1,0:T(8,128)S(1)} %get-tuple-element.39), channel_id=1, source_target_pairs={{0,4},{2,6},{4,8},{6,10},{8,12},{10,14},{12,0},{14,2},{1,5},{3,7},... | collective-permute-start | bytes 393224 | tf_op jit(solution)/shard_map/ppermute | solution.py:437
  20.7 3.1 %collective-permute-start.4 = (f32[128,256]{1,0:T(8,128)S(1)}, f32[128,256]{1,0:T(8,128)S(1)}, u32[]{:S(2)}, u32[]{:S(2)}) collective-permute-start(f32[128,256]{1,0:T(8,128)S(1)} %get-tuple-element.44), channel_id=1, source_target_pairs={{0,12},{2,14},{4,0},{6,2},{8,4},{10,6},{12,8},{14,10},{1,13},{3,15... | collective-permute-start | bytes 393224 | tf_op jit(solution)/shard_map/ppermute | solution.py:437
  23.8 5.1 %collective-permute-done.1.refs_0_ = f32[128,256]{1,0:T(8,128)S(1)} collective-permute-done((f32[128,256]{1,0:T(8,128)S(1)}, f32[128,256]{1,0:T(8,128)S(1)}, u32[]{:S(2)}, u32[]{:S(2)}) %collective-permute-start.1) | collective-permute-done | bytes 131104 | tf_op jit(solution)/shard_map/ppermute | solution.py:437
  29.2 2.4 %collective-permute-start.10 = (f32[128,256]{1,0:T(8,128)S(1)}, f32[128,256]{1,0:T(8,128)S(1)}, u32[]{:S(2)}, u32[]{:S(2)}) collective-permute-start(f32[128,256]{1,0:T(8,128)S(1)} %shard_map.47.refs_0_), channel_id=1, source_target_pairs={{0,12},{2,14},{4,0},{6,2},{8,4},{10,6},{12,8},{14,10},{1,13},{3,15... | collective-permute-start | bytes 393224 | tf_op jit(solution)/shard_map/ppermute | solution.py:437
  31.6 1.6 %collective-permute-start.8 = (f32[128,256]{1,0:T(8,128)S(1)}, f32[128,256]{1,0:T(8,128)S(1)}, u32[]{:S(2)}, u32[]{:S(2)}) collective-permute-start(f32[128,256]{1,0:T(8,128)S(1)} %shard_map.47.refs_0_), channel_id=1, source_target_pairs={{0,8},{2,10},{4,12},{6,14},{8,0},{10,2},{12,4},{14,6},{1,9},{3,11}... | collective-permute-start | bytes 393224 | tf_op jit(solution)/shard_map/ppermute | solution.py:437
  33.3 1.9 %collective-permute-start.6 = (f32[128,256]{1,0:T(8,128)S(1)}, f32[128,256]{1,0:T(8,128)S(1)}, u32[]{:S(2)}, u32[]{:S(2)}) collective-permute-start(f32[128,256]{1,0:T(8,128)S(1)} %shard_map.47.refs_0_), channel_id=1, source_target_pairs={{0,4},{2,6},{4,8},{6,10},{8,12},{10,14},{12,0},{14,2},{1,5},{3,7},... | collective-permute-start | bytes 393224 | tf_op jit(solution)/shard_map/ppermute | solution.py:437
  35.2 1.5 %collective-permute-start.5 = (f32[128,256]{1,0:T(8,128)S(1)}, f32[128,256]{1,0:T(8,128)S(1)}, u32[]{:S(2)}, u32[]{:S(2)}) collective-permute-start(f32[128,256]{1,0:T(8,128)S(1)} %shard_map.47.refs_0_), channel_id=1, source_target_pairs={{0,2},{2,0},{4,6},{6,4},{8,10},{10,8},{12,14},{14,12},{1,3},{3,1},... | collective-permute-start | bytes 393224 | tf_op jit(solution)/shard_map/ppermute | solution.py:433
  37.2 7.8 %collective-permute-done.8.refs_4_ = f32[128,256]{1,0:T(8,128)S(1)} collective-permute-done((f32[128,256]{1,0:T(8,128)S(1)}, f32[128,256]{1,0:T(8,128)S(1)}, u32[]{:S(2)}, u32[]{:S(2)}) %collective-permute-start.8) | collective-permute-done | bytes 131104 | tf_op jit(solution)/shard_map/ppermute | solution.py:437
  45.0 1.5 %collective-permute-start.9 = (f32[128,256]{1,0:T(8,128)S(1)}, f32[128,256]{1,0:T(8,128)S(1)}, u32[]{:S(2)}, u32[]{:S(2)}) collective-permute-start(f32[128,256]{1,0:T(8,128)S(1)} %collective-permute-done.8.refs_4_), channel_id=1, source_target_pairs={{0,2},{2,0},{4,6},{6,4},{8,10},{10,8},{12,14},{14,12},{1,3},{3,1},... | collective-permute-start | bytes 393224 | tf_op jit(solution)/shard_map/ppermute | solution.py:433
  46.6 0.5 collective-permute-start.7
  47.1 4.0 %collective-permute-done.9.refs_5_ = f32[128,256]{1,0:T(8,128)S(1)} collective-permute-done((f32[128,256]{1,0:T(8,128)S(1)}, f32[128,256]{1,0:T(8,128)S(1)}, u32[]{:S(2)}, u32[]{:S(2)}) %collective-permute-start.9) | collective-permute-done | bytes 131104 | tf_op jit(solution)/shard_map/ppermute | solution.py:433
  51.0 1.4 %collective-permute-done.7.refs_3_ = f32[128,256]{1,0:T(8,128)S(1)} collective-permute-done((f32[128,256]{1,0:T(8,128)S(1)}, f32[128,256]{1,0:T(8,128)S(1)}, u32[]{:S(2)}, u32[]{:S(2)}) %collective-permute-start.7) | collective-permute-done | bytes 131104 | tf_op jit(solution)/shard_map/ppermute | solution.py:433
  52.5 0.8 %shard_map.48.gram = f32[256,256]{1,0:T(8,128)S(1)} custom-call(f32[128,256]{1,0:T(8,128)S(1)} %shard_map.47.refs_0_, f32[128,256]{1,0:T(8,128)S(1)} %collective-permute-done.5.refs_1_, f32[128,256]{1,0:T(8,128)S(1)} %collective-permute-done.6.refs_2_, f32[128,256]{1,0:T(8,128)S(1)} %collective-permute-done.7.refs_3_, ...), custom_call_target="tpu_custom_call" | custom-call | flops 536870912 | bytes 1048576 | tf_op jit(solution)/shard_map/pallas_call | solution.py:311
  53.3 1.5 %collective-permute-done.12.came = f32[256,256]{1,0:T(8,128)S(1)} collective-permute-done((f32[256,256]{1,0:T(8,128)S(1)}, f32[256,256]{1,0:T(8,128)S(1)}, u32[]{:S(2)}, u32[]{:S(2)}) %collective-permute-start.12) | collective-permute-done | bytes 262176 | tf_op jit(solution)/shard_map/ppermute | solution.py:440
  54.9 6.4 %shard_map.49.inverse_ref = f32[256,256]{1,0:T(8,128)S(1)} custom-call(f32[256,256]{1,0:T(8,128)S(1)} %shard_map.48.gram, f32[256,256]{1,0:T(8,128)S(1)} %collective-permute-done.12.came), custom_call_target="tpu_custom_call" | custom-call | flops 50331648 | bytes 524288 | tf_op jit(solution)/shard_map/pallas_call | solution.py:259
  61.3 1.3 %shard_map.50 = (f32[1024,256]{1,0:T(8,128)S(1)}, bf16[256,1024]{1,0:T(8,128)(2,1)S(1)}) custom-call(f32[256,256]{1,0:T(8,128)S(1)} %shard_map.49.inverse_ref, f32[128,256]{1,0:T(8,128)S(1)} %shard_map.47.refs_0_, f32[128,256]{1,0:T(8,128)S(1)} %collective-permute-done.5.refs_1_, f32[128,256]{1,0:T(8,128)S(1)} %collective-permute-done.6.refs_2_, ...), custom_call_target="tpu_custom_call" | custom-call | flops 402653184 | bytes 2097152 | tf_op jit(solution)/shard_map/pallas_call | solution.py:349
  62.6 0.7 shard_map.54
  63.3 0.7 shard_map.53
  64.0 0.7 shard_map.52
  64.8 0.7 shard_map.51
  66.6 1.0 %copy.4 = f32[1024,256]{1,0:T(8,128)} copy(f32[1024,256]{1,0:T(8,128)S(1)} %get-tuple-element.60) | data formatting | bytes 2097152
  67.5 0.7 collective-permute-done.15.refs_6_
  68.2 0.7 %collective-permute-done.14.refs_5_ = f32[128,1024]{1,0:T(8,128)S(1)} collective-permute-done((f32[128,1024]{1,0:T(8,128)S(1)}, f32[128,1024]{1,0:T(8,128)S(1)}, u32[]{:S(2)}, u32[]{:S(2)}) %collective-permute-start.14) | collective-permute-done | bytes 524320 | tf_op jit(solution)/shard_map/ppermute | solution.py:440
  68.9 0.7 %collective-permute-done.13.refs_4_ = f32[128,1024]{1,0:T(8,128)S(1)} collective-permute-done((f32[128,1024]{1,0:T(8,128)S(1)}, f32[128,1024]{1,0:T(8,128)S(1)}, u32[]{:S(2)}, u32[]{:S(2)}) %collective-permute-start.13) | collective-permute-done | bytes 524320 | tf_op jit(solution)/shard_map/ppermute | solution.py:440
  69.7 1.1 %shard_map.55 = bf16[128,32,128]{2,1,0:T(8,128)(2,1)} custom-call(f32[128,1024]{1,0:T(8,128)S(1)} %get-tuple-element.52.refs_0_, f32[128,1024]{1,0:T(8,128)S(1)} %get-tuple-element.53.refs_1_, f32[128,1024]{1,0:T(8,128)S(1)} %get-tuple-element.54.refs_2_, f32[128,1024]{1,0:T(8,128)S(1)} %get-tuple-element.55.refs_3_, ...), custom_call_target="tpu_custom_call" | custom-call | bytes 5242880 | tf_op jit(solution)/shard_map/pallas_call | solution.py:414
  (20 shorter events, 2.1 us)
Async XLA Ops:
  0.6 0.7 copy-start
  4.9 11.0 %collective-permute-start = (f32[256,256]{1,0:T(8,128)S(1)}, f32[256,256]{1,0:T(8,128)S(1)}, u32[]{:S(2)}, u32[]{:S(2)}) collective-permute-start(f32[256,256]{1,0:T(8,128)S(1)} %get-tuple-element.37), channel_id=1, source_target_pairs={{0,2},{2,0},{4,6},{6,4},{8,10},{10,8},{12,14},{14,12},{1,3},{3,1},... | collective-permute-start | bytes 786440 | tf_op jit(solution)/shard_map/ppermute | solution.py:433
  11.0 9.6 %collective-permute-start.3 = (f32[256,256]{1,0:T(8,128)S(1)}, f32[256,256]{1,0:T(8,128)S(1)}, u32[]{:S(2)}, u32[]{:S(2)}) collective-permute-start(f32[256,256]{1,0:T(8,128)S(1)} %get-tuple-element.43), channel_id=1, source_target_pairs={{0,2},{2,0},{4,6},{6,4},{8,10},{10,8},{12,14},{14,12},{1,3},{3,1},... | collective-permute-start | bytes 786440 | tf_op jit(solution)/shard_map/ppermute | solution.py:433
  16.0 12.9 %collective-permute-start.1 = (f32[128,256]{1,0:T(8,128)S(1)}, f32[128,256]{1,0:T(8,128)S(1)}, u32[]{:S(2)}, u32[]{:S(2)}) collective-permute-start(f32[128,256]{1,0:T(8,128)S(1)} %get-tuple-element.38), channel_id=1, source_target_pairs={{0,8},{2,10},{4,12},{6,14},{8,0},{10,2},{12,4},{14,6},{1,9},{3,11}... | collective-permute-start | bytes 393224 | tf_op jit(solution)/shard_map/ppermute | solution.py:437
  19.1 9.8 %collective-permute-start.2 = (f32[128,256]{1,0:T(8,128)S(1)}, f32[128,256]{1,0:T(8,128)S(1)}, u32[]{:S(2)}, u32[]{:S(2)}) collective-permute-start(f32[128,256]{1,0:T(8,128)S(1)} %get-tuple-element.39), channel_id=1, source_target_pairs={{0,4},{2,6},{4,8},{6,10},{8,12},{10,14},{12,0},{14,2},{1,5},{3,7},... | collective-permute-start | bytes 393224 | tf_op jit(solution)/shard_map/ppermute | solution.py:437
  20.7 8.4 %collective-permute-start.4 = (f32[128,256]{1,0:T(8,128)S(1)}, f32[128,256]{1,0:T(8,128)S(1)}, u32[]{:S(2)}, u32[]{:S(2)}) collective-permute-start(f32[128,256]{1,0:T(8,128)S(1)} %get-tuple-element.44), channel_id=1, source_target_pairs={{0,12},{2,14},{4,0},{6,2},{8,4},{10,6},{12,8},{14,10},{1,13},{3,15... | collective-permute-start | bytes 393224 | tf_op jit(solution)/shard_map/ppermute | solution.py:437
  29.2 7.6 %collective-permute-start.10 = (f32[128,256]{1,0:T(8,128)S(1)}, f32[128,256]{1,0:T(8,128)S(1)}, u32[]{:S(2)}, u32[]{:S(2)}) collective-permute-start(f32[128,256]{1,0:T(8,128)S(1)} %shard_map.47.refs_0_), channel_id=1, source_target_pairs={{0,12},{2,14},{4,0},{6,2},{8,4},{10,6},{12,8},{14,10},{1,13},{3,15... | collective-permute-start | bytes 393224 | tf_op jit(solution)/shard_map/ppermute | solution.py:437
  31.6 13.4 %collective-permute-start.8 = (f32[128,256]{1,0:T(8,128)S(1)}, f32[128,256]{1,0:T(8,128)S(1)}, u32[]{:S(2)}, u32[]{:S(2)}) collective-permute-start(f32[128,256]{1,0:T(8,128)S(1)} %shard_map.47.refs_0_), channel_id=1, source_target_pairs={{0,8},{2,10},{4,12},{6,14},{8,0},{10,2},{12,4},{14,6},{1,9},{3,11}... | collective-permute-start | bytes 393224 | tf_op jit(solution)/shard_map/ppermute | solution.py:437
  33.3 13.3 %collective-permute-start.6 = (f32[128,256]{1,0:T(8,128)S(1)}, f32[128,256]{1,0:T(8,128)S(1)}, u32[]{:S(2)}, u32[]{:S(2)}) collective-permute-start(f32[128,256]{1,0:T(8,128)S(1)} %shard_map.47.refs_0_), channel_id=1, source_target_pairs={{0,4},{2,6},{4,8},{6,10},{8,12},{10,14},{12,0},{14,2},{1,5},{3,7},... | collective-permute-start | bytes 393224 | tf_op jit(solution)/shard_map/ppermute | solution.py:437
  35.2 11.9 %collective-permute-start.5 = (f32[128,256]{1,0:T(8,128)S(1)}, f32[128,256]{1,0:T(8,128)S(1)}, u32[]{:S(2)}, u32[]{:S(2)}) collective-permute-start(f32[128,256]{1,0:T(8,128)S(1)} %shard_map.47.refs_0_), channel_id=1, source_target_pairs={{0,2},{2,0},{4,6},{6,4},{8,10},{10,8},{12,14},{14,12},{1,3},{3,1},... | collective-permute-start | bytes 393224 | tf_op jit(solution)/shard_map/ppermute | solution.py:433
  36.7 10.3 %collective-permute-start.11 = (f32[128,256]{1,0:T(8,128)S(1)}, f32[128,256]{1,0:T(8,128)S(1)}, u32[]{:S(2)}, u32[]{:S(2)}) collective-permute-start(f32[128,256]{1,0:T(8,128)S(1)} %collective-permute-done.10.refs_6_), channel_id=1, source_target_pairs={{0,2},{2,0},{4,6},{6,4},{8,10},{10,8},{12,14},{14,12},{1,3},{3,1},... | collective-permute-start | bytes 393224 | tf_op jit(solution)/shard_map/ppermute | solution.py:433
  45.0 6.0 %collective-permute-start.9 = (f32[128,256]{1,0:T(8,128)S(1)}, f32[128,256]{1,0:T(8,128)S(1)}, u32[]{:S(2)}, u32[]{:S(2)}) collective-permute-start(f32[128,256]{1,0:T(8,128)S(1)} %collective-permute-done.8.refs_4_), channel_id=1, source_target_pairs={{0,2},{2,0},{4,6},{6,4},{8,10},{10,8},{12,14},{14,12},{1,3},{3,1},... | collective-permute-start | bytes 393224 | tf_op jit(solution)/shard_map/ppermute | solution.py:433
  46.6 5.9 %collective-permute-start.7 = (f32[128,256]{1,0:T(8,128)S(1)}, f32[128,256]{1,0:T(8,128)S(1)}, u32[]{:S(2)}, u32[]{:S(2)}) collective-permute-start(f32[128,256]{1,0:T(8,128)S(1)} %collective-permute-done.6.refs_2_), channel_id=1, source_target_pairs={{0,2},{2,0},{4,6},{6,4},{8,10},{10,8},{12,14},{14,12},{1,3},{3,1},... | collective-permute-start | bytes 393224 | tf_op jit(solution)/shard_map/ppermute | solution.py:433
  53.3 1.6 %collective-permute-start.12 = (f32[256,256]{1,0:T(8,128)S(1)}, f32[256,256]{1,0:T(8,128)S(1)}, u32[]{:S(2)}, u32[]{:S(2)}) collective-permute-start(f32[256,256]{1,0:T(8,128)S(1)} %shard_map.48.gram), channel_id=1, source_target_pairs={{0,1},{1,0},{2,3},{3,2},{4,5},{5,4},{6,7},{7,6},{8,9},{9,8},{10,11... | collective-permute-start | bytes 786440 | tf_op jit(solution)/shard_map/ppermute | solution.py:440
  65.5 2.1 %collective-permute-start.16 = (f32[128,1024]{1,0:T(8,128)S(1)}, f32[128,1024]{1,0:T(8,128)S(1)}, u32[]{:S(2)}, u32[]{:S(2)}) collective-permute-start(f32[128,1024]{1,0:T(8,128)S(1)} %get-tuple-element.59), channel_id=1, source_target_pairs={{0,1},{1,0},{2,3},{3,2},{4,5},{5,4},{6,7},{7,6},{8,9},{9,8},{10,11... | collective-permute-start | bytes 1572872 | tf_op jit(solution)/shard_map/ppermute | solution.py:440
  65.7 2.5 %collective-permute-start.15 = (f32[128,1024]{1,0:T(8,128)S(1)}, f32[128,1024]{1,0:T(8,128)S(1)}, u32[]{:S(2)}, u32[]{:S(2)}) collective-permute-start(f32[128,1024]{1,0:T(8,128)S(1)} %get-tuple-element.58), channel_id=1, source_target_pairs={{0,1},{1,0},{2,3},{3,2},{4,5},{5,4},{6,7},{7,6},{8,9},{9,8},{10,11... | collective-permute-start | bytes 1572872 | tf_op jit(solution)/shard_map/ppermute | solution.py:440
  66.0 2.9 %collective-permute-start.14 = (f32[128,1024]{1,0:T(8,128)S(1)}, f32[128,1024]{1,0:T(8,128)S(1)}, u32[]{:S(2)}, u32[]{:S(2)}) collective-permute-start(f32[128,1024]{1,0:T(8,128)S(1)} %get-tuple-element.57), channel_id=1, source_target_pairs={{0,1},{1,0},{2,3},{3,2},{4,5},{5,4},{6,7},{7,6},{8,9},{9,8},{10,11... | collective-permute-start | bytes 1572872 | tf_op jit(solution)/shard_map/ppermute | solution.py:440
  66.2 3.5 %collective-permute-start.13 = (f32[128,1024]{1,0:T(8,128)S(1)}, f32[128,1024]{1,0:T(8,128)S(1)}, u32[]{:S(2)}, u32[]{:S(2)}) collective-permute-start(f32[128,1024]{1,0:T(8,128)S(1)} %get-tuple-element.56), channel_id=1, source_target_pairs={{0,1},{1,0},{2,3},{3,2},{4,5},{5,4},{6,7},{7,6},{8,9},{9,8},{10,11... | collective-permute-start | bytes 1572872 | tf_op jit(solution)/shard_map/ppermute | solution.py:440

commit v3 on v2

--- a/solution.py
+++ b/solution.py
@@ -30,7 +30,6 @@
 
 LIMIT = 14 << 20
 VMEM_SPACE = pl.BlockSpec(memory_space=pltpu.VMEM)
-SMEM_SPACE = pl.BlockSpec(memory_space=pltpu.SMEM)
 ANY_SPACE = pl.BlockSpec(memory_space=pl.ANY)
 HBM_SPACE = pl.BlockSpec(memory_space=pltpu.HBM)
 SUB = 64
@@ -60,6 +59,7 @@
     sub = min(SUB, chunk)
     stride = y_local + 1
     parts = chunk // sub
+    piece = min(32, sub)
     span = len(wanted)
     total = span * chunk
     opening = carried is None
@@ -68,7 +68,7 @@
         refs = list(refs)
         field_ref, sems = refs.pop(0), refs.pop()
         if opening:
-            seeds_ref, rows = refs.pop(0), refs.pop()
+            seeds_hbm, seeds_ref, rows = refs.pop(0), refs.pop(), refs.pop()
         else:
             rows, omega_z, omega_y = refs.pop(0), refs.pop(0), refs.pop(0)
         outs = [refs.pop(0) for _ in range(1 if joined else span)]
@@ -83,14 +83,18 @@
         copies = []
         for (d, flip), target, k in moves:
             chosen = lax.rem(o + d, outer) * inner + (inner - 1 - y if flip else y)
-            copy = pltpu.make_async_copy(
-                field_ref.at[pl.ds(chosen * chunk, chunk)],
-                target.at[pl.ds(k * chunk, chunk)],
-                sems.at[len(copies)],
-            )
-            copy.start()
-            copies.append(copy)
+            for start in range(0, chunk, piece):
+                copy = pltpu.make_async_copy(
+                    field_ref.at[pl.ds(chosen * chunk + start, piece)],
+                    target.at[pl.ds(k * chunk + start, piece)],
+                    sems.at[len(copies)],
+                )
+                copy.start()
+                copies.append(copy)
         if opening:
+            seeds_copy = pltpu.make_async_copy(seeds_hbm, seeds_ref, sems.at[len(copies)])
+            seeds_copy.start()
+            seeds_copy.wait()
             omega_z[...] = omega_table(
                 seeds_ref[3], seeds_ref[4], seeds_ref[5], 0, z_local
             ).astype(bf16)
@@ -101,8 +105,9 @@
         table_z = omega_z[...]
 
         def spread(block):
-            if opening and block % parts == 0:
-                copies[block // parts].wait()
+            if opening:
+                for k in range(block * sub // piece, (block + 1) * sub // piece):
+                    copies[k].wait()
             for x in range(sub):
                 scratch[block % 2][x * stride:x * stride + y_local, :] = (
                     rows[block * sub + x].astype(f32)
@@ -131,7 +136,7 @@
             else:
                 start = block % parts * sub
                 outs[block // parts][start:start + sub, :] = sums
-        for copy in copies[span if opening else 0:]:
+        for copy in copies[total // piece if opening else 0:]:
             copy.wait()
 
     count = 1 if joined else span
@@ -142,15 +147,16 @@
     if follow:
         out_shape.append(held((len(follow) * chunk, y_local, z_local), bf16))
     if opening:
-        operands.append(seeds)
-        in_specs = [HBM_SPACE, SMEM_SPACE]
+        operands.append(pltpu.with_memory_space_constraint(seeds, pltpu.HBM))
+        in_specs = [HBM_SPACE, HBM_SPACE]
         out_shape += [held((z_local, RANK), bf16), held((y_local, RANK), f32)]
         scratch_shapes.append(pltpu.VMEM((total, y_local, z_local), bf16))
+        scratch_shapes.append(pltpu.SMEM(seeds.shape, i32))
     else:
         operands += carried
         in_specs = [HBM_SPACE] + [VMEM_SPACE] * 3
-    copies = len(follow) + (span if opening else 0)
-    scratch_shapes.append(pltpu.SemaphoreType.DMA((max(copies, 1),)))
+    copies = (len(follow) + (span if opening else 0)) * (chunk // piece)
+    scratch_shapes.append(pltpu.SemaphoreType.DMA((copies + 1,)))
     result = call(
         kernel, out_shape, in_specs,
         flops=2 * total * y_local * z_local * RANK, moved=2 * total * y_local * z_local,
@@ -441,31 +447,22 @@
 
     sizes = (outer, inner, chunk)
     order = sorted(range(1, outer), key=lambda d: -min(d, outer - d)) + [0]
-    cut = (outer + 1) // 2
-    groups = [group for group in (order[:cut], order[cut:]) if group]
-    turns = [(group, 1) for group in groups if inner == 2] + [(group, 0) for group in groups]
-    turns = [[(d, flip) for d in group] for group, flip in turns]
-    wanted = [pair for pairs in turns for pair in pairs]
-    flats, sends, carried, turn = [], [], None, 0
-    if inner == 2:
-        for _ in range(len(groups)):
-            (rows,), flat, carried = sketch_chunks(
-                field, sketch_seeds, turns[turn], turns[turn + 1], sizes, True, carried
-            )
-            sends.append(neighbour(rows))
-            turn += 1
-            flats.append(flat)
-    parts = []
-    for k, group in enumerate(groups):
-        follow = turns[turn + 1] if turn + 1 < len(turns) else []
-        kept, flat, carried = sketch_chunks(
-            field, sketch_seeds, turns[turn], follow, sizes, False, carried
+    groups = [group for group in (order[:1], order[1:-1], order[-1:] if outer > 1 else []) if group]
+    turns = turns_of(len(groups), inner)
+    pairs = [[(d, flip) for d in groups[k]] for k, flip in turns]
+    wanted = [pair for some in pairs for pair in some]
+    flats, sends, parts, carried = [], {}, [], None
+    for turn, (k, flip) in enumerate(turns):
+        follow = pairs[turn + 1] if turn + 1 < len(turns) else []
+        made, flat, carried = sketch_chunks(
+            field, sketch_seeds, pairs[turn], follow, sizes, flip == 1, carried
         )
-        turn += 1
         flats.append(flat)
-        if inner == 2:
-            kept = merge(kept, sends[k])
-        for j, d in enumerate(group):
+        if flip:
+            sends[k] = neighbour(made[0])
+            continue
+        kept = merge(made, sends[k]) if inner == 2 else made
+        for j, d in enumerate(groups[k]):
             parts.append(shift(kept[j], d) if d else kept[j])
     own = total_of(parts)
     chunks = [None] * count
@@ -495,6 +492,14 @@
 PIECES = 4
 
 
+def turns_of(groups, inner):
+    if inner == 1:
+        return [(k, 0) for k in range(groups)]
+    if groups < 3:
+        return [(k, 1) for k in range(groups)] + [(k, 0) for k in range(groups)]
+    return [(0, 1), (1, 1), (0, 0), (2, 1), (1, 0), (2, 0)]
+
+
 def solution(mesh):
     in_specs = (P(("grp", "gx"), "yz", None), P("grp"))
     out_specs = (P(("grp", "gx"), None), P(("grp", "gx"), "yz", None))

time: 71.1 us -> 70.7 us (level)
  waiting for transfers between devices: 22.2 us -> 17.7 us
  starting transfers between devices: 22.2 us -> 24.6 us
  Pallas kernels: 24 us -> 26.3 us
    ppermute x6, waiting for transfers between devices: 13.2 us -> 8.65 us  [shift(): return lax.ppermute(value, 'yz', pairs)]
    ppermute x6 -> x7, starting transfers between devices: 7.2 us -> 9.2 us  [neighbour(): return lax.ppermute(value, 'yz', [(i, i ^ 1) for i in range(count)])]
    pallas_call x4 -> x6, Pallas kernels: 11.4 us -> 12.7 us  [sketch_chunks(): call(kernel, out_shape, in_specs, flops=2 * total * y_local * z_local * R...]
    pallas_call x4, Pallas kernels: 2.81 us -> 3.87 us  [product(): call(kernel, [held(shape, f32), held(shape, f32)], [VMEM_SPACE] * (1 + le...]
    unnamed x3 -> x1, local copies, waits for them, and re-layouts: 1.62 us -> 0.97 us
    ppermute x6 -> x7, waiting for transfers between devices: 5.38 us -> 5.37 us  [neighbour(): return lax.ppermute(value, 'yz', [(i, i ^ 1) for i in range(count)])]
  transfers between devices with their start and end apart: 17 -> 18, of which waited for: 9 -> 11; matrix products, arithmetic and copies ran while one was open for 1% -> 1% of each run, Pallas kernels for 11% -> 11%
where the time goes in v3:
time: 70.7 us; the launch traced here: 70.5 us
  Pallas kernels  26.3 us (37%)
  starting transfers between devices  24.6 us (35%)
  waiting for transfers between devices  17.7 us (25%)
  local copies, waits for them, and re-layouts  0.97 us (1%)
  between operations  0.94 us (1%)
    ppermute x6, starting transfers between devices, shift(): return lax.ppermute(value, 'yz', pairs)  14.2 us
    pallas_call x6, Pallas kernels, sketch_chunks(): call(kernel, out_shape, in_specs, flops=2 * total * y_local * z_local * R...  12.7 us
    ppermute x7, starting transfers between devices, neighbour(): return lax.ppermute(value, 'yz', [(i, i ^ 1) for i in range(count)])  9.2 us
    ppermute x6, waiting for transfers between devices, shift(): return lax.ppermute(value, 'yz', pairs)  8.65 us
    pallas_call x1, Pallas kernels, inverse_factor(): call(inverse_factor_kernel, held(gram.shape, f32), [VMEM_SPACE] * 2, flop...  6.43 us
    ppermute x7, waiting for transfers between devices, neighbour(): return lax.ppermute(value, 'yz', [(i, i ^ 1) for i in range(count)])  5.37 us
    pallas_call x4, Pallas kernels, product(): call(kernel, [held(shape, f32), held(shape, f32)], [VMEM_SPACE] * (1 + le...  3.87 us
    ppermute x5, waiting for transfers between devices, other_core(): return lax.ppermute(value, 'gx', [(0, 1), (1, 0)])  3.69 us
  transfers between devices with their start and end apart: 18, of which 11 were waited for; matrix products, arithmetic and copies ran while one was open for 1% of the time, Pallas kernels for 11%

profile of v3, /device:TPU:0, one launch (start us, length us, event | category | flops | bytes accessed | tf_op | source)
XLA Modules:
  0.0 70.5 jit_solution(16970216497929157490)
XLA Ops:
  0.6 2.2 %shard_map.41 = (f32[128,256]{1,0:T(8,128)S(1)}, bf16[128,4096]{1,0:T(8,128)(2,1)S(1)}, bf16[256,32,128]{2,1,0:T(8,128)(2,1)S(1)}, bf16[128,256]{1,0:T(8,128)(2,1)S(1)}, f32[32,256]{1,0:T(8,128)S(1)}) custom-call(bf16[1024,32,128]{2,1,0:T(8,128)(2,1)} %refs_0_.11, s32[6]{0:T(128)} %refs_1_.1), custom_call_target="tpu_custom_call" | custom-call | flops 268435456 | bytes 1048576 | tf_op jit(solution)/shard_map/pallas_call | solution.py:160
  2.8 2.7 %shard_map.42 = (f32[256,256]{1,0:T(8,128)S(1)}, bf16[256,4096]{1,0:T(8,128)(2,1)S(1)}, bf16[128,32,128]{2,1,0:T(8,128)(2,1)S(1)}) custom-call(bf16[1024,32,128]{2,1,0:T(8,128)(2,1)} %refs_0_.11, bf16[256,32,128]{2,1,0:T(8,128)(2,1)S(1)} %get-tuple-element.34.refs_1_, bf16[128,256]{1,0:T(8,128)(2,1)S(1)} %get-tuple-element.35.refs_2_, ...), custom_call_target="tpu_custom_call" | custom-call | flops 536870912 | bytes 2097152 | tf_op jit(solution)/shard_map/pallas_call | solution.py:160
  5.5 3.1 %collective-permute-start.2 = (f32[256,256]{1,0:T(8,128)S(1)}, f32[256,256]{1,0:T(8,128)S(1)}, u32[]{:S(2)}, u32[]{:S(2)}) collective-permute-start(f32[256,256]{1,0:T(8,128)S(1)} %get-tuple-element.44), channel_id=1, source_target_pairs={{0,2},{2,0},{4,6},{6,4},{8,10},{10,8},{12,14},{14,12},{1,3},{3,1},... | collective-permute-start | bytes 786440 | tf_op jit(solution)/shard_map/ppermute | solution.py:439
  8.7 1.9 %shard_map.43 = (f32[128,256]{1,0:T(8,128)S(1)}, bf16[128,4096]{1,0:T(8,128)(2,1)S(1)}, bf16[128,32,128]{2,1,0:T(8,128)(2,1)S(1)}) custom-call(bf16[1024,32,128]{2,1,0:T(8,128)(2,1)} %refs_0_.11, bf16[128,32,128]{2,1,0:T(8,128)(2,1)S(1)} %get-tuple-element.37.refs_1_, bf16[128,256]{1,0:T(8,128)(2,1)S(1)} %get-tuple-element.35.refs_2_, ...), custom_call_target="tpu_custom_call" | custom-call | flops 268435456 | bytes 1048576 | tf_op jit(solution)/shard_map/pallas_call | solution.py:160
  10.6 2.3 %shard_map.45 = (f32[128,256]{1,0:T(8,128)S(1)}, bf16[128,4096]{1,0:T(8,128)(2,1)S(1)}, bf16[256,32,128]{2,1,0:T(8,128)(2,1)S(1)}) custom-call(bf16[1024,32,128]{2,1,0:T(8,128)(2,1)} %refs_0_.11, bf16[128,32,128]{2,1,0:T(8,128)(2,1)S(1)} %get-tuple-element.40.refs_1_, bf16[128,256]{1,0:T(8,128)(2,1)S(1)} %get-tuple-element.35.refs_2_, ...), custom_call_target="tpu_custom_call" | custom-call | flops 268435456 | bytes 1048576 | tf_op jit(solution)/shard_map/pallas_call | solution.py:160
  12.9 2.0 %collective-permute-start.5 = (f32[128,256]{1,0:T(8,128)S(1)}, f32[128,256]{1,0:T(8,128)S(1)}, u32[]{:S(2)}, u32[]{:S(2)}) collective-permute-start(f32[128,256]{1,0:T(8,128)S(1)} %get-tuple-element.49), channel_id=1, source_target_pairs={{0,2},{2,0},{4,6},{6,4},{8,10},{10,8},{12,14},{14,12},{1,3},{3,1},... | collective-permute-start | bytes 393224 | tf_op jit(solution)/shard_map/ppermute | solution.py:439
  14.9 2.7 %shard_map.46 = (f32[128,256]{1,0:T(8,128)S(1)}, f32[128,256]{1,0:T(8,128)S(1)}, bf16[256,4096]{1,0:T(8,128)(2,1)S(1)}, bf16[128,32,128]{2,1,0:T(8,128)(2,1)S(1)}) custom-call(bf16[1024,32,128]{2,1,0:T(8,128)(2,1)} %refs_0_.11, bf16[256,32,128]{2,1,0:T(8,128)(2,1)S(1)} %get-tuple-element.41.refs_1_, bf16[128,256]{1,0:T(8,128)(2,1)S(1)} %get-tuple-element.35.refs_2_, ...), custom_call_target="tpu_custom_call" | custom-call | flops 536870912 | bytes 2097152 | tf_op jit(solution)/shard_map/pallas_call | solution.py:160
  17.6 0.9 %collective-permute-done.refs_1_ = f32[128,256]{1,0:T(8,128)S(1)} collective-permute-done((f32[128,256]{1,0:T(8,128)S(1)}, f32[128,256]{1,0:T(8,128)S(1)}, u32[]{:S(2)}, u32[]{:S(2)}) %collective-permute-start) | collective-permute-done | bytes 131104 | tf_op jit(solution)/shard_map/ppermute | solution.py:439
  18.6 3.2 %collective-permute-start.1 = (f32[128,256]{1,0:T(8,128)S(1)}, f32[128,256]{1,0:T(8,128)S(1)}, u32[]{:S(2)}, u32[]{:S(2)}) collective-permute-start(f32[128,256]{1,0:T(8,128)S(1)} %shard_map.44), channel_id=1, source_target_pairs={{0,8},{2,10},{4,12},{6,14},{8,0},{10,2},{12,4},{14,6},{1,9},{3,11}... | collective-permute-start | bytes 393224 | tf_op jit(solution)/shard_map/ppermute | solution.py:443
  21.8 1.6 %collective-permute-start.3 = (f32[128,256]{1,0:T(8,128)S(1)}, f32[128,256]{1,0:T(8,128)S(1)}, u32[]{:S(2)}, u32[]{:S(2)}) collective-permute-start(f32[128,256]{1,0:T(8,128)S(1)} %get-tuple-element.45), channel_id=1, source_target_pairs={{0,4},{2,6},{4,8},{6,10},{8,12},{10,14},{12,0},{14,2},{1,5},{3,7},... | collective-permute-start | bytes 393224 | tf_op jit(solution)/shard_map/ppermute | solution.py:443
  23.4 2.2 %collective-permute-start.4 = (f32[128,256]{1,0:T(8,128)S(1)}, f32[128,256]{1,0:T(8,128)S(1)}, u32[]{:S(2)}, u32[]{:S(2)}) collective-permute-start(f32[128,256]{1,0:T(8,128)S(1)} %get-tuple-element.46), channel_id=1, source_target_pairs={{0,12},{2,14},{4,0},{6,2},{8,4},{10,6},{12,8},{14,10},{1,13},{3,15... | collective-permute-start | bytes 393224 | tf_op jit(solution)/shard_map/ppermute | solution.py:443
  25.6 0.9 %shard_map.48 = (f32[128,256]{1,0:T(8,128)S(1)}, bf16[128,4096]{1,0:T(8,128)(2,1)S(1)}) custom-call(bf16[1024,32,128]{2,1,0:T(8,128)(2,1)} %refs_0_.11, bf16[128,32,128]{2,1,0:T(8,128)(2,1)S(1)} %get-tuple-element.47.refs_1_, bf16[128,256]{1,0:T(8,128)(2,1)S(1)} %get-tuple-element.35.refs_2_, f32[32,256]{1,0:T(8,128)S(1)} %get-tuple-element.36.refs_3_), custom_call_target="tpu_custom_call" | custom-call | flops 268435456 | bytes 1048576 | tf_op jit(solution)/shard_map/pallas_call | solution.py:160
  26.6 3.7 %collective-permute-done.1.refs_0_ = f32[128,256]{1,0:T(8,128)S(1)} collective-permute-done((f32[128,256]{1,0:T(8,128)S(1)}, f32[128,256]{1,0:T(8,128)S(1)}, u32[]{:S(2)}, u32[]{:S(2)}) %collective-permute-start.1) | collective-permute-done | bytes 131104 | tf_op jit(solution)/shard_map/ppermute | solution.py:443
  30.6 3.3 %collective-permute-start.11 = (f32[128,256]{1,0:T(8,128)S(1)}, f32[128,256]{1,0:T(8,128)S(1)}, u32[]{:S(2)}, u32[]{:S(2)}) collective-permute-start(f32[128,256]{1,0:T(8,128)S(1)} %shard_map.50.refs_0_), channel_id=1, source_target_pairs={{0,12},{2,14},{4,0},{6,2},{8,4},{10,6},{12,8},{14,10},{1,13},{3,15... | collective-permute-start | bytes 393224 | tf_op jit(solution)/shard_map/ppermute | solution.py:443
  33.9 2.0 %collective-permute-start.9 = (f32[128,256]{1,0:T(8,128)S(1)}, f32[128,256]{1,0:T(8,128)S(1)}, u32[]{:S(2)}, u32[]{:S(2)}) collective-permute-start(f32[128,256]{1,0:T(8,128)S(1)} %shard_map.50.refs_0_), channel_id=1, source_target_pairs={{0,8},{2,10},{4,12},{6,14},{8,0},{10,2},{12,4},{14,6},{1,9},{3,11}... | collective-permute-start | bytes 393224 | tf_op jit(solution)/shard_map/ppermute | solution.py:443
  35.9 1.9 %collective-permute-start.7 = (f32[128,256]{1,0:T(8,128)S(1)}, f32[128,256]{1,0:T(8,128)S(1)}, u32[]{:S(2)}, u32[]{:S(2)}) collective-permute-start(f32[128,256]{1,0:T(8,128)S(1)} %shard_map.50.refs_0_), channel_id=1, source_target_pairs={{0,4},{2,6},{4,8},{6,10},{8,12},{10,14},{12,0},{14,2},{1,5},{3,7},... | collective-permute-start | bytes 393224 | tf_op jit(solution)/shard_map/ppermute | solution.py:443
  37.8 1.5 %collective-permute-start.6 = (f32[128,256]{1,0:T(8,128)S(1)}, f32[128,256]{1,0:T(8,128)S(1)}, u32[]{:S(2)}, u32[]{:S(2)}) collective-permute-start(f32[128,256]{1,0:T(8,128)S(1)} %shard_map.50.refs_0_), channel_id=1, source_target_pairs={{0,2},{2,0},{4,6},{6,4},{8,10},{10,8},{12,14},{14,12},{1,3},{3,1},... | collective-permute-start | bytes 393224 | tf_op jit(solution)/shard_map/ppermute | solution.py:439
  39.9 4.6 %collective-permute-done.9.refs_4_ = f32[128,256]{1,0:T(8,128)S(1)} collective-permute-done((f32[128,256]{1,0:T(8,128)S(1)}, f32[128,256]{1,0:T(8,128)S(1)}, u32[]{:S(2)}, u32[]{:S(2)}) %collective-permute-start.9) | collective-permute-done | bytes 131104 | tf_op jit(solution)/shard_map/ppermute | solution.py:443
  44.5 1.5 %collective-permute-start.10 = (f32[128,256]{1,0:T(8,128)S(1)}, f32[128,256]{1,0:T(8,128)S(1)}, u32[]{:S(2)}, u32[]{:S(2)}) collective-permute-start(f32[128,256]{1,0:T(8,128)S(1)} %collective-permute-done.9.refs_4_), channel_id=1, source_target_pairs={{0,2},{2,0},{4,6},{6,4},{8,10},{10,8},{12,14},{14,12},{1,3},{3,1},... | collective-permute-start | bytes 393224 | tf_op jit(solution)/shard_map/ppermute | solution.py:439
  47.0 2.5 %collective-permute-done.10.refs_5_ = f32[128,256]{1,0:T(8,128)S(1)} collective-permute-done((f32[128,256]{1,0:T(8,128)S(1)}, f32[128,256]{1,0:T(8,128)S(1)}, u32[]{:S(2)}, u32[]{:S(2)}) %collective-permute-start.10) | collective-permute-done | bytes 131104 | tf_op jit(solution)/shard_map/ppermute | solution.py:439
  49.5 1.5 %collective-permute-done.8.refs_3_ = f32[128,256]{1,0:T(8,128)S(1)} collective-permute-done((f32[128,256]{1,0:T(8,128)S(1)}, f32[128,256]{1,0:T(8,128)S(1)}, u32[]{:S(2)}, u32[]{:S(2)}) %collective-permute-start.8) | collective-permute-done | bytes 131104 | tf_op jit(solution)/shard_map/ppermute | solution.py:439
  51.0 0.8 %shard_map.51.gram = f32[256,256]{1,0:T(8,128)S(1)} custom-call(f32[128,256]{1,0:T(8,128)S(1)} %shard_map.50.refs_0_, f32[128,256]{1,0:T(8,128)S(1)} %collective-permute-done.6.refs_1_, f32[128,256]{1,0:T(8,128)S(1)} %collective-permute-done.7.refs_2_, f32[128,256]{1,0:T(8,128)S(1)} %collective-permute-done.8.refs_3_, ...), custom_call_target="tpu_custom_call" | custom-call | flops 536870912 | bytes 1048576 | tf_op jit(solution)/shard_map/pallas_call | solution.py:317
  51.9 1.5 %collective-permute-done.13.came = f32[256,256]{1,0:T(8,128)S(1)} collective-permute-done((f32[256,256]{1,0:T(8,128)S(1)}, f32[256,256]{1,0:T(8,128)S(1)}, u32[]{:S(2)}, u32[]{:S(2)}) %collective-permute-start.13) | collective-permute-done | bytes 262176 | tf_op jit(solution)/shard_map/ppermute | solution.py:446
  53.4 6.4 %shard_map.52.inverse_ref = f32[256,256]{1,0:T(8,128)S(1)} custom-call(f32[256,256]{1,0:T(8,128)S(1)} %shard_map.51.gram, f32[256,256]{1,0:T(8,128)S(1)} %collective-permute-done.13.came), custom_call_target="tpu_custom_call" | custom-call | flops 50331648 | bytes 524288 | tf_op jit(solution)/shard_map/pallas_call | solution.py:265
  59.8 1.3 %shard_map.53 = (f32[1024,256]{1,0:T(8,128)S(1)}, bf16[256,1024]{1,0:T(8,128)(2,1)S(1)}) custom-call(f32[256,256]{1,0:T(8,128)S(1)} %shard_map.52.inverse_ref, f32[128,256]{1,0:T(8,128)S(1)} %shard_map.50.refs_0_, f32[128,256]{1,0:T(8,128)S(1)} %collective-permute-done.6.refs_1_, f32[128,256]{1,0:T(8,128)S(1)} %collective-permute-done.7.refs_2_, ...), custom_call_target="tpu_custom_call" | custom-call | flops 402653184 | bytes 2097152 | tf_op jit(solution)/shard_map/pallas_call | solution.py:355
  61.1 1.0 %shard_map.57 = (f32[128,1024]{1,0:T(8,128)S(1)}, f32[128,1024]{1,0:T(8,128)S(1)}) custom-call(bf16[256,1024]{1,0:T(8,128)(2,1)S(1)} %get-tuple-element.51.turned_ref, bf16[128,4096]{1,0:T(8,128)(2,1)S(1)} %get-tuple-element.52.refs_0_, bf16[256,4096]{1,0:T(8,128)(2,1)S(1)} %get-tuple-element.53.refs_1_, bf16[128,4096]{1,0:T(8,128)(2,1)S(1)} %get-tuple-element.54.refs_2_, ...), custom_call_target="tpu_custom_call" | custom-call | flops 536870912 | bytes 2097152 | tf_op jit(solution)/shard_map/pallas_call | solution.py:385
  62.1 1.0 %shard_map.56 = (f32[128,1024]{1,0:T(8,128)S(1)}, f32[128,1024]{1,0:T(8,128)S(1)}) custom-call(bf16[256,1024]{1,0:T(8,128)(2,1)S(1)} %get-tuple-element.51.turned_ref, bf16[128,4096]{1,0:T(8,128)(2,1)S(1)} %get-tuple-element.52.refs_0_, bf16[256,4096]{1,0:T(8,128)(2,1)S(1)} %get-tuple-element.53.refs_1_, bf16[128,4096]{1,0:T(8,128)(2,1)S(1)} %get-tuple-element.54.refs_2_, ...), custom_call_target="tpu_custom_call" | custom-call | flops 536870912 | bytes 2097152 | tf_op jit(solution)/shard_map/pallas_call | solution.py:385
  63.1 1.0 %shard_map.55 = (f32[128,1024]{1,0:T(8,128)S(1)}, f32[128,1024]{1,0:T(8,128)S(1)}) custom-call(bf16[256,1024]{1,0:T(8,128)(2,1)S(1)} %get-tuple-element.51.turned_ref, bf16[128,4096]{1,0:T(8,128)(2,1)S(1)} %get-tuple-element.52.refs_0_, bf16[256,4096]{1,0:T(8,128)(2,1)S(1)} %get-tuple-element.53.refs_1_, bf16[128,4096]{1,0:T(8,128)(2,1)S(1)} %get-tuple-element.54.refs_2_, ...), custom_call_target="tpu_custom_call" | custom-call | flops 536870912 | bytes 2097152 | tf_op jit(solution)/shard_map/pallas_call | solution.py:385
  64.1 1.0 %shard_map.54 = (f32[128,1024]{1,0:T(8,128)S(1)}, f32[128,1024]{1,0:T(8,128)S(1)}) custom-call(bf16[256,1024]{1,0:T(8,128)(2,1)S(1)} %get-tuple-element.51.turned_ref, bf16[128,4096]{1,0:T(8,128)(2,1)S(1)} %get-tuple-element.52.refs_0_, bf16[256,4096]{1,0:T(8,128)(2,1)S(1)} %get-tuple-element.53.refs_1_, bf16[128,4096]{1,0:T(8,128)(2,1)S(1)} %get-tuple-element.54.refs_2_, ...), custom_call_target="tpu_custom_call" | custom-call | flops 536870912 | bytes 2097152 | tf_op jit(solution)/shard_map/pallas_call | solution.py:385
  66.1 1.0 %copy.4 = f32[1024,256]{1,0:T(8,128)} copy(f32[1024,256]{1,0:T(8,128)S(1)} %get-tuple-element.66) | data formatting | bytes 2097152
  67.8 0.7 %collective-permute-done.15.refs_5_ = f32[128,1024]{1,0:T(8,128)S(1)} collective-permute-done((f32[128,1024]{1,0:T(8,128)S(1)}, f32[128,1024]{1,0:T(8,128)S(1)}, u32[]{:S(2)}, u32[]{:S(2)}) %collective-permute-start.15) | collective-permute-done | bytes 524320 | tf_op jit(solution)/shard_map/ppermute | solution.py:446
  69.3 1.1 %shard_map.58 = bf16[128,32,128]{2,1,0:T(8,128)(2,1)} custom-call(f32[128,1024]{1,0:T(8,128)S(1)} %get-tuple-element.58.refs_0_, f32[128,1024]{1,0:T(8,128)S(1)} %get-tuple-element.59.refs_1_, f32[128,1024]{1,0:T(8,128)S(1)} %get-tuple-element.60.refs_2_, f32[128,1024]{1,0:T(8,128)S(1)} %get-tuple-element.61.refs_3_, ...), custom_call_target="tpu_custom_call" | custom-call | bytes 5242880 | tf_op jit(solution)/shard_map/pallas_call | solution.py:420
  (23 shorter events, 4.5 us)
Async XLA Ops:
  5.5 16.2 %collective-permute-start.2 = (f32[256,256]{1,0:T(8,128)S(1)}, f32[256,256]{1,0:T(8,128)S(1)}, u32[]{:S(2)}, u32[]{:S(2)}) collective-permute-start(f32[256,256]{1,0:T(8,128)S(1)} %get-tuple-element.44), channel_id=1, source_target_pairs={{0,2},{2,0},{4,6},{6,4},{8,10},{10,8},{12,14},{14,12},{1,3},{3,1},... | collective-permute-start | bytes 786440 | tf_op jit(solution)/shard_map/ppermute | solution.py:439
  8.6 10.0 %collective-permute-start = (f32[128,256]{1,0:T(8,128)S(1)}, f32[128,256]{1,0:T(8,128)S(1)}, u32[]{:S(2)}, u32[]{:S(2)}) collective-permute-start(f32[128,256]{1,0:T(8,128)S(1)} %get-tuple-element.39), channel_id=1, source_target_pairs={{0,2},{2,0},{4,6},{6,4},{8,10},{10,8},{12,14},{14,12},{1,3},{3,1},... | collective-permute-start | bytes 393224 | tf_op jit(solution)/shard_map/ppermute | solution.py:439
  12.9 13.6 %collective-permute-start.5 = (f32[128,256]{1,0:T(8,128)S(1)}, f32[128,256]{1,0:T(8,128)S(1)}, u32[]{:S(2)}, u32[]{:S(2)}) collective-permute-start(f32[128,256]{1,0:T(8,128)S(1)} %get-tuple-element.49), channel_id=1, source_target_pairs={{0,2},{2,0},{4,6},{6,4},{8,10},{10,8},{12,14},{14,12},{1,3},{3,1},... | collective-permute-start | bytes 393224 | tf_op jit(solution)/shard_map/ppermute | solution.py:439
  18.6 11.7 %collective-permute-start.1 = (f32[128,256]{1,0:T(8,128)S(1)}, f32[128,256]{1,0:T(8,128)S(1)}, u32[]{:S(2)}, u32[]{:S(2)}) collective-permute-start(f32[128,256]{1,0:T(8,128)S(1)} %shard_map.44), channel_id=1, source_target_pairs={{0,8},{2,10},{4,12},{6,14},{8,0},{10,2},{12,4},{14,6},{1,9},{3,11}... | collective-permute-start | bytes 393224 | tf_op jit(solution)/shard_map/ppermute | solution.py:443
  21.8 8.5 %collective-permute-start.3 = (f32[128,256]{1,0:T(8,128)S(1)}, f32[128,256]{1,0:T(8,128)S(1)}, u32[]{:S(2)}, u32[]{:S(2)}) collective-permute-start(f32[128,256]{1,0:T(8,128)S(1)} %get-tuple-element.45), channel_id=1, source_target_pairs={{0,4},{2,6},{4,8},{6,10},{8,12},{10,14},{12,0},{14,2},{1,5},{3,7},... | collective-permute-start | bytes 393224 | tf_op jit(solution)/shard_map/ppermute | solution.py:443
  23.4 7.2 %collective-permute-start.4 = (f32[128,256]{1,0:T(8,128)S(1)}, f32[128,256]{1,0:T(8,128)S(1)}, u32[]{:S(2)}, u32[]{:S(2)}) collective-permute-start(f32[128,256]{1,0:T(8,128)S(1)} %get-tuple-element.46), channel_id=1, source_target_pairs={{0,12},{2,14},{4,0},{6,2},{8,4},{10,6},{12,8},{14,10},{1,13},{3,15... | collective-permute-start | bytes 393224 | tf_op jit(solution)/shard_map/ppermute | solution.py:443
  30.6 8.7 %collective-permute-start.11 = (f32[128,256]{1,0:T(8,128)S(1)}, f32[128,256]{1,0:T(8,128)S(1)}, u32[]{:S(2)}, u32[]{:S(2)}) collective-permute-start(f32[128,256]{1,0:T(8,128)S(1)} %shard_map.50.refs_0_), channel_id=1, source_target_pairs={{0,12},{2,14},{4,0},{6,2},{8,4},{10,6},{12,8},{14,10},{1,13},{3,15... | collective-permute-start | bytes 393224 | tf_op jit(solution)/shard_map/ppermute | solution.py:443
  33.9 10.6 %collective-permute-start.9 = (f32[128,256]{1,0:T(8,128)S(1)}, f32[128,256]{1,0:T(8,128)S(1)}, u32[]{:S(2)}, u32[]{:S(2)}) collective-permute-start(f32[128,256]{1,0:T(8,128)S(1)} %shard_map.50.refs_0_), channel_id=1, source_target_pairs={{0,8},{2,10},{4,12},{6,14},{8,0},{10,2},{12,4},{14,6},{1,9},{3,11}... | collective-permute-start | bytes 393224 | tf_op jit(solution)/shard_map/ppermute | solution.py:443
  35.9 10.1 %collective-permute-start.7 = (f32[128,256]{1,0:T(8,128)S(1)}, f32[128,256]{1,0:T(8,128)S(1)}, u32[]{:S(2)}, u32[]{:S(2)}) collective-permute-start(f32[128,256]{1,0:T(8,128)S(1)} %shard_map.50.refs_0_), channel_id=1, source_target_pairs={{0,4},{2,6},{4,8},{6,10},{8,12},{10,14},{12,0},{14,2},{1,5},{3,7},... | collective-permute-start | bytes 393224 | tf_op jit(solution)/shard_map/ppermute | solution.py:443
  37.8 8.7 %collective-permute-start.6 = (f32[128,256]{1,0:T(8,128)S(1)}, f32[128,256]{1,0:T(8,128)S(1)}, u32[]{:S(2)}, u32[]{:S(2)}) collective-permute-start(f32[128,256]{1,0:T(8,128)S(1)} %shard_map.50.refs_0_), channel_id=1, source_target_pairs={{0,2},{2,0},{4,6},{6,4},{8,10},{10,8},{12,14},{14,12},{1,3},{3,1},... | collective-permute-start | bytes 393224 | tf_op jit(solution)/shard_map/ppermute | solution.py:439
  39.3 7.6 %collective-permute-start.12 = (f32[128,256]{1,0:T(8,128)S(1)}, f32[128,256]{1,0:T(8,128)S(1)}, u32[]{:S(2)}, u32[]{:S(2)}) collective-permute-start(f32[128,256]{1,0:T(8,128)S(1)} %collective-permute-done.11.refs_6_), channel_id=1, source_target_pairs={{0,2},{2,0},{4,6},{6,4},{8,10},{10,8},{12,14},{14,12},{1,3},{3,1},... | collective-permute-start | bytes 393224 | tf_op jit(solution)/shard_map/ppermute | solution.py:439
  44.5 5.0 %collective-permute-start.10 = (f32[128,256]{1,0:T(8,128)S(1)}, f32[128,256]{1,0:T(8,128)S(1)}, u32[]{:S(2)}, u32[]{:S(2)}) collective-permute-start(f32[128,256]{1,0:T(8,128)S(1)} %collective-permute-done.9.refs_4_), channel_id=1, source_target_pairs={{0,2},{2,0},{4,6},{6,4},{8,10},{10,8},{12,14},{14,12},{1,3},{3,1},... | collective-permute-start | bytes 393224 | tf_op jit(solution)/shard_map/ppermute | solution.py:439
  46.0 5.0 %collective-permute-start.8 = (f32[128,256]{1,0:T(8,128)S(1)}, f32[128,256]{1,0:T(8,128)S(1)}, u32[]{:S(2)}, u32[]{:S(2)}) collective-permute-start(f32[128,256]{1,0:T(8,128)S(1)} %collective-permute-done.7.refs_2_), channel_id=1, source_target_pairs={{0,2},{2,0},{4,6},{6,4},{8,10},{10,8},{12,14},{14,12},{1,3},{3,1},... | collective-permute-start | bytes 393224 | tf_op jit(solution)/shard_map/ppermute | solution.py:439
  51.8 1.6 %collective-permute-start.13 = (f32[256,256]{1,0:T(8,128)S(1)}, f32[256,256]{1,0:T(8,128)S(1)}, u32[]{:S(2)}, u32[]{:S(2)}) collective-permute-start(f32[256,256]{1,0:T(8,128)S(1)} %shard_map.51.gram), channel_id=1, source_target_pairs={{0,1},{1,0},{2,3},{3,2},{4,5},{5,4},{6,7},{7,6},{8,9},{9,8},{10,11... | collective-permute-start | bytes 786440 | tf_op jit(solution)/shard_map/ppermute | solution.py:446
  65.0 2.1 %collective-permute-start.17 = (f32[128,1024]{1,0:T(8,128)S(1)}, f32[128,1024]{1,0:T(8,128)S(1)}, u32[]{:S(2)}, u32[]{:S(2)}) collective-permute-start(f32[128,1024]{1,0:T(8,128)S(1)} %get-tuple-element.65), channel_id=1, source_target_pairs={{0,1},{1,0},{2,3},{3,2},{4,5},{5,4},{6,7},{7,6},{8,9},{9,8},{10,11... | collective-permute-start | bytes 1572872 | tf_op jit(solution)/shard_map/ppermute | solution.py:446
  65.2 2.5 %collective-permute-start.16 = (f32[128,1024]{1,0:T(8,128)S(1)}, f32[128,1024]{1,0:T(8,128)S(1)}, u32[]{:S(2)}, u32[]{:S(2)}) collective-permute-start(f32[128,1024]{1,0:T(8,128)S(1)} %get-tuple-element.64), channel_id=1, source_target_pairs={{0,1},{1,0},{2,3},{3,2},{4,5},{5,4},{6,7},{7,6},{8,9},{9,8},{10,11... | collective-permute-start | bytes 1572872 | tf_op jit(solution)/shard_map/ppermute | solution.py:446
  65.6 2.9 %collective-permute-start.15 = (f32[128,1024]{1,0:T(8,128)S(1)}, f32[128,1024]{1,0:T(8,128)S(1)}, u32[]{:S(2)}, u32[]{:S(2)}) collective-permute-start(f32[128,1024]{1,0:T(8,128)S(1)} %get-tuple-element.63), channel_id=1, source_target_pairs={{0,1},{1,0},{2,3},{3,2},{4,5},{5,4},{6,7},{7,6},{8,9},{9,8},{10,11... | collective-permute-start | bytes 1572872 | tf_op jit(solution)/shard_map/ppermute | solution.py:446
  65.8 3.5 %collective-permute-start.14 = (f32[128,1024]{1,0:T(8,128)S(1)}, f32[128,1024]{1,0:T(8,128)S(1)}, u32[]{:S(2)}, u32[]{:S(2)}) collective-permute-start(f32[128,1024]{1,0:T(8,128)S(1)} %get-tuple-element.62), channel_id=1, source_target_pairs={{0,1},{1,0},{2,3},{3,2},{4,5},{5,4},{6,7},{7,6},{8,9},{9,8},{10,11... | collective-permute-start | bytes 1572872 | tf_op jit(solution)/shard_map/ppermute | solution.py:446

commit v4 on v3

--- a/solution.py
+++ b/solution.py
@@ -91,51 +91,63 @@
                 )
                 copy.start()
                 copies.append(copy)
-        if opening:
-            seeds_copy = pltpu.make_async_copy(seeds_hbm, seeds_ref, sems.at[len(copies)])
-            seeds_copy.start()
-            seeds_copy.wait()
+
+        def make_tables():
             omega_z[...] = omega_table(
                 seeds_ref[3], seeds_ref[4], seeds_ref[5], 0, z_local
             ).astype(bf16)
             omega_y[...] = omega_table(
                 seeds_ref[0], seeds_ref[1], seeds_ref[2], me * y_local, y_local
             )
-        scratch = refs
-        table_z = omega_z[...]
-
-        def spread(block):
+
+        def make_rows():
+            scratch = refs
+            table_z = omega_z[...]
+
+            def spread(block):
+                if opening:
+                    for k in range(block * sub // piece, (block + 1) * sub // piece):
+                        copies[k].wait()
+                for x in range(sub):
+                    scratch[block % 2][x * stride:x * stride + y_local, :] = (
+                        rows[block * sub + x].astype(f32)
+                    )
+
+            spread(0)
+            for block in range(span * parts):
+                if block + 1 < span * parts:
+                    spread(block + 1)
+                low = block * sub
+                sums = None
+                for y_cell in range(0, y_local, CELLS):
+                    cells = []
+                    for y_at in range(y_cell, y_cell + CELLS):
+                        cell = scratch[block % 2][pl.ds(y_at, sub, stride=stride), :].astype(bf16)
+                        flat[low:low + sub, y_at * z_local:(y_at + 1) * z_local] = cell
+                        cells.append(cell)
+                    parted = jnp.dot(
+                        jnp.concatenate(cells, axis=0), table_z, preferred_element_type=f32
+                    )
+                    for k in range(CELLS):
+                        part = parted[k * sub:(k + 1) * sub] * omega_y[y_cell + k:y_cell + k + 1, :]
+                        sums = part if sums is None else sums + part
+                if joined:
+                    outs[0][low:low + sub, :] = sums
+                else:
+                    start = block % parts * sub
+                    outs[block // parts][start:start + sub, :] = sums
+
+        if opening:
+            seeds_copy = pltpu.make_async_copy(seeds_hbm, seeds_ref, sems.at[len(copies)])
+            seeds_copy.start()
+
+        @pl.when(me >= 0)
+        def compute():
             if opening:
-                for k in range(block * sub // piece, (block + 1) * sub // piece):
-                    copies[k].wait()
-            for x in range(sub):
-                scratch[block % 2][x * stride:x * stride + y_local, :] = (
-                    rows[block * sub + x].astype(f32)
-                )
-
-        spread(0)
-        for block in range(span * parts):
-            if block + 1 < span * parts:
-                spread(block + 1)
-            low = block * sub
-            sums = None
-            for y_cell in range(0, y_local, CELLS):
-                cells = []
-                for y_at in range(y_cell, y_cell + CELLS):
-                    cell = scratch[block % 2][pl.ds(y_at, sub, stride=stride), :].astype(bf16)
-                    flat[low:low + sub, y_at * z_local:(y_at + 1) * z_local] = cell
-                    cells.append(cell)
-                parted = jnp.dot(
-                    jnp.concatenate(cells, axis=0), table_z, preferred_element_type=f32
-                )
-                for k in range(CELLS):
-                    part = parted[k * sub:(k + 1) * sub] * omega_y[y_cell + k:y_cell + k + 1, :]
-                    sums = part if sums is None else sums + part
-            if joined:
-                outs[0][low:low + sub, :] = sums
-            else:
-                start = block % parts * sub
-                outs[block // parts][start:start + sub, :] = sums
+                seeds_copy.wait()
+                make_tables()
+            make_rows()
+
         for copy in copies[total // piece if opening else 0:]:
             copy.wait()
 
@@ -369,14 +381,8 @@
     def kernel(turned_ref, *refs):
         flat_refs, (other, own) = refs[:-2], refs[-2:]
         for start in range(low, high, WIDTH):
-            sums, depth = None, 0
-            for flat in flat_refs:
-                part = jnp.dot(
-                    turned_ref[:, depth:depth + flat.shape[0]], flat[:, start:start + WIDTH],
-                    preferred_element_type=f32,
-                )
-                depth += flat.shape[0]
-                sums = part if sums is None else sums + part
+            cells = jnp.concatenate([flat[:, start:start + WIDTH] for flat in flat_refs], axis=0)
+            sums = jnp.dot(turned_ref[...], cells, preferred_element_type=f32)
             other[:, start - low:start - low + WIDTH] = sums[:half]
             own[:, start - low:start - low + WIDTH] = sums[half:]
 

time: 70.7 us -> 68.6 us (0.970)
  Pallas kernels: 26.3 us -> 21.9 us
  waiting for transfers between devices: 17.7 us -> 20.1 us
    pallas_call x6, Pallas kernels: 12.7 us -> 9.34 us  [sketch_chunks(): call(kernel, out_shape, in_specs, flops=2 * total * y_local * z_local * R...]
    ppermute x7, waiting for transfers between devices: 5.37 us -> 7.78 us  [neighbour(): return lax.ppermute(value, 'yz', [(i, i ^ 1) for i in range(count)])]
    pallas_call x4, Pallas kernels: 3.87 us -> 2.81 us  [product(): call(kernel, [held(shape, f32), held(shape, f32)], [VMEM_SPACE] * (1 + le...]
  transfers between devices with their start and end apart: 18 -> 18, of which waited for: 11 -> 11; matrix products, arithmetic and copies ran while one was open for 1% -> 1% of each run, Pallas kernels for 11% -> 8%
where the time goes in v4:
time: 68.6 us; the launch traced here: 68.4 us
  starting transfers between devices  24.6 us (36%)
  Pallas kernels  21.9 us (32%)
  waiting for transfers between devices  20.1 us (29%)
  local copies, waits for them, and re-layouts  0.97 us (1%)
  between operations  0.94 us (1%)
    ppermute x6, starting transfers between devices, shift(): return lax.ppermute(value, 'yz', pairs)  14.2 us
    pallas_call x6, Pallas kernels, sketch_chunks(): call(kernel, out_shape, in_specs, flops=2 * total * y_local * z_local * R...  9.34 us
    ppermute x7, starting transfers between devices, neighbour(): return lax.ppermute(value, 'yz', [(i, i ^ 1) for i in range(count)])  9.2 us
    ppermute x6, waiting for transfers between devices, shift(): return lax.ppermute(value, 'yz', pairs)  8.64 us
    ppermute x7, waiting for transfers between devices, neighbour(): return lax.ppermute(value, 'yz', [(i, i ^ 1) for i in range(count)])  7.78 us
    pallas_call x1, Pallas kernels, inverse_factor(): call(inverse_factor_kernel, held(gram.shape, f32), [VMEM_SPACE] * 2, flop...  6.43 us
    ppermute x5, waiting for transfers between devices, other_core(): return lax.ppermute(value, 'gx', [(0, 1), (1, 0)])  3.69 us
    pallas_call x4, Pallas kernels, product(): call(kernel, [held(shape, f32), held(shape, f32)], [VMEM_SPACE] * (1 + le...  2.81 us
  transfers between devices with their start and end apart: 18, of which 11 were waited for; matrix products, arithmetic and copies ran while one was open for 1% of the time, Pallas kernels for 8%

profile of v4, /device:TPU:0, one launch (start us, length us, event | category | flops | bytes accessed | tf_op | source)
XLA Modules:
  0.0 68.4 jit_solution(14306971919758830176)
XLA Ops:
  0.6 2.2 %shard_map.41 = (f32[128,256]{1,0:T(8,128)S(1)}, bf16[128,4096]{1,0:T(8,128)(2,1)S(1)}, bf16[256,32,128]{2,1,0:T(8,128)(2,1)S(1)}, bf16[128,256]{1,0:T(8,128)(2,1)S(1)}, f32[32,256]{1,0:T(8,128)S(1)}) custom-call(bf16[1024,32,128]{2,1,0:T(8,128)(2,1)} %refs_0_.11, s32[6]{0:T(128)} %refs_1_.1), custom_call_target="tpu_custom_call" | custom-call | flops 268435456 | bytes 1048576 | tf_op jit(solution)/shard_map/pallas_call | solution.py:172
  2.8 1.7 %shard_map.42 = (f32[256,256]{1,0:T(8,128)S(1)}, bf16[256,4096]{1,0:T(8,128)(2,1)S(1)}, bf16[128,32,128]{2,1,0:T(8,128)(2,1)S(1)}) custom-call(bf16[1024,32,128]{2,1,0:T(8,128)(2,1)} %refs_0_.11, bf16[256,32,128]{2,1,0:T(8,128)(2,1)S(1)} %get-tuple-element.34.refs_1_, bf16[128,256]{1,0:T(8,128)(2,1)S(1)} %get-tuple-element.35.refs_2_, ...), custom_call_target="tpu_custom_call" | custom-call | flops 536870912 | bytes 2097152 | tf_op jit(solution)/shard_map/pallas_call | solution.py:172
  4.6 3.1 %collective-permute-start.2 = (f32[256,256]{1,0:T(8,128)S(1)}, f32[256,256]{1,0:T(8,128)S(1)}, u32[]{:S(2)}, u32[]{:S(2)}) collective-permute-start(f32[256,256]{1,0:T(8,128)S(1)} %get-tuple-element.44), channel_id=1, source_target_pairs={{0,2},{2,0},{4,6},{6,4},{8,10},{10,8},{12,14},{14,12},{1,3},{3,1},... | collective-permute-start | bytes 786440 | tf_op jit(solution)/shard_map/ppermute | solution.py:445
  7.7 1.2 %shard_map.43 = (f32[128,256]{1,0:T(8,128)S(1)}, bf16[128,4096]{1,0:T(8,128)(2,1)S(1)}, bf16[128,32,128]{2,1,0:T(8,128)(2,1)S(1)}) custom-call(bf16[1024,32,128]{2,1,0:T(8,128)(2,1)} %refs_0_.11, bf16[128,32,128]{2,1,0:T(8,128)(2,1)S(1)} %get-tuple-element.37.refs_1_, bf16[128,256]{1,0:T(8,128)(2,1)S(1)} %get-tuple-element.35.refs_2_, ...), custom_call_target="tpu_custom_call" | custom-call | flops 268435456 | bytes 1048576 | tf_op jit(solution)/shard_map/pallas_call | solution.py:172
  8.9 1.6 %shard_map.45 = (f32[128,256]{1,0:T(8,128)S(1)}, bf16[128,4096]{1,0:T(8,128)(2,1)S(1)}, bf16[256,32,128]{2,1,0:T(8,128)(2,1)S(1)}) custom-call(bf16[1024,32,128]{2,1,0:T(8,128)(2,1)} %refs_0_.11, bf16[128,32,128]{2,1,0:T(8,128)(2,1)S(1)} %get-tuple-element.40.refs_1_, bf16[128,256]{1,0:T(8,128)(2,1)S(1)} %get-tuple-element.35.refs_2_, ...), custom_call_target="tpu_custom_call" | custom-call | flops 268435456 | bytes 1048576 | tf_op jit(solution)/shard_map/pallas_call | solution.py:172
  10.5 2.0 %collective-permute-start.5 = (f32[128,256]{1,0:T(8,128)S(1)}, f32[128,256]{1,0:T(8,128)S(1)}, u32[]{:S(2)}, u32[]{:S(2)}) collective-permute-start(f32[128,256]{1,0:T(8,128)S(1)} %get-tuple-element.49), channel_id=1, source_target_pairs={{0,2},{2,0},{4,6},{6,4},{8,10},{10,8},{12,14},{14,12},{1,3},{3,1},... | collective-permute-start | bytes 393224 | tf_op jit(solution)/shard_map/ppermute | solution.py:445
  12.6 1.7 %shard_map.46 = (f32[128,256]{1,0:T(8,128)S(1)}, f32[128,256]{1,0:T(8,128)S(1)}, bf16[256,4096]{1,0:T(8,128)(2,1)S(1)}, bf16[128,32,128]{2,1,0:T(8,128)(2,1)S(1)}) custom-call(bf16[1024,32,128]{2,1,0:T(8,128)(2,1)} %refs_0_.11, bf16[256,32,128]{2,1,0:T(8,128)(2,1)S(1)} %get-tuple-element.41.refs_1_, bf16[128,256]{1,0:T(8,128)(2,1)S(1)} %get-tuple-element.35.refs_2_, ...), custom_call_target="tpu_custom_call" | custom-call | flops 536870912 | bytes 2097152 | tf_op jit(solution)/shard_map/pallas_call | solution.py:172
  14.3 3.3 %collective-permute-done.refs_1_ = f32[128,256]{1,0:T(8,128)S(1)} collective-permute-done((f32[128,256]{1,0:T(8,128)S(1)}, f32[128,256]{1,0:T(8,128)S(1)}, u32[]{:S(2)}, u32[]{:S(2)}) %collective-permute-start) | collective-permute-done | bytes 131104 | tf_op jit(solution)/shard_map/ppermute | solution.py:445
  17.6 3.2 %collective-permute-start.1 = (f32[128,256]{1,0:T(8,128)S(1)}, f32[128,256]{1,0:T(8,128)S(1)}, u32[]{:S(2)}, u32[]{:S(2)}) collective-permute-start(f32[128,256]{1,0:T(8,128)S(1)} %shard_map.44), channel_id=1, source_target_pairs={{0,8},{2,10},{4,12},{6,14},{8,0},{10,2},{12,4},{14,6},{1,9},{3,11}... | collective-permute-start | bytes 393224 | tf_op jit(solution)/shard_map/ppermute | solution.py:449
  20.8 1.6 %collective-permute-start.3 = (f32[128,256]{1,0:T(8,128)S(1)}, f32[128,256]{1,0:T(8,128)S(1)}, u32[]{:S(2)}, u32[]{:S(2)}) collective-permute-start(f32[128,256]{1,0:T(8,128)S(1)} %get-tuple-element.45), channel_id=1, source_target_pairs={{0,4},{2,6},{4,8},{6,10},{8,12},{10,14},{12,0},{14,2},{1,5},{3,7},... | collective-permute-start | bytes 393224 | tf_op jit(solution)/shard_map/ppermute | solution.py:449
  22.4 2.3 %collective-permute-start.4 = (f32[128,256]{1,0:T(8,128)S(1)}, f32[128,256]{1,0:T(8,128)S(1)}, u32[]{:S(2)}, u32[]{:S(2)}) collective-permute-start(f32[128,256]{1,0:T(8,128)S(1)} %get-tuple-element.46), channel_id=1, source_target_pairs={{0,12},{2,14},{4,0},{6,2},{8,4},{10,6},{12,8},{14,10},{1,13},{3,15... | collective-permute-start | bytes 393224 | tf_op jit(solution)/shard_map/ppermute | solution.py:449
  24.7 0.9 %shard_map.48 = (f32[128,256]{1,0:T(8,128)S(1)}, bf16[128,4096]{1,0:T(8,128)(2,1)S(1)}) custom-call(bf16[1024,32,128]{2,1,0:T(8,128)(2,1)} %refs_0_.11, bf16[128,32,128]{2,1,0:T(8,128)(2,1)S(1)} %get-tuple-element.47.refs_1_, bf16[128,256]{1,0:T(8,128)(2,1)S(1)} %get-tuple-element.35.refs_2_, f32[32,256]{1,0:T(8,128)S(1)} %get-tuple-element.36.refs_3_), custom_call_target="tpu_custom_call" | custom-call | flops 268435456 | bytes 1048576 | tf_op jit(solution)/shard_map/pallas_call | solution.py:172
  25.6 3.7 %collective-permute-done.1.refs_0_ = f32[128,256]{1,0:T(8,128)S(1)} collective-permute-done((f32[128,256]{1,0:T(8,128)S(1)}, f32[128,256]{1,0:T(8,128)S(1)}, u32[]{:S(2)}, u32[]{:S(2)}) %collective-permute-start.1) | collective-permute-done | bytes 131104 | tf_op jit(solution)/shard_map/ppermute | solution.py:449
  29.7 3.3 %collective-permute-start.11 = (f32[128,256]{1,0:T(8,128)S(1)}, f32[128,256]{1,0:T(8,128)S(1)}, u32[]{:S(2)}, u32[]{:S(2)}) collective-permute-start(f32[128,256]{1,0:T(8,128)S(1)} %shard_map.50.refs_0_), channel_id=1, source_target_pairs={{0,12},{2,14},{4,0},{6,2},{8,4},{10,6},{12,8},{14,10},{1,13},{3,15... | collective-permute-start | bytes 393224 | tf_op jit(solution)/shard_map/ppermute | solution.py:449
  32.9 2.0 %collective-permute-start.9 = (f32[128,256]{1,0:T(8,128)S(1)}, f32[128,256]{1,0:T(8,128)S(1)}, u32[]{:S(2)}, u32[]{:S(2)}) collective-permute-start(f32[128,256]{1,0:T(8,128)S(1)} %shard_map.50.refs_0_), channel_id=1, source_target_pairs={{0,8},{2,10},{4,12},{6,14},{8,0},{10,2},{12,4},{14,6},{1,9},{3,11}... | collective-permute-start | bytes 393224 | tf_op jit(solution)/shard_map/ppermute | solution.py:449
  34.9 1.9 %collective-permute-start.7 = (f32[128,256]{1,0:T(8,128)S(1)}, f32[128,256]{1,0:T(8,128)S(1)}, u32[]{:S(2)}, u32[]{:S(2)}) collective-permute-start(f32[128,256]{1,0:T(8,128)S(1)} %shard_map.50.refs_0_), channel_id=1, source_target_pairs={{0,4},{2,6},{4,8},{6,10},{8,12},{10,14},{12,0},{14,2},{1,5},{3,7},... | collective-permute-start | bytes 393224 | tf_op jit(solution)/shard_map/ppermute | solution.py:449
  36.8 1.5 %collective-permute-start.6 = (f32[128,256]{1,0:T(8,128)S(1)}, f32[128,256]{1,0:T(8,128)S(1)}, u32[]{:S(2)}, u32[]{:S(2)}) collective-permute-start(f32[128,256]{1,0:T(8,128)S(1)} %shard_map.50.refs_0_), channel_id=1, source_target_pairs={{0,2},{2,0},{4,6},{6,4},{8,10},{10,8},{12,14},{14,12},{1,3},{3,1},... | collective-permute-start | bytes 393224 | tf_op jit(solution)/shard_map/ppermute | solution.py:445
  38.9 4.6 %collective-permute-done.9.refs_4_ = f32[128,256]{1,0:T(8,128)S(1)} collective-permute-done((f32[128,256]{1,0:T(8,128)S(1)}, f32[128,256]{1,0:T(8,128)S(1)}, u32[]{:S(2)}, u32[]{:S(2)}) %collective-permute-start.9) | collective-permute-done | bytes 131104 | tf_op jit(solution)/shard_map/ppermute | solution.py:449
  43.5 1.5 %collective-permute-start.10 = (f32[128,256]{1,0:T(8,128)S(1)}, f32[128,256]{1,0:T(8,128)S(1)}, u32[]{:S(2)}, u32[]{:S(2)}) collective-permute-start(f32[128,256]{1,0:T(8,128)S(1)} %collective-permute-done.9.refs_4_), channel_id=1, source_target_pairs={{0,2},{2,0},{4,6},{6,4},{8,10},{10,8},{12,14},{14,12},{1,3},{3,1},... | collective-permute-start | bytes 393224 | tf_op jit(solution)/shard_map/ppermute | solution.py:445
  46.0 2.4 %collective-permute-done.10.refs_5_ = f32[128,256]{1,0:T(8,128)S(1)} collective-permute-done((f32[128,256]{1,0:T(8,128)S(1)}, f32[128,256]{1,0:T(8,128)S(1)}, u32[]{:S(2)}, u32[]{:S(2)}) %collective-permute-start.10) | collective-permute-done | bytes 131104 | tf_op jit(solution)/shard_map/ppermute | solution.py:445
  48.5 1.5 %collective-permute-done.8.refs_3_ = f32[128,256]{1,0:T(8,128)S(1)} collective-permute-done((f32[128,256]{1,0:T(8,128)S(1)}, f32[128,256]{1,0:T(8,128)S(1)}, u32[]{:S(2)}, u32[]{:S(2)}) %collective-permute-start.8) | collective-permute-done | bytes 131104 | tf_op jit(solution)/shard_map/ppermute | solution.py:445
  50.0 0.8 %shard_map.51.gram = f32[256,256]{1,0:T(8,128)S(1)} custom-call(f32[128,256]{1,0:T(8,128)S(1)} %shard_map.50.refs_0_, f32[128,256]{1,0:T(8,128)S(1)} %collective-permute-done.6.refs_1_, f32[128,256]{1,0:T(8,128)S(1)} %collective-permute-done.7.refs_2_, f32[128,256]{1,0:T(8,128)S(1)} %collective-permute-done.8.refs_3_, ...), custom_call_target="tpu_custom_call" | custom-call | flops 536870912 | bytes 1048576 | tf_op jit(solution)/shard_map/pallas_call | solution.py:329
  50.9 1.5 %collective-permute-done.13.came = f32[256,256]{1,0:T(8,128)S(1)} collective-permute-done((f32[256,256]{1,0:T(8,128)S(1)}, f32[256,256]{1,0:T(8,128)S(1)}, u32[]{:S(2)}, u32[]{:S(2)}) %collective-permute-start.13) | collective-permute-done | bytes 262176 | tf_op jit(solution)/shard_map/ppermute | solution.py:452
  52.4 6.4 %shard_map.52.inverse_ref = f32[256,256]{1,0:T(8,128)S(1)} custom-call(f32[256,256]{1,0:T(8,128)S(1)} %shard_map.51.gram, f32[256,256]{1,0:T(8,128)S(1)} %collective-permute-done.13.came), custom_call_target="tpu_custom_call" | custom-call | flops 50331648 | bytes 524288 | tf_op jit(solution)/shard_map/pallas_call | solution.py:277
  58.8 1.3 %shard_map.53 = (f32[1024,256]{1,0:T(8,128)S(1)}, bf16[256,1024]{1,0:T(8,128)(2,1)S(1)}) custom-call(f32[256,256]{1,0:T(8,128)S(1)} %shard_map.52.inverse_ref, f32[128,256]{1,0:T(8,128)S(1)} %shard_map.50.refs_0_, f32[128,256]{1,0:T(8,128)S(1)} %collective-permute-done.6.refs_1_, f32[128,256]{1,0:T(8,128)S(1)} %collective-permute-done.7.refs_2_, ...), custom_call_target="tpu_custom_call" | custom-call | flops 402653184 | bytes 2097152 | tf_op jit(solution)/shard_map/pallas_call | solution.py:367
  60.9 0.7 %shard_map.56 = (f32[128,1024]{1,0:T(8,128)S(1)}, f32[128,1024]{1,0:T(8,128)S(1)}) custom-call(bf16[256,1024]{1,0:T(8,128)(2,1)S(1)} %get-tuple-element.51.turned_ref, bf16[128,4096]{1,0:T(8,128)(2,1)S(1)} %get-tuple-element.52.refs_0_, bf16[256,4096]{1,0:T(8,128)(2,1)S(1)} %get-tuple-element.53.refs_1_, bf16[128,4096]{1,0:T(8,128)(2,1)S(1)} %get-tuple-element.54.refs_2_, ...), custom_call_target="tpu_custom_call" | custom-call | flops 536870912 | bytes 2097152 | tf_op jit(solution)/shard_map/pallas_call | solution.py:391
  61.6 0.7 %shard_map.55 = (f32[128,1024]{1,0:T(8,128)S(1)}, f32[128,1024]{1,0:T(8,128)S(1)}) custom-call(bf16[256,1024]{1,0:T(8,128)(2,1)S(1)} %get-tuple-element.51.turned_ref, bf16[128,4096]{1,0:T(8,128)(2,1)S(1)} %get-tuple-element.52.refs_0_, bf16[256,4096]{1,0:T(8,128)(2,1)S(1)} %get-tuple-element.53.refs_1_, bf16[128,4096]{1,0:T(8,128)(2,1)S(1)} %get-tuple-element.54.refs_2_, ...), custom_call_target="tpu_custom_call" | custom-call | flops 536870912 | bytes 2097152 | tf_op jit(solution)/shard_map/pallas_call | solution.py:391
  62.3 0.7 %shard_map.54 = (f32[128,1024]{1,0:T(8,128)S(1)}, f32[128,1024]{1,0:T(8,128)S(1)}) custom-call(bf16[256,1024]{1,0:T(8,128)(2,1)S(1)} %get-tuple-element.51.turned_ref, bf16[128,4096]{1,0:T(8,128)(2,1)S(1)} %get-tuple-element.52.refs_0_, bf16[256,4096]{1,0:T(8,128)(2,1)S(1)} %get-tuple-element.53.refs_1_, bf16[128,4096]{1,0:T(8,128)(2,1)S(1)} %get-tuple-element.54.refs_2_, ...), custom_call_target="tpu_custom_call" | custom-call | flops 536870912 | bytes 2097152 | tf_op jit(solution)/shard_map/pallas_call | solution.py:391
  64.1 1.0 %copy.4 = f32[1024,256]{1,0:T(8,128)} copy(f32[1024,256]{1,0:T(8,128)S(1)} %get-tuple-element.66) | data formatting | bytes 2097152
  65.7 0.7 %collective-permute-done.15.refs_5_ = f32[128,1024]{1,0:T(8,128)S(1)} collective-permute-done((f32[128,1024]{1,0:T(8,128)S(1)}, f32[128,1024]{1,0:T(8,128)S(1)}, u32[]{:S(2)}, u32[]{:S(2)}) %collective-permute-start.15) | collective-permute-done | bytes 524320 | tf_op jit(solution)/shard_map/ppermute | solution.py:452
  66.5 0.7 %collective-permute-done.14.refs_4_ = f32[128,1024]{1,0:T(8,128)S(1)} collective-permute-done((f32[128,1024]{1,0:T(8,128)S(1)}, f32[128,1024]{1,0:T(8,128)S(1)}, u32[]{:S(2)}, u32[]{:S(2)}) %collective-permute-start.14) | collective-permute-done | bytes 524320 | tf_op jit(solution)/shard_map/ppermute | solution.py:452
  67.2 1.1 %shard_map.58 = bf16[128,32,128]{2,1,0:T(8,128)(2,1)} custom-call(f32[128,1024]{1,0:T(8,128)S(1)} %get-tuple-element.58.refs_0_, f32[128,1024]{1,0:T(8,128)S(1)} %get-tuple-element.59.refs_1_, f32[128,1024]{1,0:T(8,128)S(1)} %get-tuple-element.60.refs_2_, f32[128,1024]{1,0:T(8,128)S(1)} %get-tuple-element.61.refs_3_, ...), custom_call_target="tpu_custom_call" | custom-call | bytes 5242880 | tf_op jit(solution)/shard_map/pallas_call | solution.py:426
  (23 shorter events, 4.5 us)
Async XLA Ops:
  4.6 16.2 %collective-permute-start.2 = (f32[256,256]{1,0:T(8,128)S(1)}, f32[256,256]{1,0:T(8,128)S(1)}, u32[]{:S(2)}, u32[]{:S(2)}) collective-permute-start(f32[256,256]{1,0:T(8,128)S(1)} %get-tuple-element.44), channel_id=1, source_target_pairs={{0,2},{2,0},{4,6},{6,4},{8,10},{10,8},{12,14},{14,12},{1,3},{3,1},... | collective-permute-start | bytes 786440 | tf_op jit(solution)/shard_map/ppermute | solution.py:445
  7.6 10.0 %collective-permute-start = (f32[128,256]{1,0:T(8,128)S(1)}, f32[128,256]{1,0:T(8,128)S(1)}, u32[]{:S(2)}, u32[]{:S(2)}) collective-permute-start(f32[128,256]{1,0:T(8,128)S(1)} %get-tuple-element.39), channel_id=1, source_target_pairs={{0,2},{2,0},{4,6},{6,4},{8,10},{10,8},{12,14},{14,12},{1,3},{3,1},... | collective-permute-start | bytes 393224 | tf_op jit(solution)/shard_map/ppermute | solution.py:445
  10.5 15.0 %collective-permute-start.5 = (f32[128,256]{1,0:T(8,128)S(1)}, f32[128,256]{1,0:T(8,128)S(1)}, u32[]{:S(2)}, u32[]{:S(2)}) collective-permute-start(f32[128,256]{1,0:T(8,128)S(1)} %get-tuple-element.49), channel_id=1, source_target_pairs={{0,2},{2,0},{4,6},{6,4},{8,10},{10,8},{12,14},{14,12},{1,3},{3,1},... | collective-permute-start | bytes 393224 | tf_op jit(solution)/shard_map/ppermute | solution.py:445
  17.6 11.7 %collective-permute-start.1 = (f32[128,256]{1,0:T(8,128)S(1)}, f32[128,256]{1,0:T(8,128)S(1)}, u32[]{:S(2)}, u32[]{:S(2)}) collective-permute-start(f32[128,256]{1,0:T(8,128)S(1)} %shard_map.44), channel_id=1, source_target_pairs={{0,8},{2,10},{4,12},{6,14},{8,0},{10,2},{12,4},{14,6},{1,9},{3,11}... | collective-permute-start | bytes 393224 | tf_op jit(solution)/shard_map/ppermute | solution.py:449
  20.8 8.5 %collective-permute-start.3 = (f32[128,256]{1,0:T(8,128)S(1)}, f32[128,256]{1,0:T(8,128)S(1)}, u32[]{:S(2)}, u32[]{:S(2)}) collective-permute-start(f32[128,256]{1,0:T(8,128)S(1)} %get-tuple-element.45), channel_id=1, source_target_pairs={{0,4},{2,6},{4,8},{6,10},{8,12},{10,14},{12,0},{14,2},{1,5},{3,7},... | collective-permute-start | bytes 393224 | tf_op jit(solution)/shard_map/ppermute | solution.py:449
  22.4 7.2 %collective-permute-start.4 = (f32[128,256]{1,0:T(8,128)S(1)}, f32[128,256]{1,0:T(8,128)S(1)}, u32[]{:S(2)}, u32[]{:S(2)}) collective-permute-start(f32[128,256]{1,0:T(8,128)S(1)} %get-tuple-element.46), channel_id=1, source_target_pairs={{0,12},{2,14},{4,0},{6,2},{8,4},{10,6},{12,8},{14,10},{1,13},{3,15... | collective-permute-start | bytes 393224 | tf_op jit(solution)/shard_map/ppermute | solution.py:449
  29.7 8.7 %collective-permute-start.11 = (f32[128,256]{1,0:T(8,128)S(1)}, f32[128,256]{1,0:T(8,128)S(1)}, u32[]{:S(2)}, u32[]{:S(2)}) collective-permute-start(f32[128,256]{1,0:T(8,128)S(1)} %shard_map.50.refs_0_), channel_id=1, source_target_pairs={{0,12},{2,14},{4,0},{6,2},{8,4},{10,6},{12,8},{14,10},{1,13},{3,15... | collective-permute-start | bytes 393224 | tf_op jit(solution)/shard_map/ppermute | solution.py:449
  32.9 10.6 %collective-permute-start.9 = (f32[128,256]{1,0:T(8,128)S(1)}, f32[128,256]{1,0:T(8,128)S(1)}, u32[]{:S(2)}, u32[]{:S(2)}) collective-permute-start(f32[128,256]{1,0:T(8,128)S(1)} %shard_map.50.refs_0_), channel_id=1, source_target_pairs={{0,8},{2,10},{4,12},{6,14},{8,0},{10,2},{12,4},{14,6},{1,9},{3,11}... | collective-permute-start | bytes 393224 | tf_op jit(solution)/shard_map/ppermute | solution.py:449
  34.9 10.1 %collective-permute-start.7 = (f32[128,256]{1,0:T(8,128)S(1)}, f32[128,256]{1,0:T(8,128)S(1)}, u32[]{:S(2)}, u32[]{:S(2)}) collective-permute-start(f32[128,256]{1,0:T(8,128)S(1)} %shard_map.50.refs_0_), channel_id=1, source_target_pairs={{0,4},{2,6},{4,8},{6,10},{8,12},{10,14},{12,0},{14,2},{1,5},{3,7},... | collective-permute-start | bytes 393224 | tf_op jit(solution)/shard_map/ppermute | solution.py:449
  36.8 8.7 %collective-permute-start.6 = (f32[128,256]{1,0:T(8,128)S(1)}, f32[128,256]{1,0:T(8,128)S(1)}, u32[]{:S(2)}, u32[]{:S(2)}) collective-permute-start(f32[128,256]{1,0:T(8,128)S(1)} %shard_map.50.refs_0_), channel_id=1, source_target_pairs={{0,2},{2,0},{4,6},{6,4},{8,10},{10,8},{12,14},{14,12},{1,3},{3,1},... | collective-permute-start | bytes 393224 | tf_op jit(solution)/shard_map/ppermute | solution.py:445
  38.4 7.6 %collective-permute-start.12 = (f32[128,256]{1,0:T(8,128)S(1)}, f32[128,256]{1,0:T(8,128)S(1)}, u32[]{:S(2)}, u32[]{:S(2)}) collective-permute-start(f32[128,256]{1,0:T(8,128)S(1)} %collective-permute-done.11.refs_6_), channel_id=1, source_target_pairs={{0,2},{2,0},{4,6},{6,4},{8,10},{10,8},{12,14},{14,12},{1,3},{3,1},... | collective-permute-start | bytes 393224 | tf_op jit(solution)/shard_map/ppermute | solution.py:445
  43.5 5.0 %collective-permute-start.10 = (f32[128,256]{1,0:T(8,128)S(1)}, f32[128,256]{1,0:T(8,128)S(1)}, u32[]{:S(2)}, u32[]{:S(2)}) collective-permute-start(f32[128,256]{1,0:T(8,128)S(1)} %collective-permute-done.9.refs_4_), channel_id=1, source_target_pairs={{0,2},{2,0},{4,6},{6,4},{8,10},{10,8},{12,14},{14,12},{1,3},{3,1},... | collective-permute-start | bytes 393224 | tf_op jit(solution)/shard_map/ppermute | solution.py:445
  45.0 5.0 %collective-permute-start.8 = (f32[128,256]{1,0:T(8,128)S(1)}, f32[128,256]{1,0:T(8,128)S(1)}, u32[]{:S(2)}, u32[]{:S(2)}) collective-permute-start(f32[128,256]{1,0:T(8,128)S(1)} %collective-permute-done.7.refs_2_), channel_id=1, source_target_pairs={{0,2},{2,0},{4,6},{6,4},{8,10},{10,8},{12,14},{14,12},{1,3},{3,1},... | collective-permute-start | bytes 393224 | tf_op jit(solution)/shard_map/ppermute | solution.py:445
  50.8 1.6 %collective-permute-start.13 = (f32[256,256]{1,0:T(8,128)S(1)}, f32[256,256]{1,0:T(8,128)S(1)}, u32[]{:S(2)}, u32[]{:S(2)}) collective-permute-start(f32[256,256]{1,0:T(8,128)S(1)} %shard_map.51.gram), channel_id=1, source_target_pairs={{0,1},{1,0},{2,3},{3,2},{4,5},{5,4},{6,7},{7,6},{8,9},{9,8},{10,11... | collective-permute-start | bytes 786440 | tf_op jit(solution)/shard_map/ppermute | solution.py:452
  63.0 2.1 %collective-permute-start.17 = (f32[128,1024]{1,0:T(8,128)S(1)}, f32[128,1024]{1,0:T(8,128)S(1)}, u32[]{:S(2)}, u32[]{:S(2)}) collective-permute-start(f32[128,1024]{1,0:T(8,128)S(1)} %get-tuple-element.65), channel_id=1, source_target_pairs={{0,1},{1,0},{2,3},{3,2},{4,5},{5,4},{6,7},{7,6},{8,9},{9,8},{10,11... | collective-permute-start | bytes 1572872 | tf_op jit(solution)/shard_map/ppermute | solution.py:452
  63.2 2.5 %collective-permute-start.16 = (f32[128,1024]{1,0:T(8,128)S(1)}, f32[128,1024]{1,0:T(8,128)S(1)}, u32[]{:S(2)}, u32[]{:S(2)}) collective-permute-start(f32[128,1024]{1,0:T(8,128)S(1)} %get-tuple-element.64), channel_id=1, source_target_pairs={{0,1},{1,0},{2,3},{3,2},{4,5},{5,4},{6,7},{7,6},{8,9},{9,8},{10,11... | collective-permute-start | bytes 1572872 | tf_op jit(solution)/shard_map/ppermute | solution.py:452
  63.6 2.9 %collective-permute-start.15 = (f32[128,1024]{1,0:T(8,128)S(1)}, f32[128,1024]{1,0:T(8,128)S(1)}, u32[]{:S(2)}, u32[]{:S(2)}) collective-permute-start(f32[128,1024]{1,0:T(8,128)S(1)} %get-tuple-element.63), channel_id=1, source_target_pairs={{0,1},{1,0},{2,3},{3,2},{4,5},{5,4},{6,7},{7,6},{8,9},{9,8},{10,11... | collective-permute-start | bytes 1572872 | tf_op jit(solution)/shard_map/ppermute | solution.py:452
  63.7 3.5 %collective-permute-start.14 = (f32[128,1024]{1,0:T(8,128)S(1)}, f32[128,1024]{1,0:T(8,128)S(1)}, u32[]{:S(2)}, u32[]{:S(2)}) collective-permute-start(f32[128,1024]{1,0:T(8,128)S(1)} %get-tuple-element.62), channel_id=1, source_target_pairs={{0,1},{1,0},{2,3},{3,2},{4,5},{5,4},{6,7},{7,6},{8,9},{9,8},{10,11... | collective-permute-start | bytes 1572872 | tf_op jit(solution)/shard_map/ppermute | solution.py:452

commit v5 on v4

--- a/solution.py
+++ b/solution.py
@@ -154,7 +154,7 @@
     count = 1 if joined else span
     shape = held((total if joined else chunk, RANK), f32)
     out_shape = [shape] * count + [held((total, y_local * z_local), bf16)]
-    scratch_shapes = [pltpu.VMEM((sub * stride, z_local), f32)] * 2
+    scratch_shapes = [pltpu.VMEM(((sub + 1) * stride, z_local), f32)] * 2
     operands = [pltpu.with_memory_space_constraint(field, pltpu.HBM)]
     if follow:
         out_shape.append(held((len(follow) * chunk, y_local, z_local), bf16))
@@ -187,6 +187,7 @@
 
 
 PANEL = 32
+PIVOTS = 16
 
 
 def inverse_factor_kernel(gram, came, out, state):
@@ -214,38 +215,41 @@
             [jnp.where(lane == row + (offset + 8 * q), 1.0, 0.0).astype(f32) for q in range(groups)]
         )
         done = [[None] * groups for _ in range(3)]
-        for g in range(groups):
-            base = offset + 8 * g
+        scales = [jnp.zeros((8, 128), f32)] * groups
+        ratios = [jnp.zeros((8, 128), f32)] * groups
+        for base in range(0, PANEL, PIVOTS):
             column = [
-                {q: over_lanes(rows[tile][q], base + m) + zero for q in range(g, groups)}
-                for m in range(8)
+                {q: over_lanes(rows[tile][q], offset + base + m) + zero for q in range(base // 8, groups)}
+                for m in range(PIVOTS)
             ]
-            scales, ratios = jnp.zeros((8, 128), f32), jnp.zeros((8, 128), f32)
-            for i in range(0, 8, 2):
-                d11, d12 = over_rows(column[i][g], i), over_rows(column[i + 1][g], i)
-                d22 = over_rows(column[i + 1][g], i + 1)
+            for c in range(0, PIVOTS, 2):
+                g, i = (base + c) // 8, c % 8
+                d11, d12 = over_rows(column[c][g], i), over_rows(column[c + 1][g], i)
+                d22 = over_rows(column[c + 1][g], i + 1)
                 inverse = pl.reciprocal(d11 * d22 - d12 * d12)
                 k11, k12, k22 = d22 * inverse, d12 * inverse, d11 * inverse
                 ratio = d12 * pl.reciprocal(d11)
                 root1, root2 = lax.rsqrt(d11), lax.rsqrt(d22 - ratio * d12)
-                scales = jnp.where(row == i, root1, jnp.where(row == i + 1, root2, scales))
-                ratios = jnp.where(row == i + 1, ratio, ratios)
-                left, right = dict(column[i]), dict(column[i + 1])
+                scales[g] = jnp.where(row == i, root1, jnp.where(row == i + 1, root2, scales[g]))
+                ratios[g] = jnp.where(row == i + 1, ratio, ratios[g])
+                left, right = dict(column[c]), dict(column[c + 1])
                 left[g] = jnp.where(row > i + 1, left[g], 0.0)
                 right[g] = jnp.where(row > i + 1, right[g], 0.0)
-                for m in range(i + 2, 8):
+                start = g if i + 2 < 8 else g + 1
+                for m in range(c + 2, PIVOTS):
                     a, b = over_rows(column[m][g], i), over_rows(column[m][g], i + 1)
                     first, second = k11 * a - k12 * b, k22 * b - k12 * a
-                    for q in range(g, groups):
+                    for q in range(start, groups):
                         column[m][q] = column[m][q] - (left[q] * first + right[q] * second)
                 for k in range(3):
                     a, b = over_rows(rows[k][g], i), over_rows(rows[k][g], i + 1)
                     first, second = k11 * a - k12 * b, k22 * b - k12 * a
-                    for q in range(g if i + 2 < 8 else g + 1, groups):
+                    for q in range(start, groups):
                         rows[k][q] = rows[k][q] - (left[q] * first + right[q] * second)
-            for k in range(3):
-                above = pltpu.roll(rows[k][g], 1, 0)
-                done[k][g] = (rows[k][g] - ratios * above) * scales
+                if i == 6:
+                    for k in range(3):
+                        above = pltpu.roll(rows[k][g], 1, 0)
+                        done[k][g] = (rows[k][g] - ratios[g] * above) * scales[g]
         factor = [jnp.concatenate(part, axis=0) for part in done]
         lanes = lax.broadcasted_iota(i32, (PANEL, 128), 1)
         inside = (lanes >= offset) & (lanes < offset + PANEL)
@@ -375,63 +379,80 @@
 WIDTH = 256
 
 
-def product(turned, flats, low, high):
+def product(turned, flats, low, high, basis, first, stored):
     half = RANK // 2
+    share = basis.shape[0] // PIECES
 
     def kernel(turned_ref, *refs):
-        flat_refs, (other, own) = refs[:-2], refs[-2:]
-        for start in range(low, high, WIDTH):
-            cells = jnp.concatenate([flat[:, start:start + WIDTH] for flat in flat_refs], axis=0)
-            sums = jnp.dot(turned_ref[...], cells, preferred_element_type=f32)
-            other[:, start - low:start - low + WIDTH] = sums[:half]
-            own[:, start - low:start - low + WIDTH] = sums[half:]
+        refs = list(refs)
+        flat_refs = [refs.pop(0) for _ in flats]
+        basis_ref = refs.pop(0)
+        other, own, out, sem = refs[-4:]
+        copy = pltpu.make_async_copy(
+            basis_ref.at[pl.ds(first, share)], out.at[pl.ds(first, share)], sem
+        )
+        copy.start()
+
+        @pl.when(lax.axis_index("yz") >= 0)
+        def compute():
+            for start in range(low, high, WIDTH):
+                cells = jnp.concatenate([flat[:, start:start + WIDTH] for flat in flat_refs], axis=0)
+                sums = jnp.dot(turned_ref[...], cells, preferred_element_type=f32)
+                other[:, start - low:start - low + WIDTH] = sums[:half]
+                own[:, start - low:start - low + WIDTH] = sums[half:]
+
+        copy.wait()
 
     shape = (half, high - low)
     depth = turned.shape[1]
-    return call(
-        kernel, [held(shape, f32), held(shape, f32)], [VMEM_SPACE] * (1 + len(flats)),
+    operands = [turned, *flats, basis]
+    in_specs = [VMEM_SPACE] * len(operands)
+    more = {}
+    if stored is not None:
+        more["input_output_aliases"] = {len(operands): 2}
+        operands.append(stored)
+        in_specs.append(ANY_SPACE)
+    return call(
+        kernel,
+        [held(shape, f32), held(shape, f32), pltpu.HBM(basis.shape, f32)], in_specs,
         flops=2 * RANK * depth * (high - low), moved=2 * depth * (high - low),
-    )(turned, *flats)
-
-
-def finish(own, came, y_local, z_local):
-    half = own[0].shape[0]
-    pieces = len(own)
-    cells = y_local // pieces
-    stride = y_local + 1
-    step = min(half, 32)
-
-    def kernel(*refs):
-        out, scratch, sems = refs[-3:]
-        rounded = scratch[1]
-        spread = scratch[0]
-        copies = []
-        for start in range(0, half, step):
-            for y_cell in range(y_local):
-                k, at = y_cell // cells, y_cell % cells * z_local
-                spread[pl.ds(start * stride + y_cell, step, stride=stride), :] = (
-                    refs[k][start:start + step, at:at + z_local]
-                    + refs[pieces + k][start:start + step, at:at + z_local]
-                )
-            for r in range(start, start + step):
-                rounded[r] = spread[r * stride:r * stride + y_local, :].astype(bf16)
-            copy = pltpu.make_async_copy(
-                rounded.at[pl.ds(start, step)], out.at[pl.ds(start, step)], sems.at[start // step]
+        out_specs=[VMEM_SPACE, VMEM_SPACE, HBM_SPACE],
+        scratch_shapes=[pltpu.SemaphoreType.DMA], **more,
+    )(*operands)
+
+
+def finish(own, came, first, y_local, z_local, stored):
+    half, columns = own.shape
+    cells = columns // z_local
+    stride = cells + 1
+
+    def kernel(own_ref, came_ref, *refs):
+        out, spread, rounded, sem = refs[-4:]
+        for k in range(cells):
+            at = k * z_local
+            spread[pl.ds(k, half, stride=stride), :] = (
+                own_ref[:, at:at + z_local] + came_ref[:, at:at + z_local]
             )
-            copy.start()
-            copies.append(copy)
-        for copy in copies:
-            copy.wait()
-
-    return call(
-        lambda *refs: kernel(*refs[:-3], (refs[-3], refs[-2]), refs[-1]),
-        jax.ShapeDtypeStruct((half, y_local, z_local), bf16), [VMEM_SPACE] * (2 * pieces),
-        out_specs=ANY_SPACE, moved=10 * half * y_local * z_local,
+        for r in range(half):
+            rounded[r] = spread[r * stride:r * stride + cells, :].astype(bf16)
+        copy = pltpu.make_async_copy(rounded, out.at[:, pl.ds(first, cells)], sem)
+        copy.start()
+        copy.wait()
+
+    operands, in_specs, more = [own, came], [VMEM_SPACE] * 2, {}
+    if stored is not None:
+        more["input_output_aliases"] = {2: 0}
+        operands.append(stored)
+        in_specs.append(ANY_SPACE)
+    return call(
+        kernel, pltpu.HBM((half, y_local, z_local), bf16), in_specs,
+        out_specs=HBM_SPACE, moved=10 * own.size,
         scratch_shapes=[
-            pltpu.VMEM((half * stride, z_local), f32), pltpu.VMEM((half, y_local, z_local), bf16),
-            pltpu.SemaphoreType.DMA((half // step,)),
+            pltpu.VMEM(((half + 1) * stride, z_local), f32), pltpu.VMEM((half, cells, z_local), bf16),
+            pltpu.SemaphoreType.DMA,
         ],
-    )(*own, *came)
+        **more,
+    )(*operands)
 
 
 def local(field, sketch_seeds):
@@ -484,15 +505,17 @@
     places = [wanted.index(((outer - k // inner) % outer, k % inner)) for k in range(count)]
     basis, turned = solve_rows(chunks, inverse, sizes, places)
     columns = y_local * z_local
-    own_parts, came_parts = [], []
+    stored, core, waiting = None, None, []
     for k in range(PIECES):
-        other, mine = product(
-            turned, flats, columns * k // PIECES, columns * (k + 1) // PIECES
+        other, mine, stored = product(
+            turned, flats, columns * k // PIECES, columns * (k + 1) // PIECES,
+            basis, x_local * k // PIECES, stored,
         )
-        came_parts.append(other_core(other))
-        own_parts.append(mine)
-    core = finish(own_parts, came_parts, y_local, z_local)
-    return (basis, core)
+        came = other_core(other)
+        waiting.append((mine, came))
+    for k, (mine, came) in enumerate(waiting):
+        core = finish(mine, came, y_local * k // PIECES, y_local, z_local, core)
+    return (stored, core)
 
 
 PIECES = 4

time: 68.6 us -> 67.7 us (0.987)
  waiting for transfers between devices: 20.1 us -> 17 us
  Pallas kernels: 21.9 us -> 23.6 us
  starting transfers between devices: 24.6 us -> 25.9 us
  local copies, waits for them, and re-layouts: 0.97 us -> 0 us
    pallas_call x5 -> x8, Pallas kernels: 3.89 us -> 6.14 us  [the longest x4 3.24 us: finish(): call(kernel, pltpu.HBM((half, y_local, z_local), bf16), in_specs, out_spe...]
    ppermute x5, waiting for transfers between devices: 3.69 us -> 1.53 us  [other_core(): return lax.ppermute(value, 'gx', [(0, 1), (1, 0)])]
    ppermute x7, starting transfers between devices: 9.2 us -> 11 us  [neighbour(): return lax.ppermute(value, 'yz', [(i, i ^ 1) for i in range(count)])]
    unnamed x1 -> x0, local copies, waits for them, and re-layouts: 0.97 us -> none
    ppermute x6, waiting for transfers between devices: 8.64 us -> 7.8 us  [shift(): return lax.ppermute(value, 'yz', pairs)]
  transfers between devices with their start and end apart: 18 -> 18, of which waited for: 11 -> 8; matrix products, arithmetic and copies ran while one was open for 1% -> 0% of each run, Pallas kernels for 8% -> 15%
where the time goes in v5:
time: 67.7 us; the launch traced here: 67.5 us
  starting transfers between devices  25.9 us (38%)
  Pallas kernels  23.6 us (35%)
  waiting for transfers between devices  17 us (25%)
  between operations  0.99 us (1%)
    ppermute x6, starting transfers between devices, shift(): return lax.ppermute(value, 'yz', pairs)  13.6 us
    ppermute x7, starting transfers between devices, neighbour(): return lax.ppermute(value, 'yz', [(i, i ^ 1) for i in range(count)])  11 us
    pallas_call x6, Pallas kernels, sketch_chunks(): call(kernel, out_shape, in_specs, flops=2 * total * y_local * z_local * R...  9.34 us
    ppermute x6, waiting for transfers between devices, shift(): return lax.ppermute(value, 'yz', pairs)  7.8 us
    ppermute x7, waiting for transfers between devices, neighbour(): return lax.ppermute(value, 'yz', [(i, i ^ 1) for i in range(count)])  7.67 us
    pallas_call x1, Pallas kernels, inverse_factor(): call(inverse_factor_kernel, held(gram.shape, f32), [VMEM_SPACE] * 2, flop...  5.93 us
    pallas_call x4, Pallas kernels, finish(): call(kernel, pltpu.HBM((half, y_local, z_local), bf16), in_specs, out_spe...  3.24 us
    pallas_call x4, Pallas kernels, product(): call(kernel, [held(shape, f32), held(shape, f32), pltpu.HBM(basis.shape,...  2.89 us
  transfers between devices with their start and end apart: 18, of which 8 were waited for; matrix products, arithmetic and copies ran while one was open for 0% of the time, Pallas kernels for 15%

profile of v5, /device:TPU:0, one launch (start us, length us, event | category | flops | bytes accessed | tf_op | source)
XLA Modules:
  0.0 67.5 jit_solution(13769388000585603401)
XLA Ops:
  0.6 2.2 %shard_map.41 = (f32[128,256]{1,0:T(8,128)S(1)}, bf16[128,4096]{1,0:T(8,128)(2,1)S(1)}, bf16[256,32,128]{2,1,0:T(8,128)(2,1)S(1)}, bf16[128,256]{1,0:T(8,128)(2,1)S(1)}, f32[32,256]{1,0:T(8,128)S(1)}) custom-call(bf16[1024,32,128]{2,1,0:T(8,128)(2,1)} %refs_0_.11, s32[6]{0:T(128)} %refs_1_.1), custom_call_target="tpu_custom_call" | custom-call | flops 268435456 | bytes 1048576 | tf_op jit(solution)/shard_map/pallas_call | solution.py:172
  2.8 1.7 %shard_map.42 = (f32[256,256]{1,0:T(8,128)S(1)}, bf16[256,4096]{1,0:T(8,128)(2,1)S(1)}, bf16[128,32,128]{2,1,0:T(8,128)(2,1)S(1)}) custom-call(bf16[1024,32,128]{2,1,0:T(8,128)(2,1)} %refs_0_.11, bf16[256,32,128]{2,1,0:T(8,128)(2,1)S(1)} %get-tuple-element.38.refs_1_, bf16[128,256]{1,0:T(8,128)(2,1)S(1)} %get-tuple-element.39.refs_2_, ...), custom_call_target="tpu_custom_call" | custom-call | flops 536870912 | bytes 2097152 | tf_op jit(solution)/shard_map/pallas_call | solution.py:172
  4.6 3.1 %collective-permute-start.2 = (f32[256,256]{1,0:T(8,128)S(1)}, f32[256,256]{1,0:T(8,128)S(1)}, u32[]{:S(2)}, u32[]{:S(2)}) collective-permute-start(f32[256,256]{1,0:T(8,128)S(1)} %get-tuple-element.48), channel_id=1, source_target_pairs={{0,2},{2,0},{4,6},{6,4},{8,10},{10,8},{12,14},{14,12},{1,3},{3,1},... | collective-permute-start | bytes 786440 | tf_op jit(solution)/shard_map/ppermute | solution.py:466
  7.7 1.2 %shard_map.43 = (f32[128,256]{1,0:T(8,128)S(1)}, bf16[128,4096]{1,0:T(8,128)(2,1)S(1)}, bf16[128,32,128]{2,1,0:T(8,128)(2,1)S(1)}) custom-call(bf16[1024,32,128]{2,1,0:T(8,128)(2,1)} %refs_0_.11, bf16[128,32,128]{2,1,0:T(8,128)(2,1)S(1)} %get-tuple-element.41.refs_1_, bf16[128,256]{1,0:T(8,128)(2,1)S(1)} %get-tuple-element.39.refs_2_, ...), custom_call_target="tpu_custom_call" | custom-call | flops 268435456 | bytes 1048576 | tf_op jit(solution)/shard_map/pallas_call | solution.py:172
  8.9 1.6 %shard_map.45 = (f32[128,256]{1,0:T(8,128)S(1)}, bf16[128,4096]{1,0:T(8,128)(2,1)S(1)}, bf16[256,32,128]{2,1,0:T(8,128)(2,1)S(1)}) custom-call(bf16[1024,32,128]{2,1,0:T(8,128)(2,1)} %refs_0_.11, bf16[128,32,128]{2,1,0:T(8,128)(2,1)S(1)} %get-tuple-element.44.refs_1_, bf16[128,256]{1,0:T(8,128)(2,1)S(1)} %get-tuple-element.39.refs_2_, ...), custom_call_target="tpu_custom_call" | custom-call | flops 268435456 | bytes 1048576 | tf_op jit(solution)/shard_map/pallas_call | solution.py:172
  10.5 2.0 %collective-permute-start.5 = (f32[128,256]{1,0:T(8,128)S(1)}, f32[128,256]{1,0:T(8,128)S(1)}, u32[]{:S(2)}, u32[]{:S(2)}) collective-permute-start(f32[128,256]{1,0:T(8,128)S(1)} %get-tuple-element.53), channel_id=1, source_target_pairs={{0,2},{2,0},{4,6},{6,4},{8,10},{10,8},{12,14},{14,12},{1,3},{3,1},... | collective-permute-start | bytes 393224 | tf_op jit(solution)/shard_map/ppermute | solution.py:466
  12.6 1.7 %shard_map.46 = (f32[128,256]{1,0:T(8,128)S(1)}, f32[128,256]{1,0:T(8,128)S(1)}, bf16[256,4096]{1,0:T(8,128)(2,1)S(1)}, bf16[128,32,128]{2,1,0:T(8,128)(2,1)S(1)}) custom-call(bf16[1024,32,128]{2,1,0:T(8,128)(2,1)} %refs_0_.11, bf16[256,32,128]{2,1,0:T(8,128)(2,1)S(1)} %get-tuple-element.45.refs_1_, bf16[128,256]{1,0:T(8,128)(2,1)S(1)} %get-tuple-element.39.refs_2_, ...), custom_call_target="tpu_custom_call" | custom-call | flops 536870912 | bytes 2097152 | tf_op jit(solution)/shard_map/pallas_call | solution.py:172
  14.3 3.3 %collective-permute-done.refs_1_ = f32[128,256]{1,0:T(8,128)S(1)} collective-permute-done((f32[128,256]{1,0:T(8,128)S(1)}, f32[128,256]{1,0:T(8,128)S(1)}, u32[]{:S(2)}, u32[]{:S(2)}) %collective-permute-start) | collective-permute-done | bytes 131104 | tf_op jit(solution)/shard_map/ppermute | solution.py:466
  17.6 3.2 %collective-permute-start.1 = (f32[128,256]{1,0:T(8,128)S(1)}, f32[128,256]{1,0:T(8,128)S(1)}, u32[]{:S(2)}, u32[]{:S(2)}) collective-permute-start(f32[128,256]{1,0:T(8,128)S(1)} %shard_map.44), channel_id=1, source_target_pairs={{0,8},{2,10},{4,12},{6,14},{8,0},{10,2},{12,4},{14,6},{1,9},{3,11}... | collective-permute-start | bytes 393224 | tf_op jit(solution)/shard_map/ppermute | solution.py:470
  20.8 1.6 %collective-permute-start.3 = (f32[128,256]{1,0:T(8,128)S(1)}, f32[128,256]{1,0:T(8,128)S(1)}, u32[]{:S(2)}, u32[]{:S(2)}) collective-permute-start(f32[128,256]{1,0:T(8,128)S(1)} %get-tuple-element.49), channel_id=1, source_target_pairs={{0,4},{2,6},{4,8},{6,10},{8,12},{10,14},{12,0},{14,2},{1,5},{3,7},... | collective-permute-start | bytes 393224 | tf_op jit(solution)/shard_map/ppermute | solution.py:470
  22.4 2.2 %collective-permute-start.4 = (f32[128,256]{1,0:T(8,128)S(1)}, f32[128,256]{1,0:T(8,128)S(1)}, u32[]{:S(2)}, u32[]{:S(2)}) collective-permute-start(f32[128,256]{1,0:T(8,128)S(1)} %get-tuple-element.50), channel_id=1, source_target_pairs={{0,12},{2,14},{4,0},{6,2},{8,4},{10,6},{12,8},{14,10},{1,13},{3,15... | collective-permute-start | bytes 393224 | tf_op jit(solution)/shard_map/ppermute | solution.py:470
  24.7 0.9 %shard_map.48 = (f32[128,256]{1,0:T(8,128)S(1)}, bf16[128,4096]{1,0:T(8,128)(2,1)S(1)}) custom-call(bf16[1024,32,128]{2,1,0:T(8,128)(2,1)} %refs_0_.11, bf16[128,32,128]{2,1,0:T(8,128)(2,1)S(1)} %get-tuple-element.51.refs_1_, bf16[128,256]{1,0:T(8,128)(2,1)S(1)} %get-tuple-element.39.refs_2_, f32[32,256]{1,0:T(8,128)S(1)} %get-tuple-element.40.refs_3_), custom_call_target="tpu_custom_call" | custom-call | flops 268435456 | bytes 1048576 | tf_op jit(solution)/shard_map/pallas_call | solution.py:172
  25.6 3.7 %collective-permute-done.1.refs_0_ = f32[128,256]{1,0:T(8,128)S(1)} collective-permute-done((f32[128,256]{1,0:T(8,128)S(1)}, f32[128,256]{1,0:T(8,128)S(1)}, u32[]{:S(2)}, u32[]{:S(2)}) %collective-permute-start.1) | collective-permute-done | bytes 131104 | tf_op jit(solution)/shard_map/ppermute | solution.py:470
  29.7 4.5 %collective-permute-start.9 = (f32[128,256]{1,0:T(8,128)S(1)}, f32[128,256]{1,0:T(8,128)S(1)}, u32[]{:S(2)}, u32[]{:S(2)}) collective-permute-start(f32[128,256]{1,0:T(8,128)S(1)} %shard_map.50.refs_0_), channel_id=1, source_target_pairs={{0,8},{2,10},{4,12},{6,14},{8,0},{10,2},{12,4},{14,6},{1,9},{3,11}... | collective-permute-start | bytes 393224 | tf_op jit(solution)/shard_map/ppermute | solution.py:470
  34.6 1.6 %collective-permute-start.7 = (f32[128,256]{1,0:T(8,128)S(1)}, f32[128,256]{1,0:T(8,128)S(1)}, u32[]{:S(2)}, u32[]{:S(2)}) collective-permute-start(f32[128,256]{1,0:T(8,128)S(1)} %shard_map.50.refs_0_), channel_id=1, source_target_pairs={{0,4},{2,6},{4,8},{6,10},{8,12},{10,14},{12,0},{14,2},{1,5},{3,7},... | collective-permute-start | bytes 393224 | tf_op jit(solution)/shard_map/ppermute | solution.py:470
  36.2 2.1 %collective-permute-start.6 = (f32[128,256]{1,0:T(8,128)S(1)}, f32[128,256]{1,0:T(8,128)S(1)}, u32[]{:S(2)}, u32[]{:S(2)}) collective-permute-start(f32[128,256]{1,0:T(8,128)S(1)} %shard_map.50.refs_0_), channel_id=1, source_target_pairs={{0,2},{2,0},{4,6},{6,4},{8,10},{10,8},{12,14},{14,12},{1,3},{3,1},... | collective-permute-start | bytes 393224 | tf_op jit(solution)/shard_map/ppermute | solution.py:466
  38.3 3.8 %collective-permute-done.9.refs_4_ = f32[128,256]{1,0:T(8,128)S(1)} collective-permute-done((f32[128,256]{1,0:T(8,128)S(1)}, f32[128,256]{1,0:T(8,128)S(1)}, u32[]{:S(2)}, u32[]{:S(2)}) %collective-permute-start.9) | collective-permute-done | bytes 131104 | tf_op jit(solution)/shard_map/ppermute | solution.py:470
  42.1 1.7 %collective-permute-start.10 = (f32[128,256]{1,0:T(8,128)S(1)}, f32[128,256]{1,0:T(8,128)S(1)}, u32[]{:S(2)}, u32[]{:S(2)}) collective-permute-start(f32[128,256]{1,0:T(8,128)S(1)} %collective-permute-done.9.refs_4_), channel_id=1, source_target_pairs={{0,2},{2,0},{4,6},{6,4},{8,10},{10,8},{12,14},{14,12},{1,3},{3,1},... | collective-permute-start | bytes 393224 | tf_op jit(solution)/shard_map/ppermute | solution.py:466
  44.1 1.7 %collective-permute-start.8 = (f32[128,256]{1,0:T(8,128)S(1)}, f32[128,256]{1,0:T(8,128)S(1)}, u32[]{:S(2)}, u32[]{:S(2)}) collective-permute-start(f32[128,256]{1,0:T(8,128)S(1)} %collective-permute-done.7.refs_2_), channel_id=1, source_target_pairs={{0,2},{2,0},{4,6},{6,4},{8,10},{10,8},{12,14},{14,12},{1,3},{3,1},... | collective-permute-start | bytes 393224 | tf_op jit(solution)/shard_map/ppermute | solution.py:466
  45.8 1.3 %collective-permute-done.10.refs_5_ = f32[128,256]{1,0:T(8,128)S(1)} collective-permute-done((f32[128,256]{1,0:T(8,128)S(1)}, f32[128,256]{1,0:T(8,128)S(1)}, u32[]{:S(2)}, u32[]{:S(2)}) %collective-permute-start.10) | collective-permute-done | bytes 131104 | tf_op jit(solution)/shard_map/ppermute | solution.py:466
  47.1 1.7 %collective-permute-done.12.refs_7_ = f32[128,256]{1,0:T(8,128)S(1)} collective-permute-done((f32[128,256]{1,0:T(8,128)S(1)}, f32[128,256]{1,0:T(8,128)S(1)}, u32[]{:S(2)}, u32[]{:S(2)}) %collective-permute-start.12) | collective-permute-done | bytes 131104 | tf_op jit(solution)/shard_map/ppermute | solution.py:466
  48.7 1.4 %collective-permute-done.8.refs_3_ = f32[128,256]{1,0:T(8,128)S(1)} collective-permute-done((f32[128,256]{1,0:T(8,128)S(1)}, f32[128,256]{1,0:T(8,128)S(1)}, u32[]{:S(2)}, u32[]{:S(2)}) %collective-permute-start.8) | collective-permute-done | bytes 131104 | tf_op jit(solution)/shard_map/ppermute | solution.py:466
  50.1 0.8 %shard_map.51.gram = f32[256,256]{1,0:T(8,128)S(1)} custom-call(f32[128,256]{1,0:T(8,128)S(1)} %shard_map.50.refs_0_, f32[128,256]{1,0:T(8,128)S(1)} %collective-permute-done.6.refs_1_, f32[128,256]{1,0:T(8,128)S(1)} %collective-permute-done.7.refs_2_, f32[128,256]{1,0:T(8,128)S(1)} %collective-permute-done.8.refs_3_, ...), custom_call_target="tpu_custom_call" | custom-call | flops 536870912 | bytes 1048576 | tf_op jit(solution)/shard_map/pallas_call | solution.py:333
  51.0 1.5 %collective-permute-done.13.came = f32[256,256]{1,0:T(8,128)S(1)} collective-permute-done((f32[256,256]{1,0:T(8,128)S(1)}, f32[256,256]{1,0:T(8,128)S(1)}, u32[]{:S(2)}, u32[]{:S(2)}) %collective-permute-start.13) | collective-permute-done | bytes 262176 | tf_op jit(solution)/shard_map/ppermute | solution.py:473
  52.6 5.9 %shard_map.52.inverse_ref = f32[256,256]{1,0:T(8,128)S(1)} custom-call(f32[256,256]{1,0:T(8,128)S(1)} %shard_map.51.gram, f32[256,256]{1,0:T(8,128)S(1)} %collective-permute-done.13.came), custom_call_target="tpu_custom_call" | custom-call | flops 50331648 | bytes 524288 | tf_op jit(solution)/shard_map/pallas_call | solution.py:281
  58.5 1.3 %shard_map.53 = (f32[1024,256]{1,0:T(8,128)S(1)}, bf16[256,1024]{1,0:T(8,128)(2,1)S(1)}) custom-call(f32[256,256]{1,0:T(8,128)S(1)} %shard_map.52.inverse_ref, f32[128,256]{1,0:T(8,128)S(1)} %shard_map.50.refs_0_, f32[128,256]{1,0:T(8,128)S(1)} %collective-permute-done.6.refs_1_, f32[128,256]{1,0:T(8,128)S(1)} %collective-permute-done.7.refs_2_, ...), custom_call_target="tpu_custom_call" | custom-call | flops 402653184 | bytes 2097152 | tf_op jit(solution)/shard_map/pallas_call | solution.py:371
  59.8 0.7 %shard_map.54 = (f32[128,1024]{1,0:T(8,128)S(1)}, f32[128,1024]{1,0:T(8,128)S(1)}, f32[1024,256]{1,0:T(8,128)}) custom-call(bf16[256,1024]{1,0:T(8,128)(2,1)S(1)} %get-tuple-element.54.turned_ref, bf16[128,4096]{1,0:T(8,128)(2,1)S(1)} %get-tuple-element.55.refs_0_, bf16[256,4096]{1,0:T(8,128)(2,1)S(1)} %get-tuple-element.56.refs_1_, ...), custom_call_target="tpu_custom_call" | custom-call | flops 536870912 | bytes 2097152 | tf_op jit(solution)/shard_map/pallas_call | solution.py:415
  61.9 0.7 %shard_map.56 = (f32[128,1024]{1,0:T(8,128)S(1)}, f32[128,1024]{1,0:T(8,128)S(1)}, f32[1024,256]{1,0:T(8,128)}) custom-call(bf16[256,1024]{1,0:T(8,128)(2,1)S(1)} %get-tuple-element.54.turned_ref, bf16[128,4096]{1,0:T(8,128)(2,1)S(1)} %get-tuple-element.55.refs_0_, bf16[256,4096]{1,0:T(8,128)(2,1)S(1)} %get-tuple-element.56.refs_1_, ...), custom_call_target="tpu_custom_call", output_to_operand_aliasing={{2}: (8, {})} | custom-call | flops 536870912 | bytes 2097152 | tf_op jit(solution)/shard_map/pallas_call | solution.py:415
  64.0 0.8 %shard_map.58.refs_0_ = bf16[128,32,128]{2,1,0:T(8,128)(2,1)} custom-call(f32[128,1024]{1,0:T(8,128)S(1)} %get-tuple-element.72.own_ref, f32[128,1024]{1,0:T(8,128)S(1)} %collective-permute-done.17.came_ref), custom_call_target="tpu_custom_call" | custom-call | bytes 1310720 | tf_op jit(solution)/shard_map/pallas_call | solution.py:447
  64.8 0.8 %shard_map.59.refs_0_ = bf16[128,32,128]{2,1,0:T(8,128)(2,1)} custom-call(f32[128,1024]{1,0:T(8,128)S(1)} %get-tuple-element.70.own_ref, f32[128,1024]{1,0:T(8,128)S(1)} %collective-permute-done.16.came_ref, bf16[128,32,128]{2,1,0:T(8,128)(2,1)} %shard_map.58.refs_0_), custom_call_target="tpu_custom_call", output_to_operand_aliasing={{}: (2, {})} | custom-call | bytes 1310720 | tf_op jit(solution)/shard_map/pallas_call | solution.py:447
  65.7 0.8 %shard_map.60.refs_0_ = bf16[128,32,128]{2,1,0:T(8,128)(2,1)} custom-call(f32[128,1024]{1,0:T(8,128)S(1)} %get-tuple-element.68.own_ref, f32[128,1024]{1,0:T(8,128)S(1)} %collective-permute-done.15.came_ref, bf16[128,32,128]{2,1,0:T(8,128)(2,1)} %shard_map.59.refs_0_), custom_call_target="tpu_custom_call", output_to_operand_aliasing={{}: (2, {})} | custom-call | bytes 1310720 | tf_op jit(solution)/shard_map/pallas_call | solution.py:447
  66.5 0.8 %shard_map.61 = bf16[128,32,128]{2,1,0:T(8,128)(2,1)} custom-call(f32[128,1024]{1,0:T(8,128)S(1)} %get-tuple-element.66.own_ref, f32[128,1024]{1,0:T(8,128)S(1)} %collective-permute-done.14.came_ref, bf16[128,32,128]{2,1,0:T(8,128)(2,1)} %shard_map.60.refs_0_), custom_call_target="tpu_custom_call", output_to_operand_aliasing={{}: (2, {})} | custom-call | bytes 1310720 | tf_op jit(solution)/shard_map/pallas_call | solution.py:447
  (25 shorter events, 4.1 us)
Async XLA Ops:
  4.6 16.2 %collective-permute-start.2 = (f32[256,256]{1,0:T(8,128)S(1)}, f32[256,256]{1,0:T(8,128)S(1)}, u32[]{:S(2)}, u32[]{:S(2)}) collective-permute-start(f32[256,256]{1,0:T(8,128)S(1)} %get-tuple-element.48), channel_id=1, source_target_pairs={{0,2},{2,0},{4,6},{6,4},{8,10},{10,8},{12,14},{14,12},{1,3},{3,1},... | collective-permute-start | bytes 786440 | tf_op jit(solution)/shard_map/ppermute | solution.py:466
  7.6 10.0 %collective-permute-start = (f32[128,256]{1,0:T(8,128)S(1)}, f32[128,256]{1,0:T(8,128)S(1)}, u32[]{:S(2)}, u32[]{:S(2)}) collective-permute-start(f32[128,256]{1,0:T(8,128)S(1)} %get-tuple-element.43), channel_id=1, source_target_pairs={{0,2},{2,0},{4,6},{6,4},{8,10},{10,8},{12,14},{14,12},{1,3},{3,1},... | collective-permute-start | bytes 393224 | tf_op jit(solution)/shard_map/ppermute | solution.py:466
  10.5 15.0 %collective-permute-start.5 = (f32[128,256]{1,0:T(8,128)S(1)}, f32[128,256]{1,0:T(8,128)S(1)}, u32[]{:S(2)}, u32[]{:S(2)}) collective-permute-start(f32[128,256]{1,0:T(8,128)S(1)} %get-tuple-element.53), channel_id=1, source_target_pairs={{0,2},{2,0},{4,6},{6,4},{8,10},{10,8},{12,14},{14,12},{1,3},{3,1},... | collective-permute-start | bytes 393224 | tf_op jit(solution)/shard_map/ppermute | solution.py:466
  17.6 11.7 %collective-permute-start.1 = (f32[128,256]{1,0:T(8,128)S(1)}, f32[128,256]{1,0:T(8,128)S(1)}, u32[]{:S(2)}, u32[]{:S(2)}) collective-permute-start(f32[128,256]{1,0:T(8,128)S(1)} %shard_map.44), channel_id=1, source_target_pairs={{0,8},{2,10},{4,12},{6,14},{8,0},{10,2},{12,4},{14,6},{1,9},{3,11}... | collective-permute-start | bytes 393224 | tf_op jit(solution)/shard_map/ppermute | solution.py:470
  20.8 8.5 %collective-permute-start.3 = (f32[128,256]{1,0:T(8,128)S(1)}, f32[128,256]{1,0:T(8,128)S(1)}, u32[]{:S(2)}, u32[]{:S(2)}) collective-permute-start(f32[128,256]{1,0:T(8,128)S(1)} %get-tuple-element.49), channel_id=1, source_target_pairs={{0,4},{2,6},{4,8},{6,10},{8,12},{10,14},{12,0},{14,2},{1,5},{3,7},... | collective-permute-start | bytes 393224 | tf_op jit(solution)/shard_map/ppermute | solution.py:470
  22.4 7.2 %collective-permute-start.4 = (f32[128,256]{1,0:T(8,128)S(1)}, f32[128,256]{1,0:T(8,128)S(1)}, u32[]{:S(2)}, u32[]{:S(2)}) collective-permute-start(f32[128,256]{1,0:T(8,128)S(1)} %get-tuple-element.50), channel_id=1, source_target_pairs={{0,12},{2,14},{4,0},{6,2},{8,4},{10,6},{12,8},{14,10},{1,13},{3,15... | collective-permute-start | bytes 393224 | tf_op jit(solution)/shard_map/ppermute | solution.py:470
  29.7 12.4 %collective-permute-start.9 = (f32[128,256]{1,0:T(8,128)S(1)}, f32[128,256]{1,0:T(8,128)S(1)}, u32[]{:S(2)}, u32[]{:S(2)}) collective-permute-start(f32[128,256]{1,0:T(8,128)S(1)} %shard_map.50.refs_0_), channel_id=1, source_target_pairs={{0,8},{2,10},{4,12},{6,14},{8,0},{10,2},{12,4},{14,6},{1,9},{3,11}... | collective-permute-start | bytes 393224 | tf_op jit(solution)/shard_map/ppermute | solution.py:470
  34.2 9.6 %collective-permute-start.11 = (f32[128,256]{1,0:T(8,128)S(1)}, f32[128,256]{1,0:T(8,128)S(1)}, u32[]{:S(2)}, u32[]{:S(2)}) collective-permute-start(f32[128,256]{1,0:T(8,128)S(1)} %shard_map.50.refs_0_), channel_id=1, source_target_pairs={{0,12},{2,14},{4,0},{6,2},{8,4},{10,6},{12,8},{14,10},{1,13},{3,15... | collective-permute-start | bytes 393224 | tf_op jit(solution)/shard_map/ppermute | solution.py:470
  34.6 9.5 %collective-permute-start.7 = (f32[128,256]{1,0:T(8,128)S(1)}, f32[128,256]{1,0:T(8,128)S(1)}, u32[]{:S(2)}, u32[]{:S(2)}) collective-permute-start(f32[128,256]{1,0:T(8,128)S(1)} %shard_map.50.refs_0_), channel_id=1, source_target_pairs={{0,4},{2,6},{4,8},{6,10},{8,12},{10,14},{12,0},{14,2},{1,5},{3,7},... | collective-permute-start | bytes 393224 | tf_op jit(solution)/shard_map/ppermute | solution.py:470
  36.2 9.6 %collective-permute-start.6 = (f32[128,256]{1,0:T(8,128)S(1)}, f32[128,256]{1,0:T(8,128)S(1)}, u32[]{:S(2)}, u32[]{:S(2)}) collective-permute-start(f32[128,256]{1,0:T(8,128)S(1)} %shard_map.50.refs_0_), channel_id=1, source_target_pairs={{0,2},{2,0},{4,6},{6,4},{8,10},{10,8},{12,14},{14,12},{1,3},{3,1},... | collective-permute-start | bytes 393224 | tf_op jit(solution)/shard_map/ppermute | solution.py:466
  42.1 5.0 %collective-permute-start.10 = (f32[128,256]{1,0:T(8,128)S(1)}, f32[128,256]{1,0:T(8,128)S(1)}, u32[]{:S(2)}, u32[]{:S(2)}) collective-permute-start(f32[128,256]{1,0:T(8,128)S(1)} %collective-permute-done.9.refs_4_), channel_id=1, source_target_pairs={{0,2},{2,0},{4,6},{6,4},{8,10},{10,8},{12,14},{14,12},{1,3},{3,1},... | collective-permute-start | bytes 393224 | tf_op jit(solution)/shard_map/ppermute | solution.py:466
  43.8 5.0 %collective-permute-start.12 = (f32[128,256]{1,0:T(8,128)S(1)}, f32[128,256]{1,0:T(8,128)S(1)}, u32[]{:S(2)}, u32[]{:S(2)}) collective-permute-start(f32[128,256]{1,0:T(8,128)S(1)} %collective-permute-done.11.refs_6_), channel_id=1, source_target_pairs={{0,2},{2,0},{4,6},{6,4},{8,10},{10,8},{12,14},{14,12},{1,3},{3,1},... | collective-permute-start | bytes 393224 | tf_op jit(solution)/shard_map/ppermute | solution.py:466
  44.1 6.0 %collective-permute-start.8 = (f32[128,256]{1,0:T(8,128)S(1)}, f32[128,256]{1,0:T(8,128)S(1)}, u32[]{:S(2)}, u32[]{:S(2)}) collective-permute-start(f32[128,256]{1,0:T(8,128)S(1)} %collective-permute-done.7.refs_2_), channel_id=1, source_target_pairs={{0,2},{2,0},{4,6},{6,4},{8,10},{10,8},{12,14},{14,12},{1,3},{3,1},... | collective-permute-start | bytes 393224 | tf_op jit(solution)/shard_map/ppermute | solution.py:466
  51.0 1.6 %collective-permute-start.13 = (f32[256,256]{1,0:T(8,128)S(1)}, f32[256,256]{1,0:T(8,128)S(1)}, u32[]{:S(2)}, u32[]{:S(2)}) collective-permute-start(f32[256,256]{1,0:T(8,128)S(1)} %shard_map.51.gram), channel_id=1, source_target_pairs={{0,1},{1,0},{2,3},{3,2},{4,5},{5,4},{6,7},{7,6},{8,9},{9,8},{10,11... | collective-permute-start | bytes 786440 | tf_op jit(solution)/shard_map/ppermute | solution.py:473
  60.6 3.5 %collective-permute-start.17 = (f32[128,1024]{1,0:T(8,128)S(1)}, f32[128,1024]{1,0:T(8,128)S(1)}, u32[]{:S(2)}, u32[]{:S(2)}) collective-permute-start(f32[128,1024]{1,0:T(8,128)S(1)} %get-tuple-element.73), channel_id=1, source_target_pairs={{0,1},{1,0},{2,3},{3,2},{4,5},{5,4},{6,7},{7,6},{8,9},{9,8},{10,11... | collective-permute-start | bytes 1572872 | tf_op jit(solution)/shard_map/ppermute | solution.py:473
  61.5 3.4 %collective-permute-start.16 = (f32[128,1024]{1,0:T(8,128)S(1)}, f32[128,1024]{1,0:T(8,128)S(1)}, u32[]{:S(2)}, u32[]{:S(2)}) collective-permute-start(f32[128,1024]{1,0:T(8,128)S(1)} %get-tuple-element.71), channel_id=1, source_target_pairs={{0,1},{1,0},{2,3},{3,2},{4,5},{5,4},{6,7},{7,6},{8,9},{9,8},{10,11... | collective-permute-start | bytes 1572872 | tf_op jit(solution)/shard_map/ppermute | solution.py:473
  62.6 3.0 %collective-permute-start.15 = (f32[128,1024]{1,0:T(8,128)S(1)}, f32[128,1024]{1,0:T(8,128)S(1)}, u32[]{:S(2)}, u32[]{:S(2)}) collective-permute-start(f32[128,1024]{1,0:T(8,128)S(1)} %get-tuple-element.69), channel_id=1, source_target_pairs={{0,1},{1,0},{2,3},{3,2},{4,5},{5,4},{6,7},{7,6},{8,9},{9,8},{10,11... | collective-permute-start | bytes 1572872 | tf_op jit(solution)/shard_map/ppermute | solution.py:473
  63.6 2.9 %collective-permute-start.14 = (f32[128,1024]{1,0:T(8,128)S(1)}, f32[128,1024]{1,0:T(8,128)S(1)}, u32[]{:S(2)}, u32[]{:S(2)}) collective-permute-start(f32[128,1024]{1,0:T(8,128)S(1)} %get-tuple-element.67), channel_id=1, source_target_pairs={{0,1},{1,0},{2,3},{3,2},{4,5},{5,4},{6,7},{7,6},{8,9},{9,8},{10,11... | collective-permute-start | bytes 1572872 | tf_op jit(solution)/shard_map/ppermute | solution.py:473

commit v6 on v5

--- a/solution.py
+++ b/solution.py
@@ -312,12 +312,12 @@
     )(*parts)
 
 
-def gram_of(chunks):
+def gram_of(chunks, base=None):
     chunk = chunks[0].shape[0]
     total = len(chunks) * chunk
 
     def kernel(*refs):
-        rows_refs, (out, terms) = refs[:-2], refs[-2:]
+        rows_refs, (out, terms) = refs[:len(chunks)], refs[-2:]
         for k, ref in enumerate(rows_refs):
             for j, term in enumerate(split3(ref[...])):
                 terms[k * chunk:(k + 1) * chunk, j * RANK:(j + 1) * RANK] = term
@@ -328,13 +328,15 @@
         middle = terms[:, RANK:2 * RANK]
         second = lax.dot_general(middle, middle, over_rows, preferred_element_type=f32)
         mixed = first[:, RANK:2 * RANK] + first[:, 2 * RANK:]
-        out[...] = first[:, :RANK] + (second + (mixed + mixed.T))
-
-    return call(
-        kernel, held((RANK, RANK), f32), [VMEM_SPACE] * len(chunks),
+        sums = first[:, :RANK] + (second + (mixed + mixed.T))
+        out[...] = sums if base is None else refs[len(chunks)][...] + sums
+
+    operands = list(chunks) + ([] if base is None else [base])
+    return call(
+        kernel, held((RANK, RANK), f32), [VMEM_SPACE] * len(operands),
         flops=8 * total * RANK ** 2, moved=4 * total * RANK,
         scratch_shapes=[pltpu.VMEM((total, 3 * RANK), bf16)],
-    )(*chunks)
+    )(*operands)
 
 
 def split2(value):
@@ -421,38 +423,42 @@
     )(*operands)
 
 
-def finish(own, came, first, y_local, z_local, stored):
-    half, columns = own.shape
-    cells = columns // z_local
-    stride = cells + 1
-
-    def kernel(own_ref, came_ref, *refs):
-        out, spread, rounded, sem = refs[-4:]
-        for k in range(cells):
-            at = k * z_local
-            spread[pl.ds(k, half, stride=stride), :] = (
-                own_ref[:, at:at + z_local] + came_ref[:, at:at + z_local]
+def finish(own, came, y_local, z_local):
+    half = own[0].shape[0]
+    pieces = len(own)
+    cells = y_local // pieces
+    stride = y_local + 1
+    step = min(half, 32)
+
+    def kernel(*refs):
+        out, spread, rounded, sems = refs[-4:]
+        copies = []
+        for start in range(0, half, step):
+            for y_cell in range(y_local):
+                k, at = y_cell // cells, y_cell % cells * z_local
+                spread[pl.ds(start * stride + y_cell, step, stride=stride), :] = (
+                    refs[k][start:start + step, at:at + z_local]
+                    + refs[pieces + k][start:start + step, at:at + z_local]
+                )
+            for r in range(start, start + step):
+                rounded[r] = spread[r * stride:r * stride + y_local, :].astype(bf16)
+            copy = pltpu.make_async_copy(
+                rounded.at[pl.ds(start, step)], out.at[pl.ds(start, step)], sems.at[start // step]
             )
-        for r in range(half):
-            rounded[r] = spread[r * stride:r * stride + cells, :].astype(bf16)
-        copy = pltpu.make_async_copy(rounded, out.at[:, pl.ds(first, cells)], sem)
-        copy.start()
-        copy.wait()
-
-    operands, in_specs, more = [own, came], [VMEM_SPACE] * 2, {}
-    if stored is not None:
-        more["input_output_aliases"] = {2: 0}
-        operands.append(stored)
-        in_specs.append(ANY_SPACE)
-    return call(
-        kernel, pltpu.HBM((half, y_local, z_local), bf16), in_specs,
-        out_specs=HBM_SPACE, moved=10 * own.size,
+            copy.start()
+            copies.append(copy)
+        for copy in copies:
+            copy.wait()
+
+    return call(
+        kernel, pltpu.HBM((half, y_local, z_local), bf16), [VMEM_SPACE] * (2 * pieces),
+        out_specs=HBM_SPACE, moved=10 * half * y_local * z_local,
         scratch_shapes=[
-            pltpu.VMEM(((half + 1) * stride, z_local), f32), pltpu.VMEM((half, cells, z_local), bf16),
-            pltpu.SemaphoreType.DMA,
+            pltpu.VMEM(((half + 1) * stride, z_local), f32),
+            pltpu.VMEM((half, y_local, z_local), bf16),
+            pltpu.SemaphoreType.DMA((half // step,)),
         ],
-        **more,
-    )(*operands)
+    )(*own, *came)
 
 
 def local(field, sketch_seeds):
@@ -499,26 +505,32 @@
         chunks[d * inner] = came
         if inner == 2:
             chunks[d * inner + 1] = neighbour(came)
-    gram = gram_of(chunks)
+    late = [d * inner + 1 for d in near[-2:]] if early_gram(inner, outer) else []
+    gram = None
+    if late:
+        gram = gram_of([chunks[k] for k in range(count) if k not in late])
+    gram = gram_of([chunks[k] for k in late or range(count)], gram)
     came = other_core(gram)
     inverse = inverse_factor(gram, came)
     places = [wanted.index(((outer - k // inner) % outer, k % inner)) for k in range(count)]
     basis, turned = solve_rows(chunks, inverse, sizes, places)
     columns = y_local * z_local
-    stored, core, waiting = None, None, []
+    stored, mine, came = None, [], []
     for k in range(PIECES):
-        other, mine, stored = product(
+        other, own_part, stored = product(
             turned, flats, columns * k // PIECES, columns * (k + 1) // PIECES,
             basis, x_local * k // PIECES, stored,
         )
-        came = other_core(other)
-        waiting.append((mine, came))
-    for k, (mine, came) in enumerate(waiting):
-        core = finish(mine, came, y_local * k // PIECES, y_local, z_local, core)
-    return (stored, core)
+        came.append(other_core(other))
+        mine.append(own_part)
+    return (stored, finish(mine, came, y_local, z_local))
 
 
 PIECES = 4
+
+
+def early_gram(inner, outer):
+    return inner == 2 and outer > 2
 
 
 def turns_of(groups, inner):

time: 67.7 us -> 65.6 us (0.969)
  Pallas kernels: 23.6 us -> 21.7 us
    ppermute x5, waiting for transfers between devices: 1.53 us -> 3.67 us  [other_core(): return lax.ppermute(value, 'gx', [(0, 1), (1, 0)])]
    pallas_call x5 -> x3, Pallas kernels: 4.06 us -> 2.14 us  [the longest x1 1.07 us: finish(): call(kernel, pltpu.HBM((half, y_local, z_local), bf16), [VMEM_SPACE] * (2...]
    ppermute x6, waiting for transfers between devices: 7.8 us -> 6.31 us  [shift(): return lax.ppermute(value, 'yz', pairs)]
  transfers between devices with their start and end apart: 18 -> 18, of which waited for: 8 -> 11; matrix products, arithmetic and copies ran while one was open for 0% -> 0% of each run, Pallas kernels for 15% -> 13%
where the time goes in v6:
time: 65.6 us; the launch traced here: 65.1 us
  starting transfers between devices  25.4 us (39%)
  Pallas kernels  21.7 us (33%)
  waiting for transfers between devices  17.1 us (26%)
  between operations  0.95 us (1%)
    ppermute x6, starting transfers between devices, shift(): return lax.ppermute(value, 'yz', pairs)  13.7 us
    ppermute x7, starting transfers between devices, neighbour(): return lax.ppermute(value, 'yz', [(i, i ^ 1) for i in range(count)])  10.4 us
    pallas_call x6, Pallas kernels, sketch_chunks(): call(kernel, out_shape, in_specs, flops=2 * total * y_local * z_local * R...  9.34 us
    ppermute x7, waiting for transfers between devices, neighbour(): return lax.ppermute(value, 'yz', [(i, i ^ 1) for i in range(count)])  7.1 us
    ppermute x6, waiting for transfers between devices, shift(): return lax.ppermute(value, 'yz', pairs)  6.31 us
    pallas_call x1, Pallas kernels, inverse_factor(): call(inverse_factor_kernel, held(gram.shape, f32), [VMEM_SPACE] * 2, flop...  5.93 us
    ppermute x5, waiting for transfers between devices, other_core(): return lax.ppermute(value, 'gx', [(0, 1), (1, 0)])  3.67 us
    pallas_call x4, Pallas kernels, product(): call(kernel, [held(shape, f32), held(shape, f32), pltpu.HBM(basis.shape,...  2.91 us
  transfers between devices with their start and end apart: 18, of which 11 were waited for; matrix products, arithmetic and copies ran while one was open for 0% of the time, Pallas kernels for 13%

profile of v6, /device:TPU:0, one launch (start us, length us, event | category | flops | bytes accessed | tf_op | source)
XLA Modules:
  0.0 65.1 jit_solution(15243387450666434192)
XLA Ops:
  0.6 2.2 %shard_map.41 = (f32[128,256]{1,0:T(8,128)S(1)}, bf16[128,4096]{1,0:T(8,128)(2,1)S(1)}, bf16[256,32,128]{2,1,0:T(8,128)(2,1)S(1)}, bf16[128,256]{1,0:T(8,128)(2,1)S(1)}, f32[32,256]{1,0:T(8,128)S(1)}) custom-call(bf16[1024,32,128]{2,1,0:T(8,128)(2,1)} %refs_0_.11, s32[6]{0:T(128)} %refs_1_.1), custom_call_target="tpu_custom_call" | custom-call | flops 268435456 | bytes 1048576 | tf_op jit(solution)/shard_map/pallas_call | solution.py:172
  2.8 1.7 %shard_map.42 = (f32[256,256]{1,0:T(8,128)S(1)}, bf16[256,4096]{1,0:T(8,128)(2,1)S(1)}, bf16[128,32,128]{2,1,0:T(8,128)(2,1)S(1)}) custom-call(bf16[1024,32,128]{2,1,0:T(8,128)(2,1)} %refs_0_.11, bf16[256,32,128]{2,1,0:T(8,128)(2,1)S(1)} %get-tuple-element.38.refs_1_, bf16[128,256]{1,0:T(8,128)(2,1)S(1)} %get-tuple-element.39.refs_2_, ...), custom_call_target="tpu_custom_call" | custom-call | flops 536870912 | bytes 2097152 | tf_op jit(solution)/shard_map/pallas_call | solution.py:172
  4.6 3.1 %collective-permute-start.2 = (f32[256,256]{1,0:T(8,128)S(1)}, f32[256,256]{1,0:T(8,128)S(1)}, u32[]{:S(2)}, u32[]{:S(2)}) collective-permute-start(f32[256,256]{1,0:T(8,128)S(1)} %get-tuple-element.48), channel_id=1, source_target_pairs={{0,2},{2,0},{4,6},{6,4},{8,10},{10,8},{12,14},{14,12},{1,3},{3,1},... | collective-permute-start | bytes 786440 | tf_op jit(solution)/shard_map/ppermute | solution.py:472
  7.7 1.2 %shard_map.43 = (f32[128,256]{1,0:T(8,128)S(1)}, bf16[128,4096]{1,0:T(8,128)(2,1)S(1)}, bf16[128,32,128]{2,1,0:T(8,128)(2,1)S(1)}) custom-call(bf16[1024,32,128]{2,1,0:T(8,128)(2,1)} %refs_0_.11, bf16[128,32,128]{2,1,0:T(8,128)(2,1)S(1)} %get-tuple-element.41.refs_1_, bf16[128,256]{1,0:T(8,128)(2,1)S(1)} %get-tuple-element.39.refs_2_, ...), custom_call_target="tpu_custom_call" | custom-call | flops 268435456 | bytes 1048576 | tf_op jit(solution)/shard_map/pallas_call | solution.py:172
  8.9 1.6 %shard_map.45 = (f32[128,256]{1,0:T(8,128)S(1)}, bf16[128,4096]{1,0:T(8,128)(2,1)S(1)}, bf16[256,32,128]{2,1,0:T(8,128)(2,1)S(1)}) custom-call(bf16[1024,32,128]{2,1,0:T(8,128)(2,1)} %refs_0_.11, bf16[128,32,128]{2,1,0:T(8,128)(2,1)S(1)} %get-tuple-element.44.refs_1_, bf16[128,256]{1,0:T(8,128)(2,1)S(1)} %get-tuple-element.39.refs_2_, ...), custom_call_target="tpu_custom_call" | custom-call | flops 268435456 | bytes 1048576 | tf_op jit(solution)/shard_map/pallas_call | solution.py:172
  10.5 2.0 %collective-permute-start.5 = (f32[128,256]{1,0:T(8,128)S(1)}, f32[128,256]{1,0:T(8,128)S(1)}, u32[]{:S(2)}, u32[]{:S(2)}) collective-permute-start(f32[128,256]{1,0:T(8,128)S(1)} %get-tuple-element.53), channel_id=1, source_target_pairs={{0,2},{2,0},{4,6},{6,4},{8,10},{10,8},{12,14},{14,12},{1,3},{3,1},... | collective-permute-start | bytes 393224 | tf_op jit(solution)/shard_map/ppermute | solution.py:472
  12.6 1.7 %shard_map.46 = (f32[128,256]{1,0:T(8,128)S(1)}, f32[128,256]{1,0:T(8,128)S(1)}, bf16[256,4096]{1,0:T(8,128)(2,1)S(1)}, bf16[128,32,128]{2,1,0:T(8,128)(2,1)S(1)}) custom-call(bf16[1024,32,128]{2,1,0:T(8,128)(2,1)} %refs_0_.11, bf16[256,32,128]{2,1,0:T(8,128)(2,1)S(1)} %get-tuple-element.45.refs_1_, bf16[128,256]{1,0:T(8,128)(2,1)S(1)} %get-tuple-element.39.refs_2_, ...), custom_call_target="tpu_custom_call" | custom-call | flops 536870912 | bytes 2097152 | tf_op jit(solution)/shard_map/pallas_call | solution.py:172
  14.3 3.3 %collective-permute-done.refs_1_ = f32[128,256]{1,0:T(8,128)S(1)} collective-permute-done((f32[128,256]{1,0:T(8,128)S(1)}, f32[128,256]{1,0:T(8,128)S(1)}, u32[]{:S(2)}, u32[]{:S(2)}) %collective-permute-start) | collective-permute-done | bytes 131104 | tf_op jit(solution)/shard_map/ppermute | solution.py:472
  17.6 3.2 %collective-permute-start.1 = (f32[128,256]{1,0:T(8,128)S(1)}, f32[128,256]{1,0:T(8,128)S(1)}, u32[]{:S(2)}, u32[]{:S(2)}) collective-permute-start(f32[128,256]{1,0:T(8,128)S(1)} %shard_map.44), channel_id=1, source_target_pairs={{0,8},{2,10},{4,12},{6,14},{8,0},{10,2},{12,4},{14,6},{1,9},{3,11}... | collective-permute-start | bytes 393224 | tf_op jit(solution)/shard_map/ppermute | solution.py:476
  20.8 1.6 %collective-permute-start.3 = (f32[128,256]{1,0:T(8,128)S(1)}, f32[128,256]{1,0:T(8,128)S(1)}, u32[]{:S(2)}, u32[]{:S(2)}) collective-permute-start(f32[128,256]{1,0:T(8,128)S(1)} %get-tuple-element.49), channel_id=1, source_target_pairs={{0,4},{2,6},{4,8},{6,10},{8,12},{10,14},{12,0},{14,2},{1,5},{3,7},... | collective-permute-start | bytes 393224 | tf_op jit(solution)/shard_map/ppermute | solution.py:476
  22.4 2.2 %collective-permute-start.4 = (f32[128,256]{1,0:T(8,128)S(1)}, f32[128,256]{1,0:T(8,128)S(1)}, u32[]{:S(2)}, u32[]{:S(2)}) collective-permute-start(f32[128,256]{1,0:T(8,128)S(1)} %get-tuple-element.50), channel_id=1, source_target_pairs={{0,12},{2,14},{4,0},{6,2},{8,4},{10,6},{12,8},{14,10},{1,13},{3,15... | collective-permute-start | bytes 393224 | tf_op jit(solution)/shard_map/ppermute | solution.py:476
  24.7 0.9 %shard_map.48 = (f32[128,256]{1,0:T(8,128)S(1)}, bf16[128,4096]{1,0:T(8,128)(2,1)S(1)}) custom-call(bf16[1024,32,128]{2,1,0:T(8,128)(2,1)} %refs_0_.11, bf16[128,32,128]{2,1,0:T(8,128)(2,1)S(1)} %get-tuple-element.51.refs_1_, bf16[128,256]{1,0:T(8,128)(2,1)S(1)} %get-tuple-element.39.refs_2_, f32[32,256]{1,0:T(8,128)S(1)} %get-tuple-element.40.refs_3_), custom_call_target="tpu_custom_call" | custom-call | flops 268435456 | bytes 1048576 | tf_op jit(solution)/shard_map/pallas_call | solution.py:172
  25.6 3.7 %collective-permute-done.1.refs_0_ = f32[128,256]{1,0:T(8,128)S(1)} collective-permute-done((f32[128,256]{1,0:T(8,128)S(1)}, f32[128,256]{1,0:T(8,128)S(1)}, u32[]{:S(2)}, u32[]{:S(2)}) %collective-permute-start.1) | collective-permute-done | bytes 131104 | tf_op jit(solution)/shard_map/ppermute | solution.py:476
  29.7 3.2 %collective-permute-start.11 = (f32[128,256]{1,0:T(8,128)S(1)}, f32[128,256]{1,0:T(8,128)S(1)}, u32[]{:S(2)}, u32[]{:S(2)}) collective-permute-start(f32[128,256]{1,0:T(8,128)S(1)} %shard_map.50.refs_0_), channel_id=1, source_target_pairs={{0,4},{2,6},{4,8},{6,10},{8,12},{10,14},{12,0},{14,2},{1,5},{3,7},... | collective-permute-start | bytes 393224 | tf_op jit(solution)/shard_map/ppermute | solution.py:476
  33.5 2.8 %collective-permute-start.6 = (f32[128,256]{1,0:T(8,128)S(1)}, f32[128,256]{1,0:T(8,128)S(1)}, u32[]{:S(2)}, u32[]{:S(2)}) collective-permute-start(f32[128,256]{1,0:T(8,128)S(1)} %shard_map.50.refs_0_), channel_id=1, source_target_pairs={{0,12},{2,14},{4,0},{6,2},{8,4},{10,6},{12,8},{14,10},{1,13},{3,15... | collective-permute-start | bytes 393224 | tf_op jit(solution)/shard_map/ppermute | solution.py:476
  36.3 1.5 %collective-permute-start.10 = (f32[128,256]{1,0:T(8,128)S(1)}, f32[128,256]{1,0:T(8,128)S(1)}, u32[]{:S(2)}, u32[]{:S(2)}) collective-permute-start(f32[128,256]{1,0:T(8,128)S(1)} %shard_map.50.refs_0_), channel_id=1, source_target_pairs={{0,2},{2,0},{4,6},{6,4},{8,10},{10,8},{12,14},{14,12},{1,3},{3,1},... | collective-permute-start | bytes 393224 | tf_op jit(solution)/shard_map/ppermute | solution.py:472
  37.9 1.7 %collective-permute-start.12 = (f32[128,256]{1,0:T(8,128)S(1)}, f32[128,256]{1,0:T(8,128)S(1)}, u32[]{:S(2)}, u32[]{:S(2)}) collective-permute-start(f32[128,256]{1,0:T(8,128)S(1)} %collective-permute-done.11.refs_2_), channel_id=1, source_target_pairs={{0,2},{2,0},{4,6},{6,4},{8,10},{10,8},{12,14},{14,12},{1,3},{3,1},... | collective-permute-start | bytes 393224 | tf_op jit(solution)/shard_map/ppermute | solution.py:472
  39.6 2.2 %collective-permute-done.8.refs_4_ = f32[128,256]{1,0:T(8,128)S(1)} collective-permute-done((f32[128,256]{1,0:T(8,128)S(1)}, f32[128,256]{1,0:T(8,128)S(1)}, u32[]{:S(2)}, u32[]{:S(2)}) %collective-permute-start.8) | collective-permute-done | bytes 131104 | tf_op jit(solution)/shard_map/ppermute | solution.py:476
  41.8 1.0 %collective-permute-start.9 = (f32[128,256]{1,0:T(8,128)S(1)}, f32[128,256]{1,0:T(8,128)S(1)}, u32[]{:S(2)}, u32[]{:S(2)}) collective-permute-start(f32[128,256]{1,0:T(8,128)S(1)} %collective-permute-done.8.refs_4_), channel_id=1, source_target_pairs={{0,2},{2,0},{4,6},{6,4},{8,10},{10,8},{12,14},{14,12},{1,3},{3,1},... | collective-permute-start | bytes 393224 | tf_op jit(solution)/shard_map/ppermute | solution.py:472
  42.8 1.1 %collective-permute-start.7 = (f32[128,256]{1,0:T(8,128)S(1)}, f32[128,256]{1,0:T(8,128)S(1)}, u32[]{:S(2)}, u32[]{:S(2)}) collective-permute-start(f32[128,256]{1,0:T(8,128)S(1)} %collective-permute-done.6.refs_5_.refs_6_), channel_id=1, source_target_pairs={{0,2},{2,0},{4,6},{6,4},{8,10},{10,8},{12,14},{14,12},{1,3},{3,1},... | collective-permute-start | bytes 393224 | tf_op jit(solution)/shard_map/ppermute | solution.py:472
  43.9 1.4 %collective-permute-done.12.refs_3_ = f32[128,256]{1,0:T(8,128)S(1)} collective-permute-done((f32[128,256]{1,0:T(8,128)S(1)}, f32[128,256]{1,0:T(8,128)S(1)}, u32[]{:S(2)}, u32[]{:S(2)}) %collective-permute-start.12) | collective-permute-done | bytes 131104 | tf_op jit(solution)/shard_map/ppermute | solution.py:472
  45.9 1.0 %collective-permute-done.9.refs_1_.refs_5_ = f32[128,256]{1,0:T(8,128)S(1)} collective-permute-done((f32[128,256]{1,0:T(8,128)S(1)}, f32[128,256]{1,0:T(8,128)S(1)}, u32[]{:S(2)}, u32[]{:S(2)}) %collective-permute-start.9) | collective-permute-done | bytes 131104 | tf_op jit(solution)/shard_map/ppermute | solution.py:472
  46.9 1.4 %collective-permute-done.7.refs_0_.refs_7_ = f32[128,256]{1,0:T(8,128)S(1)} collective-permute-done((f32[128,256]{1,0:T(8,128)S(1)}, f32[128,256]{1,0:T(8,128)S(1)}, u32[]{:S(2)}, u32[]{:S(2)}) %collective-permute-start.7) | collective-permute-done | bytes 131104 | tf_op jit(solution)/shard_map/ppermute | solution.py:472
  48.8 1.5 %collective-permute-done.13.came = f32[256,256]{1,0:T(8,128)S(1)} collective-permute-done((f32[256,256]{1,0:T(8,128)S(1)}, f32[256,256]{1,0:T(8,128)S(1)}, u32[]{:S(2)}, u32[]{:S(2)}) %collective-permute-start.13) | collective-permute-done | bytes 262176 | tf_op jit(solution)/shard_map/ppermute | solution.py:479
  50.3 5.9 %shard_map.53.inverse_ref = f32[256,256]{1,0:T(8,128)S(1)} custom-call(f32[256,256]{1,0:T(8,128)S(1)} %shard_map.52.gram, f32[256,256]{1,0:T(8,128)S(1)} %collective-permute-done.13.came), custom_call_target="tpu_custom_call" | custom-call | flops 50331648 | bytes 524288 | tf_op jit(solution)/shard_map/pallas_call | solution.py:281
  56.3 1.3 %shard_map.54 = (f32[1024,256]{1,0:T(8,128)S(1)}, bf16[256,1024]{1,0:T(8,128)(2,1)S(1)}) custom-call(f32[256,256]{1,0:T(8,128)S(1)} %shard_map.53.inverse_ref, f32[128,256]{1,0:T(8,128)S(1)} %shard_map.50.refs_0_, f32[128,256]{1,0:T(8,128)S(1)} %collective-permute-done.10.refs_1_, f32[128,256]{1,0:T(8,128)S(1)} %collective-permute-done.11.refs_2_, ...), custom_call_target="tpu_custom_call" | custom-call | flops 402653184 | bytes 2097152 | tf_op jit(solution)/shard_map/pallas_call | solution.py:373
  57.6 0.7 %shard_map.55 = (f32[128,1024]{1,0:T(8,128)S(1)}, f32[128,1024]{1,0:T(8,128)S(1)}, f32[1024,256]{1,0:T(8,128)}) custom-call(bf16[256,1024]{1,0:T(8,128)(2,1)S(1)} %get-tuple-element.54.turned_ref, bf16[128,4096]{1,0:T(8,128)(2,1)S(1)} %get-tuple-element.55.refs_0_, bf16[256,4096]{1,0:T(8,128)(2,1)S(1)} %get-tuple-element.56.refs_1_, ...), custom_call_target="tpu_custom_call" | custom-call | flops 536870912 | bytes 2097152 | tf_op jit(solution)/shard_map/pallas_call | solution.py:417
  59.7 0.7 %shard_map.57 = (f32[128,1024]{1,0:T(8,128)S(1)}, f32[128,1024]{1,0:T(8,128)S(1)}, f32[1024,256]{1,0:T(8,128)}) custom-call(bf16[256,1024]{1,0:T(8,128)(2,1)S(1)} %get-tuple-element.54.turned_ref, bf16[128,4096]{1,0:T(8,128)(2,1)S(1)} %get-tuple-element.55.refs_0_, bf16[256,4096]{1,0:T(8,128)(2,1)S(1)} %get-tuple-element.56.refs_1_, ...), custom_call_target="tpu_custom_call", output_to_operand_aliasing={{2}: (8, {})} | custom-call | flops 536870912 | bytes 2097152 | tf_op jit(solution)/shard_map/pallas_call | solution.py:417
  60.4 0.7 %shard_map.58 = (f32[128,1024]{1,0:T(8,128)S(1)}, f32[128,1024]{1,0:T(8,128)S(1)}, f32[1024,256]{1,0:T(8,128)}) custom-call(bf16[256,1024]{1,0:T(8,128)(2,1)S(1)} %get-tuple-element.54.turned_ref, bf16[128,4096]{1,0:T(8,128)(2,1)S(1)} %get-tuple-element.55.refs_0_, bf16[256,4096]{1,0:T(8,128)(2,1)S(1)} %get-tuple-element.56.refs_1_, ...), custom_call_target="tpu_custom_call", output_to_operand_aliasing={{2}: (8, {})} | custom-call | flops 536870912 | bytes 2097152 | tf_op jit(solution)/shard_map/pallas_call | solution.py:417
  61.7 1.4 %collective-permute-done.17.refs_7_ = f32[128,1024]{1,0:T(8,128)S(1)} collective-permute-done((f32[128,1024]{1,0:T(8,128)S(1)}, f32[128,1024]{1,0:T(8,128)S(1)}, u32[]{:S(2)}, u32[]{:S(2)}) %collective-permute-start.17) | collective-permute-done | bytes 524320 | tf_op jit(solution)/shard_map/ppermute | solution.py:479
  63.1 0.7 %collective-permute-done.16.refs_6_ = f32[128,1024]{1,0:T(8,128)S(1)} collective-permute-done((f32[128,1024]{1,0:T(8,128)S(1)}, f32[128,1024]{1,0:T(8,128)S(1)}, u32[]{:S(2)}, u32[]{:S(2)}) %collective-permute-start.16) | collective-permute-done | bytes 524320 | tf_op jit(solution)/shard_map/ppermute | solution.py:479
  63.9 1.1 %shard_map.59 = bf16[128,32,128]{2,1,0:T(8,128)(2,1)} custom-call(f32[128,1024]{1,0:T(8,128)S(1)} %get-tuple-element.66.refs_0_, f32[128,1024]{1,0:T(8,128)S(1)} %get-tuple-element.67.refs_1_, f32[128,1024]{1,0:T(8,128)S(1)} %get-tuple-element.68.refs_2_, f32[128,1024]{1,0:T(8,128)S(1)} %get-tuple-element.69.refs_3_, ...), custom_call_target="tpu_custom_call" | custom-call | bytes 5242880 | tf_op jit(solution)/shard_map/pallas_call | solution.py:453
  (23 shorter events, 4.3 us)
Async XLA Ops:
  4.6 16.2 %collective-permute-start.2 = (f32[256,256]{1,0:T(8,128)S(1)}, f32[256,256]{1,0:T(8,128)S(1)}, u32[]{:S(2)}, u32[]{:S(2)}) collective-permute-start(f32[256,256]{1,0:T(8,128)S(1)} %get-tuple-element.48), channel_id=1, source_target_pairs={{0,2},{2,0},{4,6},{6,4},{8,10},{10,8},{12,14},{14,12},{1,3},{3,1},... | collective-permute-start | bytes 786440 | tf_op jit(solution)/shard_map/ppermute | solution.py:472
  7.6 10.0 %collective-permute-start = (f32[128,256]{1,0:T(8,128)S(1)}, f32[128,256]{1,0:T(8,128)S(1)}, u32[]{:S(2)}, u32[]{:S(2)}) collective-permute-start(f32[128,256]{1,0:T(8,128)S(1)} %get-tuple-element.43), channel_id=1, source_target_pairs={{0,2},{2,0},{4,6},{6,4},{8,10},{10,8},{12,14},{14,12},{1,3},{3,1},... | collective-permute-start | bytes 393224 | tf_op jit(solution)/shard_map/ppermute | solution.py:472
  10.5 15.0 %collective-permute-start.5 = (f32[128,256]{1,0:T(8,128)S(1)}, f32[128,256]{1,0:T(8,128)S(1)}, u32[]{:S(2)}, u32[]{:S(2)}) collective-permute-start(f32[128,256]{1,0:T(8,128)S(1)} %get-tuple-element.53), channel_id=1, source_target_pairs={{0,2},{2,0},{4,6},{6,4},{8,10},{10,8},{12,14},{14,12},{1,3},{3,1},... | collective-permute-start | bytes 393224 | tf_op jit(solution)/shard_map/ppermute | solution.py:472
  17.6 11.7 %collective-permute-start.1 = (f32[128,256]{1,0:T(8,128)S(1)}, f32[128,256]{1,0:T(8,128)S(1)}, u32[]{:S(2)}, u32[]{:S(2)}) collective-permute-start(f32[128,256]{1,0:T(8,128)S(1)} %shard_map.44), channel_id=1, source_target_pairs={{0,8},{2,10},{4,12},{6,14},{8,0},{10,2},{12,4},{14,6},{1,9},{3,11}... | collective-permute-start | bytes 393224 | tf_op jit(solution)/shard_map/ppermute | solution.py:476
  20.8 8.5 %collective-permute-start.3 = (f32[128,256]{1,0:T(8,128)S(1)}, f32[128,256]{1,0:T(8,128)S(1)}, u32[]{:S(2)}, u32[]{:S(2)}) collective-permute-start(f32[128,256]{1,0:T(8,128)S(1)} %get-tuple-element.49), channel_id=1, source_target_pairs={{0,4},{2,6},{4,8},{6,10},{8,12},{10,14},{12,0},{14,2},{1,5},{3,7},... | collective-permute-start | bytes 393224 | tf_op jit(solution)/shard_map/ppermute | solution.py:476
  22.4 7.2 %collective-permute-start.4 = (f32[128,256]{1,0:T(8,128)S(1)}, f32[128,256]{1,0:T(8,128)S(1)}, u32[]{:S(2)}, u32[]{:S(2)}) collective-permute-start(f32[128,256]{1,0:T(8,128)S(1)} %get-tuple-element.50), channel_id=1, source_target_pairs={{0,12},{2,14},{4,0},{6,2},{8,4},{10,6},{12,8},{14,10},{1,13},{3,15... | collective-permute-start | bytes 393224 | tf_op jit(solution)/shard_map/ppermute | solution.py:476
  29.7 8.3 %collective-permute-start.11 = (f32[128,256]{1,0:T(8,128)S(1)}, f32[128,256]{1,0:T(8,128)S(1)}, u32[]{:S(2)}, u32[]{:S(2)}) collective-permute-start(f32[128,256]{1,0:T(8,128)S(1)} %shard_map.50.refs_0_), channel_id=1, source_target_pairs={{0,4},{2,6},{4,8},{6,10},{8,12},{10,14},{12,0},{14,2},{1,5},{3,7},... | collective-permute-start | bytes 393224 | tf_op jit(solution)/shard_map/ppermute | solution.py:476
  32.9 9.0 %collective-permute-start.8 = (f32[128,256]{1,0:T(8,128)S(1)}, f32[128,256]{1,0:T(8,128)S(1)}, u32[]{:S(2)}, u32[]{:S(2)}) collective-permute-start(f32[128,256]{1,0:T(8,128)S(1)} %shard_map.50.refs_0_), channel_id=1, source_target_pairs={{0,8},{2,10},{4,12},{6,14},{8,0},{10,2},{12,4},{14,6},{1,9},{3,11}... | collective-permute-start | bytes 393224 | tf_op jit(solution)/shard_map/ppermute | solution.py:476
  33.5 9.3 %collective-permute-start.6 = (f32[128,256]{1,0:T(8,128)S(1)}, f32[128,256]{1,0:T(8,128)S(1)}, u32[]{:S(2)}, u32[]{:S(2)}) collective-permute-start(f32[128,256]{1,0:T(8,128)S(1)} %shard_map.50.refs_0_), channel_id=1, source_target_pairs={{0,12},{2,14},{4,0},{6,2},{8,4},{10,6},{12,8},{14,10},{1,13},{3,15... | collective-permute-start | bytes 393224 | tf_op jit(solution)/shard_map/ppermute | solution.py:476
  36.3 7.5 %collective-permute-start.10 = (f32[128,256]{1,0:T(8,128)S(1)}, f32[128,256]{1,0:T(8,128)S(1)}, u32[]{:S(2)}, u32[]{:S(2)}) collective-permute-start(f32[128,256]{1,0:T(8,128)S(1)} %shard_map.50.refs_0_), channel_id=1, source_target_pairs={{0,2},{2,0},{4,6},{6,4},{8,10},{10,8},{12,14},{14,12},{1,3},{3,1},... | collective-permute-start | bytes 393224 | tf_op jit(solution)/shard_map/ppermute | solution.py:472
  37.9 7.3 %collective-permute-start.12 = (f32[128,256]{1,0:T(8,128)S(1)}, f32[128,256]{1,0:T(8,128)S(1)}, u32[]{:S(2)}, u32[]{:S(2)}) collective-permute-start(f32[128,256]{1,0:T(8,128)S(1)} %collective-permute-done.11.refs_2_), channel_id=1, source_target_pairs={{0,2},{2,0},{4,6},{6,4},{8,10},{10,8},{12,14},{14,12},{1,3},{3,1},... | collective-permute-start | bytes 393224 | tf_op jit(solution)/shard_map/ppermute | solution.py:472
  41.8 5.1 %collective-permute-start.9 = (f32[128,256]{1,0:T(8,128)S(1)}, f32[128,256]{1,0:T(8,128)S(1)}, u32[]{:S(2)}, u32[]{:S(2)}) collective-permute-start(f32[128,256]{1,0:T(8,128)S(1)} %collective-permute-done.8.refs_4_), channel_id=1, source_target_pairs={{0,2},{2,0},{4,6},{6,4},{8,10},{10,8},{12,14},{14,12},{1,3},{3,1},... | collective-permute-start | bytes 393224 | tf_op jit(solution)/shard_map/ppermute | solution.py:472
  42.8 5.5 %collective-permute-start.7 = (f32[128,256]{1,0:T(8,128)S(1)}, f32[128,256]{1,0:T(8,128)S(1)}, u32[]{:S(2)}, u32[]{:S(2)}) collective-permute-start(f32[128,256]{1,0:T(8,128)S(1)} %collective-permute-done.6.refs_5_.refs_6_), channel_id=1, source_target_pairs={{0,2},{2,0},{4,6},{6,4},{8,10},{10,8},{12,14},{14,12},{1,3},{3,1},... | collective-permute-start | bytes 393224 | tf_op jit(solution)/shard_map/ppermute | solution.py:472
  48.7 1.6 %collective-permute-start.13 = (f32[256,256]{1,0:T(8,128)S(1)}, f32[256,256]{1,0:T(8,128)S(1)}, u32[]{:S(2)}, u32[]{:S(2)}) collective-permute-start(f32[256,256]{1,0:T(8,128)S(1)} %shard_map.52.gram), channel_id=1, source_target_pairs={{0,1},{1,0},{2,3},{3,2},{4,5},{5,4},{6,7},{7,6},{8,9},{9,8},{10,11... | collective-permute-start | bytes 786440 | tf_op jit(solution)/shard_map/ppermute | solution.py:479
  58.3 3.4 %collective-permute-start.14 = (f32[128,1024]{1,0:T(8,128)S(1)}, f32[128,1024]{1,0:T(8,128)S(1)}, u32[]{:S(2)}, u32[]{:S(2)}) collective-permute-start(f32[128,1024]{1,0:T(8,128)S(1)} %get-tuple-element.70), channel_id=1, source_target_pairs={{0,1},{1,0},{2,3},{3,2},{4,5},{5,4},{6,7},{7,6},{8,9},{9,8},{10,11... | collective-permute-start | bytes 1572872 | tf_op jit(solution)/shard_map/ppermute | solution.py:479
  59.2 2.5 %collective-permute-start.15 = (f32[128,1024]{1,0:T(8,128)S(1)}, f32[128,1024]{1,0:T(8,128)S(1)}, u32[]{:S(2)}, u32[]{:S(2)}) collective-permute-start(f32[128,1024]{1,0:T(8,128)S(1)} %get-tuple-element.71), channel_id=1, source_target_pairs={{0,1},{1,0},{2,3},{3,2},{4,5},{5,4},{6,7},{7,6},{8,9},{9,8},{10,11... | collective-permute-start | bytes 1572872 | tf_op jit(solution)/shard_map/ppermute | solution.py:479
  61.2 2.0 %collective-permute-start.17 = (f32[128,1024]{1,0:T(8,128)S(1)}, f32[128,1024]{1,0:T(8,128)S(1)}, u32[]{:S(2)}, u32[]{:S(2)}) collective-permute-start(f32[128,1024]{1,0:T(8,128)S(1)} %get-tuple-element.73), channel_id=1, source_target_pairs={{0,1},{1,0},{2,3},{3,2},{4,5},{5,4},{6,7},{7,6},{8,9},{9,8},{10,11... | collective-permute-start | bytes 1572872 | tf_op jit(solution)/shard_map/ppermute | solution.py:479
  61.4 2.5 %collective-permute-start.16 = (f32[128,1024]{1,0:T(8,128)S(1)}, f32[128,1024]{1,0:T(8,128)S(1)}, u32[]{:S(2)}, u32[]{:S(2)}) collective-permute-start(f32[128,1024]{1,0:T(8,128)S(1)} %get-tuple-element.72), channel_id=1, source_target_pairs={{0,1},{1,0},{2,3},{3,2},{4,5},{5,4},{6,7},{7,6},{8,9},{9,8},{10,11... | collective-permute-start | bytes 1572872 | tf_op jit(solution)/shard_map/ppermute | solution.py:479

commit v7 on v6

--- a/solution.py
+++ b/solution.py
@@ -299,28 +299,37 @@
     )(*kept, came)
 
 
-def total_of(parts):
+def total_of(parts, cut):
+    chunk = parts[0].shape[0]
+    half = chunk // 2
+
     def kernel(*refs):
         sums = refs[0][...]
-        for ref in refs[1:-1]:
+        for ref in refs[1:len(parts)]:
             sums = sums + ref[...]
-        refs[-1][...] = sums
-
-    return call(
-        kernel, held(parts[0].shape, f32), [VMEM_SPACE] * len(parts),
+        outs = refs[len(parts):]
+        outs[0][...] = sums
+        if cut:
+            outs[1][...] = sums[:half]
+            outs[2][...] = sums[half:]
+
+    shapes = [(chunk, RANK)] + ([(half, RANK)] * 2 if cut else [])
+    return call(
+        kernel, [held(shape, f32) for shape in shapes], [VMEM_SPACE] * len(parts),
         flops=parts[0].size * len(parts), moved=4 * parts[0].size * len(parts),
     )(*parts)
 
 
 def gram_of(chunks, base=None):
-    chunk = chunks[0].shape[0]
-    total = len(chunks) * chunk
+    total = sum(rows.shape[0] for rows in chunks)
 
     def kernel(*refs):
         rows_refs, (out, terms) = refs[:len(chunks)], refs[-2:]
-        for k, ref in enumerate(rows_refs):
+        at = 0
+        for ref in rows_refs:
             for j, term in enumerate(split3(ref[...])):
-                terms[k * chunk:(k + 1) * chunk, j * RANK:(j + 1) * RANK] = term
+                terms[at:at + ref.shape[0], j * RANK:(j + 1) * RANK] = term
+            at += ref.shape[0]
         over_rows = (((0,), (0,)), ((), ()))
         first = lax.dot_general(
             terms[:, :RANK], terms[...], over_rows, preferred_element_type=f32
@@ -344,9 +353,9 @@
     return high, (value - high.astype(f32)).astype(bf16)
 
 
-def solve_rows(chunks, inverse, sizes, places):
+def solve_rows(pieces, inverse, sizes, places):
     outer, inner, chunk = sizes
-    total = len(chunks) * chunk
+    total = outer * inner * chunk
     half = RANK // 2
 
     def kernel(inverse_ref, *refs):
@@ -355,14 +364,15 @@
         o, y = me // inner, me % inner
         high, low = split2(inverse_ref[...])
         right = jnp.concatenate([high, high, low], axis=1)
-        for k in range(outer * inner):
-            d, flip = k // inner, k % inner
-            high, low = split2(rows_refs[k][...])
+        for (k, begin, _), ref in zip(pieces, rows_refs):
+            d, flip, size = k // inner, k % inner, ref.shape[0]
+            high, low = split2(ref[...])
             left = jnp.concatenate([high, low, high], axis=1)
             value = lax.dot_general(left, right, (((1,), (1,)), ((), ())), preferred_element_type=f32)
             chosen = lax.rem(o + outer - d, outer) * inner + (inner - 1 - y if flip else y)
-            basis[pl.ds(pl.multiple_of(chosen * chunk, chunk), chunk), :] = value
-            rounded[places[k] * chunk:(places[k] + 1) * chunk, :] = value
+            basis[pl.ds(pl.multiple_of(chosen * chunk + begin, size), size), :] = value
+            spot = places[k] * chunk + begin
+            rounded[spot:spot + size, :] = value
         step = 128
         for start in range(0, total, step):
             block = rounded[start:start + step, :].T.astype(bf16)
@@ -372,10 +382,10 @@
 
     return call(
         kernel, [held((total, RANK), f32), held((RANK, total), bf16)],
-        [VMEM_SPACE] * (1 + len(chunks)),
+        [VMEM_SPACE] * (1 + len(pieces)),
         flops=6 * total * RANK ** 2, moved=8 * total * RANK,
         scratch_shapes=[pltpu.VMEM((total, RANK), f32)],
-    )(inverse, *chunks)
+    )(inverse, *[rows for _, _, rows in pieces])
 
 
 WIDTH = 256
@@ -497,23 +507,29 @@
         kept = merge(made, sends[k]) if inner == 2 else made
         for j, d in enumerate(groups[k]):
             parts.append(shift(kept[j], d) if d else kept[j])
-    own = total_of(parts)
-    chunks = [None] * count
+    cut = early_gram(inner, outer)
+    own, *halves = total_of(parts, cut)
     near = [0] + sorted(range(1, outer), key=lambda d: min(d, outer - d))
-    for d in near:
-        came = shift(own, d) if d else own
-        chunks[d * inner] = came
+    sent = [(d, 0, own) for d in near[:-1 if cut else None]]
+    sent += [(near[-1], k * chunk // 2, half) for k, half in enumerate(halves)]
+    gathered, early = [], []
+    for k, (d, begin, rows) in enumerate(sent):
+        came = shift(rows, d) if d else rows
+        gathered.append((d * inner, begin, came))
+        early.append(True)
         if inner == 2:
-            chunks[d * inner + 1] = neighbour(came)
-    late = [d * inner + 1 for d in near[-2:]] if early_gram(inner, outer) else []
+            gathered.append((d * inner + 1, begin, neighbour(came)))
+            early.append(k < outer - 2)
     gram = None
-    if late:
-        gram = gram_of([chunks[k] for k in range(count) if k not in late])
-    gram = gram_of([chunks[k] for k in late or range(count)], gram)
+    if early_gram(inner, outer):
+        gram = gram_of([rows for (_, _, rows), now in zip(gathered, early) if now])
+        gram = gram_of([rows for (_, _, rows), now in zip(gathered, early) if not now], gram)
+    else:
+        gram = gram_of([rows for _, _, rows in gathered])
     came = other_core(gram)
     inverse = inverse_factor(gram, came)
     places = [wanted.index(((outer - k // inner) % outer, k % inner)) for k in range(count)]
-    basis, turned = solve_rows(chunks, inverse, sizes, places)
+    basis, turned = solve_rows(gathered, inverse, sizes, places)
     columns = y_local * z_local
     stored, mine, came = None, [], []
     for k in range(PIECES):

time: 65.6 us -> 69.9 us (1.066)
  waiting for transfers between devices: 17.1 us -> 20.5 us
  starting transfers between devices: 25.4 us -> 26.4 us
    ppermute x6 -> x7, waiting for transfers between devices: 6.31 us -> 9.93 us  [shift(): return lax.ppermute(value, 'yz', pairs)]
    ppermute x6 -> x7, starting transfers between devices: 13.7 us -> 16.1 us  [shift(): return lax.ppermute(value, 'yz', pairs)]
    ppermute x7 -> x8, starting transfers between devices: 10.4 us -> 9.03 us  [neighbour(): return lax.ppermute(value, 'yz', [(i, i ^ 1) for i in range(count)])]
    ppermute x7 -> x8, waiting for transfers between devices: 7.1 us -> 6.91 us  [neighbour(): return lax.ppermute(value, 'yz', [(i, i ^ 1) for i in range(count)])]
  transfers between devices with their start and end apart: 18 -> 20, of which waited for: 11 -> 11; matrix products, arithmetic and copies ran while one was open for 0% -> 0% of each run, Pallas kernels for 13% -> 12%
where the time goes in v7:
time: 69.9 us; the launch traced here: 69.7 us
  starting transfers between devices  26.4 us (38%)
  Pallas kernels  21.9 us (31%)
  waiting for transfers between devices  20.5 us (29%)
  between operations  0.96 us (1%)
    ppermute x7, starting transfers between devices, shift(): return lax.ppermute(value, 'yz', pairs)  16.1 us
    ppermute x7, waiting for transfers between devices, shift(): return lax.ppermute(value, 'yz', pairs)  9.93 us
    pallas_call x6, Pallas kernels, sketch_chunks(): call(kernel, out_shape, in_specs, flops=2 * total * y_local * z_local * R...  9.34 us
    ppermute x8, starting transfers between devices, neighbour(): return lax.ppermute(value, 'yz', [(i, i ^ 1) for i in range(count)])  9.03 us
    ppermute x8, waiting for transfers between devices, neighbour(): return lax.ppermute(value, 'yz', [(i, i ^ 1) for i in range(count)])  6.91 us
    pallas_call x1, Pallas kernels, inverse_factor(): call(inverse_factor_kernel, held(gram.shape, f32), [VMEM_SPACE] * 2, flop...  5.92 us
    ppermute x5, waiting for transfers between devices, other_core(): return lax.ppermute(value, 'gx', [(0, 1), (1, 0)])  3.67 us
    pallas_call x4, Pallas kernels, product(): call(kernel, [held(shape, f32), held(shape, f32), pltpu.HBM(basis.shape,...  2.91 us
  transfers between devices with their start and end apart: 20, of which 11 were waited for; matrix products, arithmetic and copies ran while one was open for 0% of the time, Pallas kernels for 12%

profile of v7, /device:TPU:0, one launch (start us, length us, event | category | flops | bytes accessed | tf_op | source)
XLA Modules:
  0.0 69.7 jit_solution(6373606053139764207)
XLA Ops:
  0.6 2.2 %shard_map.41 = (f32[128,256]{1,0:T(8,128)S(1)}, bf16[128,4096]{1,0:T(8,128)(2,1)S(1)}, bf16[256,32,128]{2,1,0:T(8,128)(2,1)S(1)}, bf16[128,256]{1,0:T(8,128)(2,1)S(1)}, f32[32,256]{1,0:T(8,128)S(1)}) custom-call(bf16[1024,32,128]{2,1,0:T(8,128)(2,1)} %refs_0_.11, s32[6]{0:T(128)} %refs_1_.1), custom_call_target="tpu_custom_call" | custom-call | flops 268435456 | bytes 1048576 | tf_op jit(solution)/shard_map/pallas_call | solution.py:172
  2.8 1.7 %shard_map.42 = (f32[256,256]{1,0:T(8,128)S(1)}, bf16[256,4096]{1,0:T(8,128)(2,1)S(1)}, bf16[128,32,128]{2,1,0:T(8,128)(2,1)S(1)}) custom-call(bf16[1024,32,128]{2,1,0:T(8,128)(2,1)} %refs_0_.11, bf16[256,32,128]{2,1,0:T(8,128)(2,1)S(1)} %get-tuple-element.41.refs_1_, bf16[128,256]{1,0:T(8,128)(2,1)S(1)} %get-tuple-element.42.refs_2_, ...), custom_call_target="tpu_custom_call" | custom-call | flops 536870912 | bytes 2097152 | tf_op jit(solution)/shard_map/pallas_call | solution.py:172
  4.6 3.1 %collective-permute-start.2 = (f32[256,256]{1,0:T(8,128)S(1)}, f32[256,256]{1,0:T(8,128)S(1)}, u32[]{:S(2)}, u32[]{:S(2)}) collective-permute-start(f32[256,256]{1,0:T(8,128)S(1)} %get-tuple-element.51), channel_id=1, source_target_pairs={{0,2},{2,0},{4,6},{6,4},{8,10},{10,8},{12,14},{14,12},{1,3},{3,1},... | collective-permute-start | bytes 786440 | tf_op jit(solution)/shard_map/ppermute | solution.py:482
  7.7 1.2 %shard_map.43 = (f32[128,256]{1,0:T(8,128)S(1)}, bf16[128,4096]{1,0:T(8,128)(2,1)S(1)}, bf16[128,32,128]{2,1,0:T(8,128)(2,1)S(1)}) custom-call(bf16[1024,32,128]{2,1,0:T(8,128)(2,1)} %refs_0_.11, bf16[128,32,128]{2,1,0:T(8,128)(2,1)S(1)} %get-tuple-element.44.refs_1_, bf16[128,256]{1,0:T(8,128)(2,1)S(1)} %get-tuple-element.42.refs_2_, ...), custom_call_target="tpu_custom_call" | custom-call | flops 268435456 | bytes 1048576 | tf_op jit(solution)/shard_map/pallas_call | solution.py:172
  8.9 1.6 %shard_map.45 = (f32[128,256]{1,0:T(8,128)S(1)}, bf16[128,4096]{1,0:T(8,128)(2,1)S(1)}, bf16[256,32,128]{2,1,0:T(8,128)(2,1)S(1)}) custom-call(bf16[1024,32,128]{2,1,0:T(8,128)(2,1)} %refs_0_.11, bf16[128,32,128]{2,1,0:T(8,128)(2,1)S(1)} %get-tuple-element.47.refs_1_, bf16[128,256]{1,0:T(8,128)(2,1)S(1)} %get-tuple-element.42.refs_2_, ...), custom_call_target="tpu_custom_call" | custom-call | flops 268435456 | bytes 1048576 | tf_op jit(solution)/shard_map/pallas_call | solution.py:172
  10.5 2.0 %collective-permute-start.5 = (f32[128,256]{1,0:T(8,128)S(1)}, f32[128,256]{1,0:T(8,128)S(1)}, u32[]{:S(2)}, u32[]{:S(2)}) collective-permute-start(f32[128,256]{1,0:T(8,128)S(1)} %get-tuple-element.56), channel_id=1, source_target_pairs={{0,2},{2,0},{4,6},{6,4},{8,10},{10,8},{12,14},{14,12},{1,3},{3,1},... | collective-permute-start | bytes 393224 | tf_op jit(solution)/shard_map/ppermute | solution.py:482
  12.6 1.7 %shard_map.46 = (f32[128,256]{1,0:T(8,128)S(1)}, f32[128,256]{1,0:T(8,128)S(1)}, bf16[256,4096]{1,0:T(8,128)(2,1)S(1)}, bf16[128,32,128]{2,1,0:T(8,128)(2,1)S(1)}) custom-call(bf16[1024,32,128]{2,1,0:T(8,128)(2,1)} %refs_0_.11, bf16[256,32,128]{2,1,0:T(8,128)(2,1)S(1)} %get-tuple-element.48.refs_1_, bf16[128,256]{1,0:T(8,128)(2,1)S(1)} %get-tuple-element.42.refs_2_, ...), custom_call_target="tpu_custom_call" | custom-call | flops 536870912 | bytes 2097152 | tf_op jit(solution)/shard_map/pallas_call | solution.py:172
  14.3 3.3 %collective-permute-done.refs_1_ = f32[128,256]{1,0:T(8,128)S(1)} collective-permute-done((f32[128,256]{1,0:T(8,128)S(1)}, f32[128,256]{1,0:T(8,128)S(1)}, u32[]{:S(2)}, u32[]{:S(2)}) %collective-permute-start) | collective-permute-done | bytes 131104 | tf_op jit(solution)/shard_map/ppermute | solution.py:482
  17.6 3.2 %collective-permute-start.1 = (f32[128,256]{1,0:T(8,128)S(1)}, f32[128,256]{1,0:T(8,128)S(1)}, u32[]{:S(2)}, u32[]{:S(2)}) collective-permute-start(f32[128,256]{1,0:T(8,128)S(1)} %shard_map.44), channel_id=1, source_target_pairs={{0,8},{2,10},{4,12},{6,14},{8,0},{10,2},{12,4},{14,6},{1,9},{3,11}... | collective-permute-start | bytes 393224 | tf_op jit(solution)/shard_map/ppermute | solution.py:486
  20.8 1.6 %collective-permute-start.3 = (f32[128,256]{1,0:T(8,128)S(1)}, f32[128,256]{1,0:T(8,128)S(1)}, u32[]{:S(2)}, u32[]{:S(2)}) collective-permute-start(f32[128,256]{1,0:T(8,128)S(1)} %get-tuple-element.52), channel_id=1, source_target_pairs={{0,4},{2,6},{4,8},{6,10},{8,12},{10,14},{12,0},{14,2},{1,5},{3,7},... | collective-permute-start | bytes 393224 | tf_op jit(solution)/shard_map/ppermute | solution.py:486
  22.4 2.2 %collective-permute-start.4 = (f32[128,256]{1,0:T(8,128)S(1)}, f32[128,256]{1,0:T(8,128)S(1)}, u32[]{:S(2)}, u32[]{:S(2)}) collective-permute-start(f32[128,256]{1,0:T(8,128)S(1)} %get-tuple-element.53), channel_id=1, source_target_pairs={{0,12},{2,14},{4,0},{6,2},{8,4},{10,6},{12,8},{14,10},{1,13},{3,15... | collective-permute-start | bytes 393224 | tf_op jit(solution)/shard_map/ppermute | solution.py:486
  24.7 0.9 %shard_map.48 = (f32[128,256]{1,0:T(8,128)S(1)}, bf16[128,4096]{1,0:T(8,128)(2,1)S(1)}) custom-call(bf16[1024,32,128]{2,1,0:T(8,128)(2,1)} %refs_0_.11, bf16[128,32,128]{2,1,0:T(8,128)(2,1)S(1)} %get-tuple-element.54.refs_1_, bf16[128,256]{1,0:T(8,128)(2,1)S(1)} %get-tuple-element.42.refs_2_, f32[32,256]{1,0:T(8,128)S(1)} %get-tuple-element.43.refs_3_), custom_call_target="tpu_custom_call" | custom-call | flops 268435456 | bytes 1048576 | tf_op jit(solution)/shard_map/pallas_call | solution.py:172
  25.6 3.7 %collective-permute-done.1.refs_0_ = f32[128,256]{1,0:T(8,128)S(1)} collective-permute-done((f32[128,256]{1,0:T(8,128)S(1)}, f32[128,256]{1,0:T(8,128)S(1)}, u32[]{:S(2)}, u32[]{:S(2)}) %collective-permute-start.1) | collective-permute-done | bytes 131104 | tf_op jit(solution)/shard_map/ppermute | solution.py:486
  29.7 3.2 %collective-permute-start.13 = (f32[128,256]{1,0:T(8,128)S(1)}, f32[128,256]{1,0:T(8,128)S(1)}, u32[]{:S(2)}, u32[]{:S(2)}) collective-permute-start(f32[128,256]{1,0:T(8,128)S(1)} %get-tuple-element.57.refs_0_), channel_id=1, source_target_pairs={{0,4},{2,6},{4,8},{6,10},{8,12},{10,14},{12,0},{14,2},{1,5},{3,7},... | collective-permute-start | bytes 393224 | tf_op jit(solution)/shard_map/ppermute | solution.py:486
  33.5 1.7 %collective-permute-start.12 = (f32[128,256]{1,0:T(8,128)S(1)}, f32[128,256]{1,0:T(8,128)S(1)}, u32[]{:S(2)}, u32[]{:S(2)}) collective-permute-start(f32[128,256]{1,0:T(8,128)S(1)} %get-tuple-element.57.refs_0_), channel_id=1, source_target_pairs={{0,2},{2,0},{4,6},{6,4},{8,10},{10,8},{12,14},{14,12},{1,3},{3,1},... | collective-permute-start | bytes 393224 | tf_op jit(solution)/shard_map/ppermute | solution.py:482
  35.2 1.3 %collective-permute-done.13.refs_2_ = f32[128,256]{1,0:T(8,128)S(1)} collective-permute-done((f32[128,256]{1,0:T(8,128)S(1)}, f32[128,256]{1,0:T(8,128)S(1)}, u32[]{:S(2)}, u32[]{:S(2)}) %collective-permute-start.13) | collective-permute-done | bytes 131104 | tf_op jit(solution)/shard_map/ppermute | solution.py:486
  36.5 1.7 %collective-permute-start.14 = (f32[128,256]{1,0:T(8,128)S(1)}, f32[128,256]{1,0:T(8,128)S(1)}, u32[]{:S(2)}, u32[]{:S(2)}) collective-permute-start(f32[128,256]{1,0:T(8,128)S(1)} %collective-permute-done.13.refs_2_), channel_id=1, source_target_pairs={{0,2},{2,0},{4,6},{6,4},{8,10},{10,8},{12,14},{14,12},{1,3},{3,1},... | collective-permute-start | bytes 393224 | tf_op jit(solution)/shard_map/ppermute | solution.py:482
  38.2 5.1 %collective-permute-start.8 = (f32[64,256]{1,0:T(8,128)S(1)}, f32[64,256]{1,0:T(8,128)S(1)}, u32[]{:S(2)}, u32[]{:S(2)}) collective-permute-start(f32[64,256]{1,0:T(8,128)S(1)} %get-tuple-element.58), channel_id=1, source_target_pairs={{0,8},{2,10},{4,12},{6,14},{8,0},{10,2},{12,4},{14,6},{1,9},{3,11}... | collective-permute-start | bytes 196616 | tf_op jit(solution)/shard_map/ppermute | solution.py:486
  43.4 2.4 %collective-permute-done.8.refs_5_.refs_6_ = f32[64,256]{1,0:T(8,128)S(1)} collective-permute-done((f32[64,256]{1,0:T(8,128)S(1)}, f32[64,256]{1,0:T(8,128)S(1)}, u32[]{:S(2)}, u32[]{:S(2)}) %collective-permute-start.8) | collective-permute-done | bytes 65568 | tf_op jit(solution)/shard_map/ppermute | solution.py:486
  46.3 2.2 %collective-permute-done.10.refs_6_.refs_8_ = f32[64,256]{1,0:T(8,128)S(1)} collective-permute-done((f32[64,256]{1,0:T(8,128)S(1)}, f32[64,256]{1,0:T(8,128)S(1)}, u32[]{:S(2)}, u32[]{:S(2)}) %collective-permute-start.10) | collective-permute-done | bytes 65568 | tf_op jit(solution)/shard_map/ppermute | solution.py:486
  49.2 0.8 %collective-permute-done.9.refs_1_.refs_7_ = f32[64,256]{1,0:T(8,128)S(1)} collective-permute-done((f32[64,256]{1,0:T(8,128)S(1)}, f32[64,256]{1,0:T(8,128)S(1)}, u32[]{:S(2)}, u32[]{:S(2)}) %collective-permute-start.9) | collective-permute-done | bytes 65568 | tf_op jit(solution)/shard_map/ppermute | solution.py:482
  50.0 2.7 %collective-permute-done.11.refs_2_.refs_9_ = f32[64,256]{1,0:T(8,128)S(1)} collective-permute-done((f32[64,256]{1,0:T(8,128)S(1)}, f32[64,256]{1,0:T(8,128)S(1)}, u32[]{:S(2)}, u32[]{:S(2)}) %collective-permute-start.11) | collective-permute-done | bytes 65568 | tf_op jit(solution)/shard_map/ppermute | solution.py:482
  53.2 1.5 %collective-permute-done.15.came = f32[256,256]{1,0:T(8,128)S(1)} collective-permute-done((f32[256,256]{1,0:T(8,128)S(1)}, f32[256,256]{1,0:T(8,128)S(1)}, u32[]{:S(2)}, u32[]{:S(2)}) %collective-permute-start.15) | collective-permute-done | bytes 262176 | tf_op jit(solution)/shard_map/ppermute | solution.py:489
  54.8 5.9 %shard_map.53.inverse_ref = f32[256,256]{1,0:T(8,128)S(1)} custom-call(f32[256,256]{1,0:T(8,128)S(1)} %shard_map.52.gram, f32[256,256]{1,0:T(8,128)S(1)} %collective-permute-done.15.came), custom_call_target="tpu_custom_call" | custom-call | flops 50331648 | bytes 524288 | tf_op jit(solution)/shard_map/pallas_call | solution.py:281
  60.7 1.5 %shard_map.54 = (f32[1024,256]{1,0:T(8,128)S(1)}, bf16[256,1024]{1,0:T(8,128)(2,1)S(1)}) custom-call(f32[256,256]{1,0:T(8,128)S(1)} %shard_map.53.inverse_ref, f32[128,256]{1,0:T(8,128)S(1)} %get-tuple-element.57.refs_0_, f32[128,256]{1,0:T(8,128)S(1)} %collective-permute-done.12.refs_1_, f32[128,256]{1,0:T(8,128)S(1)} %collective-permute-done.13.refs_2_, ...), custom_call_target="tpu_custom_call" | custom-call | flops 402653184 | bytes 2097152 | tf_op jit(solution)/shard_map/pallas_call | solution.py:383
  62.2 0.7 %shard_map.55 = (f32[128,1024]{1,0:T(8,128)S(1)}, f32[128,1024]{1,0:T(8,128)S(1)}, f32[1024,256]{1,0:T(8,128)}) custom-call(bf16[256,1024]{1,0:T(8,128)(2,1)S(1)} %get-tuple-element.60.turned_ref, bf16[128,4096]{1,0:T(8,128)(2,1)S(1)} %get-tuple-element.61.refs_0_, bf16[256,4096]{1,0:T(8,128)(2,1)S(1)} %get-tuple-element.62.refs_1_, ...), custom_call_target="tpu_custom_call" | custom-call | flops 536870912 | bytes 2097152 | tf_op jit(solution)/shard_map/pallas_call | solution.py:427
  63.1 0.7 %shard_map.56 = (f32[128,1024]{1,0:T(8,128)S(1)}, f32[128,1024]{1,0:T(8,128)S(1)}, f32[1024,256]{1,0:T(8,128)}) custom-call(bf16[256,1024]{1,0:T(8,128)(2,1)S(1)} %get-tuple-element.60.turned_ref, bf16[128,4096]{1,0:T(8,128)(2,1)S(1)} %get-tuple-element.61.refs_0_, bf16[256,4096]{1,0:T(8,128)(2,1)S(1)} %get-tuple-element.62.refs_1_, ...), custom_call_target="tpu_custom_call", output_to_operand_aliasing={{2}: (8, {})} | custom-call | flops 536870912 | bytes 2097152 | tf_op jit(solution)/shard_map/pallas_call | solution.py:427
  64.3 0.7 %shard_map.57 = (f32[128,1024]{1,0:T(8,128)S(1)}, f32[128,1024]{1,0:T(8,128)S(1)}, f32[1024,256]{1,0:T(8,128)}) custom-call(bf16[256,1024]{1,0:T(8,128)(2,1)S(1)} %get-tuple-element.60.turned_ref, bf16[128,4096]{1,0:T(8,128)(2,1)S(1)} %get-tuple-element.61.refs_0_, bf16[256,4096]{1,0:T(8,128)(2,1)S(1)} %get-tuple-element.62.refs_1_, ...), custom_call_target="tpu_custom_call", output_to_operand_aliasing={{2}: (8, {})} | custom-call | flops 536870912 | bytes 2097152 | tf_op jit(solution)/shard_map/pallas_call | solution.py:427
  65.0 0.7 %shard_map.58 = (f32[128,1024]{1,0:T(8,128)S(1)}, f32[128,1024]{1,0:T(8,128)S(1)}, f32[1024,256]{1,0:T(8,128)}) custom-call(bf16[256,1024]{1,0:T(8,128)(2,1)S(1)} %get-tuple-element.60.turned_ref, bf16[128,4096]{1,0:T(8,128)(2,1)S(1)} %get-tuple-element.61.refs_0_, bf16[256,4096]{1,0:T(8,128)(2,1)S(1)} %get-tuple-element.62.refs_1_, ...), custom_call_target="tpu_custom_call", output_to_operand_aliasing={{2}: (8, {})} | custom-call | flops 536870912 | bytes 2097152 | tf_op jit(solution)/shard_map/pallas_call | solution.py:427
  66.3 1.4 %collective-permute-done.19.refs_7_ = f32[128,1024]{1,0:T(8,128)S(1)} collective-permute-done((f32[128,1024]{1,0:T(8,128)S(1)}, f32[128,1024]{1,0:T(8,128)S(1)}, u32[]{:S(2)}, u32[]{:S(2)}) %collective-permute-start.19) | collective-permute-done | bytes 524320 | tf_op jit(solution)/shard_map/ppermute | solution.py:489
  67.7 0.7 %collective-permute-done.18.refs_6_ = f32[128,1024]{1,0:T(8,128)S(1)} collective-permute-done((f32[128,1024]{1,0:T(8,128)S(1)}, f32[128,1024]{1,0:T(8,128)S(1)}, u32[]{:S(2)}, u32[]{:S(2)}) %collective-permute-start.18) | collective-permute-done | bytes 524320 | tf_op jit(solution)/shard_map/ppermute | solution.py:489
  68.5 1.1 %shard_map.59 = bf16[128,32,128]{2,1,0:T(8,128)(2,1)} custom-call(f32[128,1024]{1,0:T(8,128)S(1)} %get-tuple-element.72.refs_0_, f32[128,1024]{1,0:T(8,128)S(1)} %get-tuple-element.73.refs_1_, f32[128,1024]{1,0:T(8,128)S(1)} %get-tuple-element.74.refs_2_, f32[128,1024]{1,0:T(8,128)S(1)} %get-tuple-element.75.refs_3_, ...), custom_call_target="tpu_custom_call" | custom-call | bytes 5242880 | tf_op jit(solution)/shard_map/pallas_call | solution.py:463
  (27 shorter events, 4.1 us)
Async XLA Ops:
  4.6 16.2 %collective-permute-start.2 = (f32[256,256]{1,0:T(8,128)S(1)}, f32[256,256]{1,0:T(8,128)S(1)}, u32[]{:S(2)}, u32[]{:S(2)}) collective-permute-start(f32[256,256]{1,0:T(8,128)S(1)} %get-tuple-element.51), channel_id=1, source_target_pairs={{0,2},{2,0},{4,6},{6,4},{8,10},{10,8},{12,14},{14,12},{1,3},{3,1},... | collective-permute-start | bytes 786440 | tf_op jit(solution)/shard_map/ppermute | solution.py:482
  7.6 10.0 %collective-permute-start = (f32[128,256]{1,0:T(8,128)S(1)}, f32[128,256]{1,0:T(8,128)S(1)}, u32[]{:S(2)}, u32[]{:S(2)}) collective-permute-start(f32[128,256]{1,0:T(8,128)S(1)} %get-tuple-element.46), channel_id=1, source_target_pairs={{0,2},{2,0},{4,6},{6,4},{8,10},{10,8},{12,14},{14,12},{1,3},{3,1},... | collective-permute-start | bytes 393224 | tf_op jit(solution)/shard_map/ppermute | solution.py:482
  10.5 15.0 %collective-permute-start.5 = (f32[128,256]{1,0:T(8,128)S(1)}, f32[128,256]{1,0:T(8,128)S(1)}, u32[]{:S(2)}, u32[]{:S(2)}) collective-permute-start(f32[128,256]{1,0:T(8,128)S(1)} %get-tuple-element.56), channel_id=1, source_target_pairs={{0,2},{2,0},{4,6},{6,4},{8,10},{10,8},{12,14},{14,12},{1,3},{3,1},... | collective-permute-start | bytes 393224 | tf_op jit(solution)/shard_map/ppermute | solution.py:482
  17.6 11.7 %collective-permute-start.1 = (f32[128,256]{1,0:T(8,128)S(1)}, f32[128,256]{1,0:T(8,128)S(1)}, u32[]{:S(2)}, u32[]{:S(2)}) collective-permute-start(f32[128,256]{1,0:T(8,128)S(1)} %shard_map.44), channel_id=1, source_target_pairs={{0,8},{2,10},{4,12},{6,14},{8,0},{10,2},{12,4},{14,6},{1,9},{3,11}... | collective-permute-start | bytes 393224 | tf_op jit(solution)/shard_map/ppermute | solution.py:486
  20.8 8.5 %collective-permute-start.3 = (f32[128,256]{1,0:T(8,128)S(1)}, f32[128,256]{1,0:T(8,128)S(1)}, u32[]{:S(2)}, u32[]{:S(2)}) collective-permute-start(f32[128,256]{1,0:T(8,128)S(1)} %get-tuple-element.52), channel_id=1, source_target_pairs={{0,4},{2,6},{4,8},{6,10},{8,12},{10,14},{12,0},{14,2},{1,5},{3,7},... | collective-permute-start | bytes 393224 | tf_op jit(solution)/shard_map/ppermute | solution.py:486
  22.4 7.2 %collective-permute-start.4 = (f32[128,256]{1,0:T(8,128)S(1)}, f32[128,256]{1,0:T(8,128)S(1)}, u32[]{:S(2)}, u32[]{:S(2)}) collective-permute-start(f32[128,256]{1,0:T(8,128)S(1)} %get-tuple-element.53), channel_id=1, source_target_pairs={{0,12},{2,14},{4,0},{6,2},{8,4},{10,6},{12,8},{14,10},{1,13},{3,15... | collective-permute-start | bytes 393224 | tf_op jit(solution)/shard_map/ppermute | solution.py:486
  29.7 6.9 %collective-permute-start.13 = (f32[128,256]{1,0:T(8,128)S(1)}, f32[128,256]{1,0:T(8,128)S(1)}, u32[]{:S(2)}, u32[]{:S(2)}) collective-permute-start(f32[128,256]{1,0:T(8,128)S(1)} %get-tuple-element.57.refs_0_), channel_id=1, source_target_pairs={{0,4},{2,6},{4,8},{6,10},{8,12},{10,14},{12,0},{14,2},{1,5},{3,7},... | collective-permute-start | bytes 393224 | tf_op jit(solution)/shard_map/ppermute | solution.py:486
  32.9 10.5 %collective-permute-start.6 = (f32[128,256]{1,0:T(8,128)S(1)}, f32[128,256]{1,0:T(8,128)S(1)}, u32[]{:S(2)}, u32[]{:S(2)}) collective-permute-start(f32[128,256]{1,0:T(8,128)S(1)} %get-tuple-element.57.refs_0_), channel_id=1, source_target_pairs={{0,12},{2,14},{4,0},{6,2},{8,4},{10,6},{12,8},{14,10},{1,13},{3,15... | collective-permute-start | bytes 393224 | tf_op jit(solution)/shard_map/ppermute | solution.py:486
  33.5 14.9 %collective-permute-start.12 = (f32[128,256]{1,0:T(8,128)S(1)}, f32[128,256]{1,0:T(8,128)S(1)}, u32[]{:S(2)}, u32[]{:S(2)}) collective-permute-start(f32[128,256]{1,0:T(8,128)S(1)} %get-tuple-element.57.refs_0_), channel_id=1, source_target_pairs={{0,2},{2,0},{4,6},{6,4},{8,10},{10,8},{12,14},{14,12},{1,3},{3,1},... | collective-permute-start | bytes 393224 | tf_op jit(solution)/shard_map/ppermute | solution.py:482
  36.5 12.0 %collective-permute-start.14 = (f32[128,256]{1,0:T(8,128)S(1)}, f32[128,256]{1,0:T(8,128)S(1)}, u32[]{:S(2)}, u32[]{:S(2)}) collective-permute-start(f32[128,256]{1,0:T(8,128)S(1)} %collective-permute-done.13.refs_2_), channel_id=1, source_target_pairs={{0,2},{2,0},{4,6},{6,4},{8,10},{10,8},{12,14},{14,12},{1,3},{3,1},... | collective-permute-start | bytes 393224 | tf_op jit(solution)/shard_map/ppermute | solution.py:482
  38.2 7.5 %collective-permute-start.8 = (f32[64,256]{1,0:T(8,128)S(1)}, f32[64,256]{1,0:T(8,128)S(1)}, u32[]{:S(2)}, u32[]{:S(2)}) collective-permute-start(f32[64,256]{1,0:T(8,128)S(1)} %get-tuple-element.58), channel_id=1, source_target_pairs={{0,8},{2,10},{4,12},{6,14},{8,0},{10,2},{12,4},{14,6},{1,9},{3,11}... | collective-permute-start | bytes 196616 | tf_op jit(solution)/shard_map/ppermute | solution.py:486
  43.3 5.2 %collective-permute-start.10 = (f32[64,256]{1,0:T(8,128)S(1)}, f32[64,256]{1,0:T(8,128)S(1)}, u32[]{:S(2)}, u32[]{:S(2)}) collective-permute-start(f32[64,256]{1,0:T(8,128)S(1)} %get-tuple-element.59), channel_id=1, source_target_pairs={{0,8},{2,10},{4,12},{6,14},{8,0},{10,2},{12,4},{14,6},{1,9},{3,11}... | collective-permute-start | bytes 196616 | tf_op jit(solution)/shard_map/ppermute | solution.py:486
  43.3 9.4 %collective-permute-start.7 = (f32[128,256]{1,0:T(8,128)S(1)}, f32[128,256]{1,0:T(8,128)S(1)}, u32[]{:S(2)}, u32[]{:S(2)}) collective-permute-start(f32[128,256]{1,0:T(8,128)S(1)} %collective-permute-done.6.refs_4_), channel_id=1, source_target_pairs={{0,2},{2,0},{4,6},{6,4},{8,10},{10,8},{12,14},{14,12},{1,3},{3,1},... | collective-permute-start | bytes 393224 | tf_op jit(solution)/shard_map/ppermute | solution.py:482
  45.7 4.3 %collective-permute-start.9 = (f32[64,256]{1,0:T(8,128)S(1)}, f32[64,256]{1,0:T(8,128)S(1)}, u32[]{:S(2)}, u32[]{:S(2)}) collective-permute-start(f32[64,256]{1,0:T(8,128)S(1)} %collective-permute-done.8.refs_5_.refs_6_), channel_id=1, source_target_pairs={{0,2},{2,0},{4,6},{6,4},{8,10},{10,8},{12,14},{14,12},{1,3},{3,1},... | collective-permute-start | bytes 196616 | tf_op jit(solution)/shard_map/ppermute | solution.py:482
  48.5 4.3 %collective-permute-start.11 = (f32[64,256]{1,0:T(8,128)S(1)}, f32[64,256]{1,0:T(8,128)S(1)}, u32[]{:S(2)}, u32[]{:S(2)}) collective-permute-start(f32[64,256]{1,0:T(8,128)S(1)} %collective-permute-done.10.refs_6_.refs_8_), channel_id=1, source_target_pairs={{0,2},{2,0},{4,6},{6,4},{8,10},{10,8},{12,14},{14,12},{1,3},{3,1},... | collective-permute-start | bytes 196616 | tf_op jit(solution)/shard_map/ppermute | solution.py:482
  53.2 1.6 %collective-permute-start.15 = (f32[256,256]{1,0:T(8,128)S(1)}, f32[256,256]{1,0:T(8,128)S(1)}, u32[]{:S(2)}, u32[]{:S(2)}) collective-permute-start(f32[256,256]{1,0:T(8,128)S(1)} %shard_map.52.gram), channel_id=1, source_target_pairs={{0,1},{1,0},{2,3},{3,2},{4,5},{5,4},{6,7},{7,6},{8,9},{9,8},{10,11... | collective-permute-start | bytes 786440 | tf_op jit(solution)/shard_map/ppermute | solution.py:489
  62.9 3.4 %collective-permute-start.16 = (f32[128,1024]{1,0:T(8,128)S(1)}, f32[128,1024]{1,0:T(8,128)S(1)}, u32[]{:S(2)}, u32[]{:S(2)}) collective-permute-start(f32[128,1024]{1,0:T(8,128)S(1)} %get-tuple-element.76), channel_id=1, source_target_pairs={{0,1},{1,0},{2,3},{3,2},{4,5},{5,4},{6,7},{7,6},{8,9},{9,8},{10,11... | collective-permute-start | bytes 1572872 | tf_op jit(solution)/shard_map/ppermute | solution.py:489
  63.9 2.5 %collective-permute-start.17 = (f32[128,1024]{1,0:T(8,128)S(1)}, f32[128,1024]{1,0:T(8,128)S(1)}, u32[]{:S(2)}, u32[]{:S(2)}) collective-permute-start(f32[128,1024]{1,0:T(8,128)S(1)} %get-tuple-element.77), channel_id=1, source_target_pairs={{0,1},{1,0},{2,3},{3,2},{4,5},{5,4},{6,7},{7,6},{8,9},{9,8},{10,11... | collective-permute-start | bytes 1572872 | tf_op jit(solution)/shard_map/ppermute | solution.py:489
  65.8 2.0 %collective-permute-start.19 = (f32[128,1024]{1,0:T(8,128)S(1)}, f32[128,1024]{1,0:T(8,128)S(1)}, u32[]{:S(2)}, u32[]{:S(2)}) collective-permute-start(f32[128,1024]{1,0:T(8,128)S(1)} %get-tuple-element.79), channel_id=1, source_target_pairs={{0,1},{1,0},{2,3},{3,2},{4,5},{5,4},{6,7},{7,6},{8,9},{9,8},{10,11... | collective-permute-start | bytes 1572872 | tf_op jit(solution)/shard_map/ppermute | solution.py:489
  66.0 2.5 %collective-permute-start.18 = (f32[128,1024]{1,0:T(8,128)S(1)}, f32[128,1024]{1,0:T(8,128)S(1)}, u32[]{:S(2)}, u32[]{:S(2)}) collective-permute-start(f32[128,1024]{1,0:T(8,128)S(1)} %get-tuple-element.78), channel_id=1, source_target_pairs={{0,1},{1,0},{2,3},{3,2},{4,5},{5,4},{6,7},{7,6},{8,9},{9,8},{10,11... | collective-permute-start | bytes 1572872 | tf_op jit(solution)/shard_map/ppermute | solution.py:489
